TPU v7x, 32 devices: a whole 2x2x4 slice. The times are simulated.
32 devices in a mesh: gx: 8 (over y, x, core), gy: 4 (over z).
Axes of the slice: x: 2, y: 2, z: 4, core: 2. Of those that a mesh axis runs over, the one named last changes fastest.
Arguments:
- pressure: float32 [64, 128, 128], P('gx', 'gy'), may hold values from -6 to 6
- source: float32 [64, 128, 128], P('gx', 'gy'), may hold values from -8 to 8, as said below
- coefficient: float32 [64, 128, 128], P('gx', 'gy'), may hold values from 0.1 to 1
Outputs:
- corrected: float32 [64, 128, 128], P('gx', 'gy')
Inputs may be any that keep to these rules, and one draw needn't show every extreme that they name: `source`: a rough field with a smooth part.
All inputs are finite; a program needn't handle non-finite values.
Results may differ from a plain program's by a relative error of at most 0.0001.
Values sent between devices are 32-bit elements; how exact they have to be, the bound alone decides.
No kernel may reach another device: no remote copies, remote signals or barrier semaphores. Data moves between devices by JAX's collectives and lax.ppermute only.
A program may use at most 128 MiB of HBM per device.

v0:
```python
import jax
import jax.numpy as jnp
from jax import lax
from jax.sharding import PartitionSpec as P

SWEEPS = 2
CSWEEPS = 4


def with_halo(shard, sides, width):
    for axis, dim in sides:
        count, length = (lax.axis_size(axis), shard.shape[dim])
        up = [(i, (i + 1) % count) for i in range(count - 1)]
        down = [(j, i) for i, j in up]
        last = lax.slice_in_dim(shard, length - width, length, axis=dim)
        initial = lax.slice_in_dim(shard, 0, width, axis=dim)
        before = lax.ppermute(last, axis, up)
        after = lax.ppermute(initial, axis, down)
        shard = jnp.concatenate([before, shard, after], axis=dim)
    return shard


def swapped(value, axis, stride):
    mask = 2**stride
    pairs = [(source, source ^ mask) for source in range(lax.axis_size(axis))]
    return lax.ppermute(value, axis, pairs)


def restrict(field):
    size_x, size_y, size_z = field.shape
    return field.reshape(size_x // 2, 2, size_y // 2, 2, size_z // 2, 2).mean(axis=(1, 3, 5))


def pad_plane(field):
    return jnp.pad(field, ((1, 1), (1, 1), (0, 0)))


def pad_depth(field):
    return jnp.pad(field, ((0, 0), (0, 0), (1, 1)))


def level_weights(coef_pad):
    padded = pad_depth(coef_pad)
    east_west = (padded[1:, 1:-1, 1:-1] + padded[:-1, 1:-1, 1:-1]) * 0.5
    north_south = (padded[1:-1, 1:, 1:-1] + padded[1:-1, :-1, 1:-1]) * 0.5
    up_down = (padded[1:-1, 1:-1, 1:] + padded[1:-1, 1:-1, :-1]) * 0.5
    diagonal = (
        east_west[1:]
        + east_west[:-1]
        + north_south[:, 1:]
        + north_south[:, :-1]
        + up_down[:, :, 1:]
        + up_down[:, :, :-1]
    )
    return ((east_west, north_south, up_down), diagonal)


def neighbour_sum(field_pad, weights):
    east_west, north_south, up_down = weights
    padded = pad_depth(field_pad)
    total = east_west[:-1] * padded[:-2, 1:-1, 1:-1] + east_west[1:] * padded[2:, 1:-1, 1:-1]
    total = (
        total
        + north_south[:, :-1] * padded[1:-1, :-2, 1:-1]
        + north_south[:, 1:] * padded[1:-1, 2:, 1:-1]
    )
    total = (
        total
        + up_down[:, :, :-1] * padded[1:-1, 1:-1, :-2]
        + up_down[:, :, 1:] * padded[1:-1, 1:-1, 2:]
    )
    return total


def parity_of(shape):
    summed = (
        lax.broadcasted_iota(jnp.int32, shape, 0)
        + lax.broadcasted_iota(jnp.int32, shape, 1)
        + lax.broadcasted_iota(jnp.int32, shape, 2)
    )
    return summed % 2


def sweep(field, rhs, weights, diagonal, level, faces):
    scale_up = 4.0**level
    parity = parity_of(field.shape)
    for colour in (0, 1):
        total = neighbour_sum(faces(field, colour), weights)
        fresh = (rhs * scale_up + total) / diagonal
        field = jnp.where(parity == colour, fresh, field)
    return field


def residual_of(field, rhs, weights, diagonal, level):
    total = neighbour_sum(exchange_faces(field), weights)
    return rhs - (diagonal * field - total) * 4.0 ** (-level)


def coarse_solve(rhs, weights, diagonal):
    scale_down = 4.0 ** (-3)
    error = jnp.zeros_like(rhs)
    remain = rhs
    direction = rhs
    norm_now = jnp.sum(remain * remain)
    for repeat in range(CSWEEPS):
        image = (diagonal * direction - neighbour_sum(pad_plane(direction), weights)) * scale_down
        alpha = norm_now / jnp.sum(direction * image)
        error = error + alpha * direction
        remain = remain - alpha * image
        norm_next = jnp.sum(remain * remain)
        direction = remain + norm_next / norm_now * direction
        norm_now = norm_next
    return error


def prolong_axis(padded, axis):
    length = padded.shape[axis]
    middle = lax.slice_in_dim(padded, 1, length - 1, axis=axis)
    before = lax.slice_in_dim(padded, 0, length - 2, axis=axis)
    after = lax.slice_in_dim(padded, 2, length, axis=axis)
    lower = 0.75 * middle + 0.25 * before
    upper = 0.75 * middle + 0.25 * after
    joined = jnp.stack([lower, upper], axis=axis + 1)
    shape = list(middle.shape)
    shape[axis] = 2 * shape[axis]
    return joined.reshape(shape)


def prolong3(plane_pad):
    padded = pad_depth(plane_pad)
    padded = prolong_axis(padded, 0)
    padded = prolong_axis(padded, 1)
    return prolong_axis(padded, 2)


def exchange_faces(field):
    return with_halo(field, (("gx", 0), ("gy", 1)), 1)


def sweep_faces(field, colour):
    return exchange_faces(field)


def coef_faces(field):
    return with_halo(field, (("gx", 0), ("gy", 1)), 1)


def correction_faces(field):
    return with_halo(field, (("gx", 0), ("gy", 1)), 1)


def agglomerate(stacked):
    position = lax.axis_index("gx")
    merged = stacked
    for level_bit in range(lax.axis_size("gx").bit_length() - 1):
        partner = swapped(merged, "gx", level_bit)
        lower_half = position >> level_bit & 1 == 0
        merged = jnp.where(
            lower_half, jnp.concatenate([merged, partner], 1), jnp.concatenate([partner, merged], 1)
        )
    merged = lax.all_gather(merged, "gy", axis=2, tiled=True)
    return merged


def on_device(pressure, source, coefficient):
    coef_one = restrict(coefficient)
    coef_two = restrict(coef_one)
    coef_three = restrict(coef_two)
    pad_zero = coef_faces(coefficient)
    pad_one = coef_faces(coef_one)
    pad_two = coef_faces(coef_two)
    weights0, diagonal0 = level_weights(pad_zero)
    weights1, diagonal1 = level_weights(pad_one)
    weights2, diagonal2 = level_weights(pad_two)
    smoothed = pressure
    for repeat in range(SWEEPS):
        smoothed = sweep(smoothed, source, weights0, diagonal0, 0, sweep_faces)
    rhs_one = restrict(residual_of(smoothed, source, weights0, diagonal0, 0))
    error_one = sweep(jnp.zeros_like(rhs_one), rhs_one, weights1, diagonal1, 1, sweep_faces)
    rhs_two = restrict(residual_of(error_one, rhs_one, weights1, diagonal1, 1))
    error_two = sweep(jnp.zeros_like(rhs_two), rhs_two, weights2, diagonal2, 2, sweep_faces)
    rhs_three = restrict(residual_of(error_two, rhs_two, weights2, diagonal2, 2))
    merged = agglomerate(jnp.stack([rhs_three, coef_three]))
    coarse_rhs = merged[0]
    coarse_coef = merged[1]
    weights3, diagonal3 = level_weights(pad_plane(coarse_coef))
    error_three = coarse_solve(coarse_rhs, weights3, diagonal3)
    cells_x = rhs_three.shape[0]
    cells_y = rhs_three.shape[1]
    start_x = lax.axis_index("gx") * cells_x
    start_y = lax.axis_index("gy") * cells_y
    window = lax.dynamic_slice(
        pad_plane(error_three),
        (start_x, start_y, jnp.int32(0)),
        (cells_x + 2, cells_y + 2, error_three.shape[2]),
    )
    error_two = error_two + prolong3(window)
    error_one = error_one + prolong3(correction_faces(error_two))
    return smoothed + prolong3(correction_faces(error_one))


def solution(mesh):
    in_specs = (P("gx", "gy", None), P("gx", "gy", None), P("gx", "gy", None))
    out_specs = P("gx", "gy", None)
    return jax.shard_map(
        on_device, mesh=mesh, in_specs=in_specs, out_specs=out_specs, check_vma=False
    )
```

profile of v0, /device:TPU:0, one launch (start us, length us, event | category | flops | bytes accessed | tf_op | source)
XLA Modules:
  0.0 293.3 jit_solution(9542998874292949107)
XLA Ops:
  4.4 5.3 %collective-permute-start.1 = (f32[1,32,128]{2,1,0:T(8,128)S(1)}, f32[1,32,128]{2,1,0:T(8,128)S(1)}, u32[]{:S(2)}, u32[]{:S(2)}) collective-permute-start(f32[1,32,128]{2,1,0:T(8,128)S(1)} %get-tuple-element.39), channel_id=1, source_target_pairs={{0,4},{4,8},{8,12},{12,16},{16,20},{20,24},{24,28},{1,5},{5,9},{9,... | collective-permute-start | bytes 49160 | tf_op jit(solution)/shard_map/ppermute | solution.py:17
  9.7 10.5 %reshape.72 = f32[4,2,16,2,64,2]{5,4,3,2,1,0:T(8,128)} reshape(f32[8,32,128]{2,1,0:T(8,128)} %param.5) | data formatting | bytes 262144 | tf_op jit(solution)/shard_map/reshape | solution.py:31
  20.2 4.0 %reduce_sum.141 = f32[4,16,64]{2,1,0:T(8,128)S(1)} reduce(f32[4,2,16,2,64,2]{5,4,3,2,1,0:T(8,128)} %reshape.72, f32[]{:T(128)} %constant.37.clone.1), dimensions={1,3,5}, to_apply=%region_1.0 | reduce | flops 28672 | bytes 147460 | tf_op jit(solution)/shard_map/reduce_sum | solution.py:31
  26.8 4.3 %collective-permute-start.41 = (f32[1,8,32]{2,1,0:T(8,128)S(1)}, f32[1,8,32]{2,1,0:T(8,128)S(1)}, u32[]{:S(2)}, u32[]{:S(2)}) collective-permute-start(f32[1,8,32]{2,1,0:T(8,128)S(1)} %get-tuple-element.92), channel_id=1, source_target_pairs={{0,4},{4,8},{8,12},{12,16},{16,20},{20,24},{24,28},{1,5},{5,9},{9,... | collective-permute-start | bytes 3080 | tf_op jit(solution)/shard_map/ppermute | solution.py:17
  32.5 4.3 %collective-permute-start.2 = (f32[1,32,128]{2,1,0:T(8,128)S(1)}, f32[1,32,128]{2,1,0:T(8,128)S(1)}, u32[]{:S(2)}, u32[]{:S(2)}) collective-permute-start(f32[1,32,128]{2,1,0:T(8,128)S(1)} %get-tuple-element.41), channel_id=1, source_target_pairs={{0,4},{4,8},{8,12},{12,16},{16,20},{20,24},{24,28},{1,5},{5,9},{9,... | collective-permute-start | bytes 49160 | tf_op jit(solution)/shard_map/ppermute | solution.py:17
  38.1 4.3 %collective-permute-start.42 = (f32[1,8,32]{2,1,0:T(8,128)S(1)}, f32[1,8,32]{2,1,0:T(8,128)S(1)}, u32[]{:S(2)}, u32[]{:S(2)}) collective-permute-start(f32[1,8,32]{2,1,0:T(8,128)S(1)} %broadcast.202), channel_id=1, source_target_pairs={{0,4},{4,8},{8,12},{12,16},{16,20},{20,24},{24,28},{1,5},{5,9},{9,... | collective-permute-start | bytes 3080 | tf_op jit(solution)/shard_map/ppermute | solution.py:17
  43.8 4.5 %collective-permute-start.5 = (f32[10,1,128]{2,1,0:T(1,128)S(1)}, f32[10,1,128]{2,1,0:T(1,128)S(1)}, u32[]{:S(2)}, u32[]{:S(2)}) collective-permute-start(f32[10,1,128]{2,1,0:T(1,128)S(1)} %get-tuple-element.22), channel_id=1, source_target_pairs={{0,1},{1,2},{2,3},{4,5},{5,6},{6,7},{8,9},{9,10},{10,11},{12,13},{... | collective-permute-start | bytes 15368 | tf_op jit(solution)/shard_map/ppermute | solution.py:17
  48.4 3.5 %collective-permute-start.6 = (f32[10,1,128]{2,1,0:T(1,128)S(1)}, f32[10,1,128]{2,1,0:T(1,128)S(1)}, u32[]{:S(2)}, u32[]{:S(2)}) collective-permute-start(f32[10,1,128]{2,1,0:T(1,128)S(1)} %get-tuple-element.24), channel_id=1, source_target_pairs={{0,1},{1,2},{2,3},{4,5},{5,6},{6,7},{8,9},{9,10},{10,11},{12,13},{... | collective-permute-start | bytes 15368 | tf_op jit(solution)/shard_map/ppermute | solution.py:17
  54.9 2.5 collective-permute-done.7
  59.2 3.0 %collective-permute-start.8 = (f32[1,32,128]{2,1,0:T(8,128)S(1)}, f32[1,32,128]{2,1,0:T(8,128)S(1)}, u32[]{:S(2)}, u32[]{:S(2)}) collective-permute-start(f32[1,32,128]{2,1,0:T(8,128)S(1)} %get-tuple-element.36), channel_id=1, source_target_pairs={{0,4},{4,8},{8,12},{12,16},{16,20},{20,24},{24,28},{1,5},{5,9},{9,... | collective-permute-start | bytes 49160 | tf_op jit(solution)/shard_map/ppermute | solution.py:17
  63.6 6.3 %collective-permute-start.25 = (f32[1,16,64]{2,1,0:T(8,128)S(1)}, f32[1,16,64]{2,1,0:T(8,128)S(1)}, u32[]{:S(2)}, u32[]{:S(2)}) collective-permute-start(f32[1,16,64]{2,1,0:T(8,128)S(1)} %get-tuple-element.64), channel_id=1, source_target_pairs={{0,4},{4,8},{8,12},{12,16},{16,20},{20,24},{24,28},{1,5},{5,9},{9,... | collective-permute-start | bytes 12296 | tf_op jit(solution)/shard_map/ppermute | solution.py:17
  71.3 4.5 %collective-permute-start.10 = (f32[10,1,128]{2,1,0:T(1,128)S(1)}, f32[10,1,128]{2,1,0:T(1,128)S(1)}, u32[]{:S(2)}, u32[]{:S(2)}) collective-permute-start(f32[10,1,128]{2,1,0:T(1,128)S(1)} %get-tuple-element.20), channel_id=1, source_target_pairs={{0,1},{1,2},{2,3},{4,5},{5,6},{6,7},{8,9},{9,10},{10,11},{12,13},{... | collective-permute-start | bytes 15368 | tf_op jit(solution)/shard_map/ppermute | solution.py:17
  77.2 4.2 %collective-permute-done.11 = f32[10,1,128]{2,1,0:T(1,128)S(1)} collective-permute-done((f32[10,1,128]{2,1,0:T(1,128)S(1)}, f32[10,1,128]{2,1,0:T(1,128)S(1)}, u32[]{:S(2)}, u32[]{:S(2)}) %collective-permute-start.11) | collective-permute-done | bytes 5152 | tf_op jit(solution)/shard_map/ppermute | solution.py:18
  85.2 3.5 %collective-permute-start.45 = (f32[4,1,32]{2,1,0:T(1,128)S(1)}, f32[4,1,32]{2,1,0:T(1,128)S(1)}, u32[]{:S(2)}, u32[]{:S(2)}) collective-permute-start(f32[4,1,32]{2,1,0:T(1,128)S(1)} %get-tuple-element.76), channel_id=1, source_target_pairs={{0,1},{1,2},{2,3},{4,5},{5,6},{6,7},{8,9},{9,10},{10,11},{12,13},{... | collective-permute-start | bytes 1544 | tf_op jit(solution)/shard_map/ppermute | solution.py:17
  89.6 3.6 %collective-permute-start.46 = (f32[4,1,32]{2,1,0:T(1,128)S(1)}, f32[4,1,32]{2,1,0:T(1,128)S(1)}, u32[]{:S(2)}, u32[]{:S(2)}) collective-permute-start(f32[4,1,32]{2,1,0:T(1,128)S(1)} %get-tuple-element.78), channel_id=1, source_target_pairs={{0,1},{1,2},{2,3},{4,5},{5,6},{6,7},{8,9},{9,10},{10,11},{12,13},{... | collective-permute-start | bytes 1544 | tf_op jit(solution)/shard_map/ppermute | solution.py:17
  93.2 3.5 %collective-permute-start.14 = (f32[10,1,128]{2,1,0:T(1,128)S(1)}, f32[10,1,128]{2,1,0:T(1,128)S(1)}, u32[]{:S(2)}, u32[]{:S(2)}) collective-permute-start(f32[10,1,128]{2,1,0:T(1,128)S(1)} %get-tuple-element.18), channel_id=1, source_target_pairs={{0,1},{1,2},{2,3},{4,5},{5,6},{6,7},{8,9},{9,10},{10,11},{12,13},{... | collective-permute-start | bytes 15368 | tf_op jit(solution)/shard_map/ppermute | solution.py:17
  99.3 2.9 collective-permute-done.15
  105.0 3.3 %collective-permute-start.16 = (f32[1,32,128]{2,1,0:T(8,128)S(1)}, f32[1,32,128]{2,1,0:T(8,128)S(1)}, u32[]{:S(2)}, u32[]{:S(2)}) collective-permute-start(f32[1,32,128]{2,1,0:T(8,128)S(1)} %get-tuple-element.32), channel_id=1, source_target_pairs={{0,4},{4,8},{8,12},{12,16},{16,20},{20,24},{24,28},{1,5},{5,9},{9,... | collective-permute-start | bytes 49160 | tf_op jit(solution)/shard_map/ppermute | solution.py:17
  109.7 2.9 collective-permute-done.17
  112.6 3.9 %collective-permute-start.18 = (f32[10,1,128]{2,1,0:T(1,128)S(1)}, f32[10,1,128]{2,1,0:T(1,128)S(1)}, u32[]{:S(2)}, u32[]{:S(2)}) collective-permute-start(f32[10,1,128]{2,1,0:T(1,128)S(1)} %get-tuple-element.16), channel_id=1, source_target_pairs={{0,1},{1,2},{2,3},{4,5},{5,6},{6,7},{8,9},{9,10},{10,11},{12,13},{... | collective-permute-start | bytes 15368 | tf_op jit(solution)/shard_map/ppermute | solution.py:17
  117.9 4.5 %collective-permute-start.30 = (f32[6,1,64]{2,1,0:T(1,128)S(1)}, f32[6,1,64]{2,1,0:T(1,128)S(1)}, u32[]{:S(2)}, u32[]{:S(2)}) collective-permute-start(f32[6,1,64]{2,1,0:T(1,128)S(1)} %get-tuple-element.54), channel_id=1, source_target_pairs={{0,1},{1,2},{2,3},{4,5},{5,6},{6,7},{8,9},{9,10},{10,11},{12,13},{... | collective-permute-start | bytes 4616 | tf_op jit(solution)/shard_map/ppermute | solution.py:17
  124.2 3.5 %collective-permute-start.20 = (f32[1,32,128]{2,1,0:T(8,128)S(1)}, f32[1,32,128]{2,1,0:T(8,128)S(1)}, u32[]{:S(2)}, u32[]{:S(2)}) collective-permute-start(f32[1,32,128]{2,1,0:T(8,128)S(1)} %get-tuple-element.30), channel_id=1, source_target_pairs={{0,4},{4,8},{8,12},{12,16},{16,20},{20,24},{24,28},{1,5},{5,9},{9,... | collective-permute-start | bytes 49160 | tf_op jit(solution)/shard_map/ppermute | solution.py:17
  129.4 2.9 collective-permute-done.21
  132.3 4.5 %collective-permute-start.22 = (f32[10,1,128]{2,1,0:T(1,128)S(1)}, f32[10,1,128]{2,1,0:T(1,128)S(1)}, u32[]{:S(2)}, u32[]{:S(2)}) collective-permute-start(f32[10,1,128]{2,1,0:T(1,128)S(1)} %get-tuple-element.14), channel_id=1, source_target_pairs={{0,1},{1,2},{2,3},{4,5},{5,6},{6,7},{8,9},{9,10},{10,11},{12,13},{... | collective-permute-start | bytes 15368 | tf_op jit(solution)/shard_map/ppermute | solution.py:17
  139.5 2.9 collective-permute-done.23
  142.8 9.8 %reshape.71 = f32[4,2,16,2,64,2]{5,4,3,2,1,0:T(8,128)} reshape(f32[8,32,128]{2,1,0:T(8,128)S(1)} %fusion.12) | data formatting | bytes 262144 | tf_op jit(solution)/shard_map/reshape | solution.py:31
  152.6 4.0 %reduce_sum.140 = f32[4,16,64]{2,1,0:T(8,128)S(1)} reduce(f32[4,2,16,2,64,2]{5,4,3,2,1,0:T(8,128)} %reshape.71, f32[]{:T(128)} %constant.37.clone.1), dimensions={1,3,5}, to_apply=%region_0.0 | reduce | flops 28672 | bytes 147460 | tf_op jit(solution)/shard_map/reduce_sum | solution.py:31
  156.7 3.5 %collective-permute-start.32 = (f32[1,16,64]{2,1,0:T(8,128)S(1)}, f32[1,16,64]{2,1,0:T(8,128)S(1)}, u32[]{:S(2)}, u32[]{:S(2)}) collective-permute-start(f32[1,16,64]{2,1,0:T(8,128)S(1)} %get-tuple-element.62), channel_id=1, source_target_pairs={{0,4},{4,8},{8,12},{12,16},{16,20},{20,24},{24,28},{1,5},{5,9},{9,... | collective-permute-start | bytes 12296 | tf_op jit(solution)/shard_map/ppermute | solution.py:17
  161.6 3.0 %collective-permute-done.33 = f32[1,16,64]{2,1,0:T(8,128)S(1)} collective-permute-done((f32[1,16,64]{2,1,0:T(8,128)S(1)}, f32[1,16,64]{2,1,0:T(8,128)S(1)}, u32[]{:S(2)}, u32[]{:S(2)}) %collective-permute-start.33) | collective-permute-done | bytes 4128 | tf_op jit(solution)/shard_map/ppermute | solution.py:18
  168.3 4.1 %collective-permute-done.35 = f32[6,1,64]{2,1,0:T(1,128)S(1)} collective-permute-done((f32[6,1,64]{2,1,0:T(1,128)S(1)}, f32[6,1,64]{2,1,0:T(1,128)S(1)}, u32[]{:S(2)}, u32[]{:S(2)}) %collective-permute-start.35) | collective-permute-done | bytes 1568 | tf_op jit(solution)/shard_map/ppermute | solution.py:18
  172.6 4.0 %collective-permute-start.36 = (f32[1,16,64]{2,1,0:T(8,128)S(1)}, f32[1,16,64]{2,1,0:T(8,128)S(1)}, u32[]{:S(2)}, u32[]{:S(2)}) collective-permute-start(f32[1,16,64]{2,1,0:T(8,128)S(1)} %get-tuple-element.60), channel_id=1, source_target_pairs={{0,4},{4,8},{8,12},{12,16},{16,20},{20,24},{24,28},{1,5},{5,9},{9,... | collective-permute-start | bytes 12296 | tf_op jit(solution)/shard_map/ppermute | solution.py:17
  178.0 2.6 collective-permute-done.37
  180.6 3.8 %collective-permute-start.38 = (f32[6,1,64]{2,1,0:T(1,128)S(1)}, f32[6,1,64]{2,1,0:T(1,128)S(1)}, u32[]{:S(2)}, u32[]{:S(2)}) collective-permute-start(f32[6,1,64]{2,1,0:T(1,128)S(1)} %get-tuple-element.48), channel_id=1, source_target_pairs={{0,1},{1,2},{2,3},{4,5},{5,6},{6,7},{8,9},{9,10},{10,11},{12,13},{... | collective-permute-start | bytes 4616 | tf_op jit(solution)/shard_map/ppermute | solution.py:17
  185.8 4.2 %collective-permute-done.39 = f32[6,1,64]{2,1,0:T(1,128)S(1)} collective-permute-done((f32[6,1,64]{2,1,0:T(1,128)S(1)}, f32[6,1,64]{2,1,0:T(1,128)S(1)}, u32[]{:S(2)}, u32[]{:S(2)}) %collective-permute-start.39) | collective-permute-done | bytes 1568 | tf_op jit(solution)/shard_map/ppermute | solution.py:18
  191.5 3.0 %collective-permute-start.48 = (f32[1,8,32]{2,1,0:T(8,128)S(1)}, f32[1,8,32]{2,1,0:T(8,128)S(1)}, u32[]{:S(2)}, u32[]{:S(2)}) collective-permute-start(f32[1,8,32]{2,1,0:T(8,128)S(1)} %get-tuple-element.90), channel_id=1, source_target_pairs={{0,4},{4,8},{8,12},{12,16},{16,20},{20,24},{24,28},{1,5},{5,9},{9,... | collective-permute-start | bytes 3080 | tf_op jit(solution)/shard_map/ppermute | solution.py:17
  195.8 3.5 %collective-permute-done.49 = f32[1,8,32]{2,1,0:T(8,128)S(1)} collective-permute-done((f32[1,8,32]{2,1,0:T(8,128)S(1)}, f32[1,8,32]{2,1,0:T(8,128)S(1)}, u32[]{:S(2)}, u32[]{:S(2)}) %collective-permute-start.49) | collective-permute-done | bytes 1056 | tf_op jit(solution)/shard_map/ppermute | solution.py:18
  202.7 4.0 %collective-permute-done.51 = f32[4,1,32]{2,1,0:T(1,128)S(1)} collective-permute-done((f32[4,1,32]{2,1,0:T(1,128)S(1)}, f32[4,1,32]{2,1,0:T(1,128)S(1)}, u32[]{:S(2)}, u32[]{:S(2)}) %collective-permute-start.51) | collective-permute-done | bytes 544 | tf_op jit(solution)/shard_map/ppermute | solution.py:18
  206.9 3.2 %collective-permute-start.52 = (f32[1,8,32]{2,1,0:T(8,128)S(1)}, f32[1,8,32]{2,1,0:T(8,128)S(1)}, u32[]{:S(2)}, u32[]{:S(2)}) collective-permute-start(f32[1,8,32]{2,1,0:T(8,128)S(1)} %get-tuple-element.86), channel_id=1, source_target_pairs={{0,4},{4,8},{8,12},{12,16},{16,20},{20,24},{24,28},{1,5},{5,9},{9,... | collective-permute-start | bytes 3080 | tf_op jit(solution)/shard_map/ppermute | solution.py:17
  211.6 3.1 %collective-permute-done.53 = f32[1,8,32]{2,1,0:T(8,128)S(1)} collective-permute-done((f32[1,8,32]{2,1,0:T(8,128)S(1)}, f32[1,8,32]{2,1,0:T(8,128)S(1)}, u32[]{:S(2)}, u32[]{:S(2)}) %collective-permute-start.53) | collective-permute-done | bytes 1056 | tf_op jit(solution)/shard_map/ppermute | solution.py:18
  218.0 4.2 %collective-permute-done.55 = f32[4,1,32]{2,1,0:T(1,128)S(1)} collective-permute-done((f32[4,1,32]{2,1,0:T(1,128)S(1)}, f32[4,1,32]{2,1,0:T(1,128)S(1)}, u32[]{:S(2)}, u32[]{:S(2)}) %collective-permute-start.55) | collective-permute-done | bytes 544 | tf_op jit(solution)/shard_map/ppermute | solution.py:18
  224.7 3.7 %collective-permute-start.57 = (f32[2,2,4,16]{3,2,1,0:T(4,128)S(1)}, f32[2,2,4,16]{3,2,1,0:T(4,128)S(1)}, u32[]{:S(2)}, u32[]{:S(2)}) collective-permute-start(f32[2,2,4,16]{3,2,1,0:T(4,128)S(1)} %maximum_select_fusion.2), channel_id=1, source_target_pairs={{0,8},{4,12},{8,0},{12,4},{16,24},{20,28},{24,16},{28,20},{1,9},{5... | collective-permute-start | bytes 3080 | tf_op jit(solution)/shard_map/ppermute | solution.py:26
  234.1 13.4 %all_gather.3 = f32[2,8,16,16]{3,1,0,2:T(8,128)S(1)} all-gather(f32[2,8,4,16]{3,1,0,2:T(8,128)S(1)} %copy.320), channel_id=1, replica_groups=mesh['gx'=8,'gy'=4] {'gy'}, dimensions={2}, use_global_device_ids=true | all-gather | bytes 20480 | tf_op jit(solution)/shard_map/all_gather | solution.py:161
  264.4 3.8 %collective-permute-done.60 = f32[1,8,32]{2,1,0:T(8,128)S(1)} collective-permute-done((f32[1,8,32]{2,1,0:T(8,128)S(1)}, f32[1,8,32]{2,1,0:T(8,128)S(1)}, u32[]{:S(2)}, u32[]{:S(2)}) %collective-permute-start.60) | collective-permute-done | bytes 1056 | tf_op jit(solution)/shard_map/ppermute | solution.py:18
  270.9 4.2 %collective-permute-done.62 = f32[4,1,32]{2,1,0:T(1,128)S(1)} collective-permute-done((f32[4,1,32]{2,1,0:T(1,128)S(1)}, f32[4,1,32]{2,1,0:T(1,128)S(1)}, u32[]{:S(2)}, u32[]{:S(2)}) %collective-permute-start.62) | collective-permute-done | bytes 544 | tf_op jit(solution)/shard_map/ppermute | solution.py:18
  275.6 3.1 %collective-permute-start.63 = (f32[1,16,64]{2,1,0:T(8,128)S(1)}, f32[1,16,64]{2,1,0:T(8,128)S(1)}, u32[]{:S(2)}, u32[]{:S(2)}) collective-permute-start(f32[1,16,64]{2,1,0:T(8,128)S(1)} %get-tuple-element.56), channel_id=1, source_target_pairs={{0,4},{4,8},{8,12},{12,16},{16,20},{20,24},{24,28},{1,5},{5,9},{9,... | collective-permute-start | bytes 12296 | tf_op jit(solution)/shard_map/ppermute | solution.py:17
  280.0 2.5 collective-permute-done.64
  282.5 3.7 %collective-permute-start.65 = (f32[6,1,64]{2,1,0:T(1,128)S(1)}, f32[6,1,64]{2,1,0:T(1,128)S(1)}, u32[]{:S(2)}, u32[]{:S(2)}) collective-permute-start(f32[6,1,64]{2,1,0:T(1,128)S(1)} %get-tuple-element.46), channel_id=1, source_target_pairs={{0,1},{1,2},{2,3},{4,5},{5,6},{6,7},{8,9},{9,10},{10,11},{12,13},{... | collective-permute-start | bytes 4616 | tf_op jit(solution)/shard_map/ppermute | solution.py:17
  287.5 4.2 %collective-permute-done.66 = f32[6,1,64]{2,1,0:T(1,128)S(1)} collective-permute-done((f32[6,1,64]{2,1,0:T(1,128)S(1)}, f32[6,1,64]{2,1,0:T(1,128)S(1)}, u32[]{:S(2)}, u32[]{:S(2)}) %collective-permute-start.66) | collective-permute-done | bytes 1568 | tf_op jit(solution)/shard_map/ppermute | solution.py:18
  (246 shorter events, 81.3 us)
Async XLA Ops:
  0.0 93.2 %collective-permute-start.26 = (f32[1,16,64]{2,1,0:T(8,128)S(1)}, f32[1,16,64]{2,1,0:T(8,128)S(1)}, u32[]{:S(2)}, u32[]{:S(2)}) collective-permute-start(f32[1,16,64]{2,1,0:T(8,128)S(1)} %broadcast.199), channel_id=1, source_target_pairs={{0,4},{4,8},{8,12},{12,16},{16,20},{20,24},{24,28},{1,5},{5,9},{9,... | collective-permute-start | bytes 12296 | tf_op jit(solution)/shard_map/ppermute | solution.py:17
  2.4 94.3 %collective-permute-start.27 = (f32[1,16,64]{2,1,0:T(8,128)S(1)}, f32[1,16,64]{2,1,0:T(8,128)S(1)}, u32[]{:S(2)}, u32[]{:S(2)}) collective-permute-start(f32[1,16,64]{2,1,0:T(8,128)S(1)} %broadcast.199), channel_id=1, source_target_pairs={{4,0},{8,4},{12,8},{16,12},{20,16},{24,20},{28,24},{5,1},{9,5},{13... | collective-permute-start | bytes 12296 | tf_op jit(solution)/shard_map/ppermute | solution.py:18
  4.4 32.4 %collective-permute-start.1 = (f32[1,32,128]{2,1,0:T(8,128)S(1)}, f32[1,32,128]{2,1,0:T(8,128)S(1)}, u32[]{:S(2)}, u32[]{:S(2)}) collective-permute-start(f32[1,32,128]{2,1,0:T(8,128)S(1)} %get-tuple-element.39), channel_id=1, source_target_pairs={{0,4},{4,8},{8,12},{12,16},{16,20},{20,24},{24,28},{1,5},{5,9},{9,... | collective-permute-start | bytes 49160 | tf_op jit(solution)/shard_map/ppermute | solution.py:17
  25.5 5.6 %collective-permute-start.40 = (f32[1,8,32]{2,1,0:T(8,128)S(1)}, f32[1,8,32]{2,1,0:T(8,128)S(1)}, u32[]{:S(2)}, u32[]{:S(2)}) collective-permute-start(f32[1,8,32]{2,1,0:T(8,128)S(1)} %get-tuple-element.93), channel_id=1, source_target_pairs={{4,0},{8,4},{12,8},{16,12},{20,16},{24,20},{28,24},{5,1},{9,5},{13... | collective-permute-start | bytes 3080 | tf_op jit(solution)/shard_map/ppermute | solution.py:18
  26.8 5.6 %collective-permute-start.41 = (f32[1,8,32]{2,1,0:T(8,128)S(1)}, f32[1,8,32]{2,1,0:T(8,128)S(1)}, u32[]{:S(2)}, u32[]{:S(2)}) collective-permute-start(f32[1,8,32]{2,1,0:T(8,128)S(1)} %get-tuple-element.92), channel_id=1, source_target_pairs={{0,4},{4,8},{8,12},{12,16},{16,20},{20,24},{24,28},{1,5},{5,9},{9,... | collective-permute-start | bytes 3080 | tf_op jit(solution)/shard_map/ppermute | solution.py:17
  31.1 7.0 %collective-permute-start = (f32[1,32,128]{2,1,0:T(8,128)S(1)}, f32[1,32,128]{2,1,0:T(8,128)S(1)}, u32[]{:S(2)}, u32[]{:S(2)}) collective-permute-start(f32[1,32,128]{2,1,0:T(8,128)S(1)} %get-tuple-element.38), channel_id=1, source_target_pairs={{4,0},{8,4},{12,8},{16,12},{20,16},{24,20},{28,24},{5,1},{9,5},{13... | collective-permute-start | bytes 49160 | tf_op jit(solution)/shard_map/ppermute | solution.py:18
  32.5 10.0 %collective-permute-start.2 = (f32[1,32,128]{2,1,0:T(8,128)S(1)}, f32[1,32,128]{2,1,0:T(8,128)S(1)}, u32[]{:S(2)}, u32[]{:S(2)}) collective-permute-start(f32[1,32,128]{2,1,0:T(8,128)S(1)} %get-tuple-element.41), channel_id=1, source_target_pairs={{0,4},{4,8},{8,12},{12,16},{16,20},{20,24},{24,28},{1,5},{5,9},{9,... | collective-permute-start | bytes 49160 | tf_op jit(solution)/shard_map/ppermute | solution.py:17
  36.8 7.0 %collective-permute-start.3 = (f32[1,32,128]{2,1,0:T(8,128)S(1)}, f32[1,32,128]{2,1,0:T(8,128)S(1)}, u32[]{:S(2)}, u32[]{:S(2)}) collective-permute-start(f32[1,32,128]{2,1,0:T(8,128)S(1)} %get-tuple-element.40), channel_id=1, source_target_pairs={{4,0},{8,4},{12,8},{16,12},{20,16},{24,20},{28,24},{5,1},{9,5},{13... | collective-permute-start | bytes 49160 | tf_op jit(solution)/shard_map/ppermute | solution.py:18
  38.1 21.0 %collective-permute-start.42 = (f32[1,8,32]{2,1,0:T(8,128)S(1)}, f32[1,8,32]{2,1,0:T(8,128)S(1)}, u32[]{:S(2)}, u32[]{:S(2)}) collective-permute-start(f32[1,8,32]{2,1,0:T(8,128)S(1)} %broadcast.202), channel_id=1, source_target_pairs={{0,4},{4,8},{8,12},{12,16},{16,20},{20,24},{24,28},{1,5},{5,9},{9,... | collective-permute-start | bytes 3080 | tf_op jit(solution)/shard_map/ppermute | solution.py:17
  42.5 6.0 %collective-permute-start.4 = (f32[10,1,128]{2,1,0:T(1,128)S(1)}, f32[10,1,128]{2,1,0:T(1,128)S(1)}, u32[]{:S(2)}, u32[]{:S(2)}) collective-permute-start(f32[10,1,128]{2,1,0:T(1,128)S(1)} %get-tuple-element.23), channel_id=1, source_target_pairs={{1,0},{2,1},{3,2},{5,4},{6,5},{7,6},{9,8},{10,9},{11,10},{13,12},{... | collective-permute-start | bytes 15368 | tf_op jit(solution)/shard_map/ppermute | solution.py:18
  43.8 8.1 %collective-permute-start.5 = (f32[10,1,128]{2,1,0:T(1,128)S(1)}, f32[10,1,128]{2,1,0:T(1,128)S(1)}, u32[]{:S(2)}, u32[]{:S(2)}) collective-permute-start(f32[10,1,128]{2,1,0:T(1,128)S(1)} %get-tuple-element.22), channel_id=1, source_target_pairs={{0,1},{1,2},{2,3},{4,5},{5,6},{6,7},{8,9},{9,10},{10,11},{12,13},{... | collective-permute-start | bytes 15368 | tf_op jit(solution)/shard_map/ppermute | solution.py:17
  48.4 5.2 %collective-permute-start.6 = (f32[10,1,128]{2,1,0:T(1,128)S(1)}, f32[10,1,128]{2,1,0:T(1,128)S(1)}, u32[]{:S(2)}, u32[]{:S(2)}) collective-permute-start(f32[10,1,128]{2,1,0:T(1,128)S(1)} %get-tuple-element.24), channel_id=1, source_target_pairs={{0,1},{1,2},{2,3},{4,5},{5,6},{6,7},{8,9},{9,10},{10,11},{12,13},{... | collective-permute-start | bytes 15368 | tf_op jit(solution)/shard_map/ppermute | solution.py:17
  51.9 5.5 %collective-permute-start.7 = (f32[10,1,128]{2,1,0:T(1,128)S(1)}, f32[10,1,128]{2,1,0:T(1,128)S(1)}, u32[]{:S(2)}, u32[]{:S(2)}) collective-permute-start(f32[10,1,128]{2,1,0:T(1,128)S(1)} %get-tuple-element.25), channel_id=1, source_target_pairs={{1,0},{2,1},{3,2},{5,4},{6,5},{7,6},{9,8},{10,9},{11,10},{13,12},{... | collective-permute-start | bytes 15368 | tf_op jit(solution)/shard_map/ppermute | solution.py:18
  53.6 8.6 %collective-permute-start.43 = (f32[1,8,32]{2,1,0:T(8,128)S(1)}, f32[1,8,32]{2,1,0:T(8,128)S(1)}, u32[]{:S(2)}, u32[]{:S(2)}) collective-permute-start(f32[1,8,32]{2,1,0:T(8,128)S(1)} %broadcast.202), channel_id=1, source_target_pairs={{4,0},{8,4},{12,8},{16,12},{20,16},{24,20},{28,24},{5,1},{9,5},{13... | collective-permute-start | bytes 3080 | tf_op jit(solution)/shard_map/ppermute | solution.py:18
  57.4 13.8 %collective-permute-start.24 = (f32[1,16,64]{2,1,0:T(8,128)S(1)}, f32[1,16,64]{2,1,0:T(8,128)S(1)}, u32[]{:S(2)}, u32[]{:S(2)}) collective-permute-start(f32[1,16,64]{2,1,0:T(8,128)S(1)} %get-tuple-element.65), channel_id=1, source_target_pairs={{4,0},{8,4},{12,8},{16,12},{20,16},{24,20},{28,24},{5,1},{9,5},{13... | collective-permute-start | bytes 12296 | tf_op jit(solution)/shard_map/ppermute | solution.py:18
  62.2 7.7 %collective-permute-start.9 = (f32[1,32,128]{2,1,0:T(8,128)S(1)}, f32[1,32,128]{2,1,0:T(8,128)S(1)}, u32[]{:S(2)}, u32[]{:S(2)}) collective-permute-start(f32[1,32,128]{2,1,0:T(8,128)S(1)} %get-tuple-element.37), channel_id=1, source_target_pairs={{4,0},{8,4},{12,8},{16,12},{20,16},{24,20},{28,24},{5,1},{9,5},{13... | collective-permute-start | bytes 49160 | tf_op jit(solution)/shard_map/ppermute | solution.py:18
  63.6 12.3 %collective-permute-start.25 = (f32[1,16,64]{2,1,0:T(8,128)S(1)}, f32[1,16,64]{2,1,0:T(8,128)S(1)}, u32[]{:S(2)}, u32[]{:S(2)}) collective-permute-start(f32[1,16,64]{2,1,0:T(8,128)S(1)} %get-tuple-element.64), channel_id=1, source_target_pairs={{0,4},{4,8},{8,12},{12,16},{16,20},{20,24},{24,28},{1,5},{5,9},{9,... | collective-permute-start | bytes 12296 | tf_op jit(solution)/shard_map/ppermute | solution.py:17
  69.9 90.2 %collective-permute-start.44 = (f32[4,1,32]{2,1,0:T(1,128)S(1)}, f32[4,1,32]{2,1,0:T(1,128)S(1)}, u32[]{:S(2)}, u32[]{:S(2)}) collective-permute-start(f32[4,1,32]{2,1,0:T(1,128)S(1)} %get-tuple-element.77), channel_id=1, source_target_pairs={{1,0},{2,1},{3,2},{5,4},{6,5},{7,6},{9,8},{10,9},{11,10},{13,12},{... | collective-permute-start | bytes 1544 | tf_op jit(solution)/shard_map/ppermute | solution.py:18
  71.3 5.9 %collective-permute-start.10 = (f32[10,1,128]{2,1,0:T(1,128)S(1)}, f32[10,1,128]{2,1,0:T(1,128)S(1)}, u32[]{:S(2)}, u32[]{:S(2)}) collective-permute-start(f32[10,1,128]{2,1,0:T(1,128)S(1)} %get-tuple-element.20), channel_id=1, source_target_pairs={{0,1},{1,2},{2,3},{4,5},{5,6},{6,7},{8,9},{9,10},{10,11},{12,13},{... | collective-permute-start | bytes 15368 | tf_op jit(solution)/shard_map/ppermute | solution.py:17
  75.8 5.5 %collective-permute-start.11 = (f32[10,1,128]{2,1,0:T(1,128)S(1)}, f32[10,1,128]{2,1,0:T(1,128)S(1)}, u32[]{:S(2)}, u32[]{:S(2)}) collective-permute-start(f32[10,1,128]{2,1,0:T(1,128)S(1)} %get-tuple-element.21), channel_id=1, source_target_pairs={{1,0},{2,1},{3,2},{5,4},{6,5},{7,6},{9,8},{10,9},{11,10},{13,12},{... | collective-permute-start | bytes 15368 | tf_op jit(solution)/shard_map/ppermute | solution.py:18
  83.8 5.7 %collective-permute-start.13 = (f32[1,32,128]{2,1,0:T(8,128)S(1)}, f32[1,32,128]{2,1,0:T(8,128)S(1)}, u32[]{:S(2)}, u32[]{:S(2)}) collective-permute-start(f32[1,32,128]{2,1,0:T(8,128)S(1)} %get-tuple-element.35), channel_id=1, source_target_pairs={{4,0},{8,4},{12,8},{16,12},{20,16},{24,20},{28,24},{5,1},{9,5},{13... | collective-permute-start | bytes 49160 | tf_op jit(solution)/shard_map/ppermute | solution.py:18
  85.2 76.3 %collective-permute-start.45 = (f32[4,1,32]{2,1,0:T(1,128)S(1)}, f32[4,1,32]{2,1,0:T(1,128)S(1)}, u32[]{:S(2)}, u32[]{:S(2)}) collective-permute-start(f32[4,1,32]{2,1,0:T(1,128)S(1)} %get-tuple-element.76), channel_id=1, source_target_pairs={{0,1},{1,2},{2,3},{4,5},{5,6},{6,7},{8,9},{9,10},{10,11},{12,13},{... | collective-permute-start | bytes 1544 | tf_op jit(solution)/shard_map/ppermute | solution.py:17
  89.6 88.3 %collective-permute-start.46 = (f32[4,1,32]{2,1,0:T(1,128)S(1)}, f32[4,1,32]{2,1,0:T(1,128)S(1)}, u32[]{:S(2)}, u32[]{:S(2)}) collective-permute-start(f32[4,1,32]{2,1,0:T(1,128)S(1)} %get-tuple-element.78), channel_id=1, source_target_pairs={{0,1},{1,2},{2,3},{4,5},{5,6},{6,7},{8,9},{9,10},{10,11},{12,13},{... | collective-permute-start | bytes 1544 | tf_op jit(solution)/shard_map/ppermute | solution.py:17
  93.2 4.8 %collective-permute-start.14 = (f32[10,1,128]{2,1,0:T(1,128)S(1)}, f32[10,1,128]{2,1,0:T(1,128)S(1)}, u32[]{:S(2)}, u32[]{:S(2)}) collective-permute-start(f32[10,1,128]{2,1,0:T(1,128)S(1)} %get-tuple-element.18), channel_id=1, source_target_pairs={{0,1},{1,2},{2,3},{4,5},{5,6},{6,7},{8,9},{9,10},{10,11},{12,13},{... | collective-permute-start | bytes 15368 | tf_op jit(solution)/shard_map/ppermute | solution.py:17
  96.7 5.5 %collective-permute-start.15 = (f32[10,1,128]{2,1,0:T(1,128)S(1)}, f32[10,1,128]{2,1,0:T(1,128)S(1)}, u32[]{:S(2)}, u32[]{:S(2)}) collective-permute-start(f32[10,1,128]{2,1,0:T(1,128)S(1)} %get-tuple-element.19), channel_id=1, source_target_pairs={{1,0},{2,1},{3,2},{5,4},{6,5},{7,6},{9,8},{10,9},{11,10},{13,12},{... | collective-permute-start | bytes 15368 | tf_op jit(solution)/shard_map/ppermute | solution.py:18
  98.0 7.0 %collective-permute-start.28 = (f32[6,1,64]{2,1,0:T(1,128)S(1)}, f32[6,1,64]{2,1,0:T(1,128)S(1)}, u32[]{:S(2)}, u32[]{:S(2)}) collective-permute-start(f32[6,1,64]{2,1,0:T(1,128)S(1)} %get-tuple-element.53), channel_id=1, source_target_pairs={{1,0},{2,1},{3,2},{5,4},{6,5},{7,6},{9,8},{10,9},{11,10},{13,12},{... | collective-permute-start | bytes 4616 | tf_op jit(solution)/shard_map/ppermute | solution.py:18
  102.2 6.1 %collective-permute-start.29 = (f32[6,1,64]{2,1,0:T(1,128)S(1)}, f32[6,1,64]{2,1,0:T(1,128)S(1)}, u32[]{:S(2)}, u32[]{:S(2)}) collective-permute-start(f32[6,1,64]{2,1,0:T(1,128)S(1)} %get-tuple-element.52), channel_id=1, source_target_pairs={{0,1},{1,2},{2,3},{4,5},{5,6},{6,7},{8,9},{9,10},{10,11},{12,13},{... | collective-permute-start | bytes 4616 | tf_op jit(solution)/shard_map/ppermute | solution.py:17
  112.6 5.3 %collective-permute-start.18 = (f32[10,1,128]{2,1,0:T(1,128)S(1)}, f32[10,1,128]{2,1,0:T(1,128)S(1)}, u32[]{:S(2)}, u32[]{:S(2)}) collective-permute-start(f32[10,1,128]{2,1,0:T(1,128)S(1)} %get-tuple-element.16), channel_id=1, source_target_pairs={{0,1},{1,2},{2,3},{4,5},{5,6},{6,7},{8,9},{9,10},{10,11},{12,13},{... | collective-permute-start | bytes 15368 | tf_op jit(solution)/shard_map/ppermute | solution.py:17
  116.5 6.0 %collective-permute-start.19 = (f32[10,1,128]{2,1,0:T(1,128)S(1)}, f32[10,1,128]{2,1,0:T(1,128)S(1)}, u32[]{:S(2)}, u32[]{:S(2)}) collective-permute-start(f32[10,1,128]{2,1,0:T(1,128)S(1)} %get-tuple-element.17), channel_id=1, source_target_pairs={{1,0},{2,1},{3,2},{5,4},{6,5},{7,6},{9,8},{10,9},{11,10},{13,12},{... | collective-permute-start | bytes 15368 | tf_op jit(solution)/shard_map/ppermute | solution.py:18
  117.9 6.3 %collective-permute-start.30 = (f32[6,1,64]{2,1,0:T(1,128)S(1)}, f32[6,1,64]{2,1,0:T(1,128)S(1)}, u32[]{:S(2)}, u32[]{:S(2)}) collective-permute-start(f32[6,1,64]{2,1,0:T(1,128)S(1)} %get-tuple-element.54), channel_id=1, source_target_pairs={{0,1},{1,2},{2,3},{4,5},{5,6},{6,7},{8,9},{9,10},{10,11},{12,13},{... | collective-permute-start | bytes 4616 | tf_op jit(solution)/shard_map/ppermute | solution.py:17
  122.5 5.5 %collective-permute-start.31 = (f32[6,1,64]{2,1,0:T(1,128)S(1)}, f32[6,1,64]{2,1,0:T(1,128)S(1)}, u32[]{:S(2)}, u32[]{:S(2)}) collective-permute-start(f32[6,1,64]{2,1,0:T(1,128)S(1)} %get-tuple-element.55), channel_id=1, source_target_pairs={{1,0},{2,1},{3,2},{5,4},{6,5},{7,6},{9,8},{10,9},{11,10},{13,12},{... | collective-permute-start | bytes 4616 | tf_op jit(solution)/shard_map/ppermute | solution.py:18
  124.2 5.1 %collective-permute-start.20 = (f32[1,32,128]{2,1,0:T(8,128)S(1)}, f32[1,32,128]{2,1,0:T(8,128)S(1)}, u32[]{:S(2)}, u32[]{:S(2)}) collective-permute-start(f32[1,32,128]{2,1,0:T(8,128)S(1)} %get-tuple-element.30), channel_id=1, source_target_pairs={{0,4},{4,8},{8,12},{12,16},{16,20},{20,24},{24,28},{1,5},{5,9},{9,... | collective-permute-start | bytes 49160 | tf_op jit(solution)/shard_map/ppermute | solution.py:17
  132.3 5.9 %collective-permute-start.22 = (f32[10,1,128]{2,1,0:T(1,128)S(1)}, f32[10,1,128]{2,1,0:T(1,128)S(1)}, u32[]{:S(2)}, u32[]{:S(2)}) collective-permute-start(f32[10,1,128]{2,1,0:T(1,128)S(1)} %get-tuple-element.14), channel_id=1, source_target_pairs={{0,1},{1,2},{2,3},{4,5},{5,6},{6,7},{8,9},{9,10},{10,11},{12,13},{... | collective-permute-start | bytes 15368 | tf_op jit(solution)/shard_map/ppermute | solution.py:17
  136.9 5.5 %collective-permute-start.23 = (f32[10,1,128]{2,1,0:T(1,128)S(1)}, f32[10,1,128]{2,1,0:T(1,128)S(1)}, u32[]{:S(2)}, u32[]{:S(2)}) collective-permute-start(f32[10,1,128]{2,1,0:T(1,128)S(1)} %get-tuple-element.15), channel_id=1, source_target_pairs={{1,0},{2,1},{3,2},{5,4},{6,5},{7,6},{9,8},{10,9},{11,10},{13,12},{... | collective-permute-start | bytes 15368 | tf_op jit(solution)/shard_map/ppermute | solution.py:18
  138.2 39.7 %collective-permute-start.47 = (f32[4,1,32]{2,1,0:T(1,128)S(1)}, f32[4,1,32]{2,1,0:T(1,128)S(1)}, u32[]{:S(2)}, u32[]{:S(2)}) collective-permute-start(f32[4,1,32]{2,1,0:T(1,128)S(1)} %get-tuple-element.79), channel_id=1, source_target_pairs={{1,0},{2,1},{3,2},{5,4},{6,5},{7,6},{9,8},{10,9},{11,10},{13,12},{... | collective-permute-start | bytes 1544 | tf_op jit(solution)/shard_map/ppermute | solution.py:18
  156.7 4.9 %collective-permute-start.32 = (f32[1,16,64]{2,1,0:T(8,128)S(1)}, f32[1,16,64]{2,1,0:T(8,128)S(1)}, u32[]{:S(2)}, u32[]{:S(2)}) collective-permute-start(f32[1,16,64]{2,1,0:T(8,128)S(1)} %get-tuple-element.62), channel_id=1, source_target_pairs={{0,4},{4,8},{8,12},{12,16},{16,20},{20,24},{24,28},{1,5},{5,9},{9,... | collective-permute-start | bytes 12296 | tf_op jit(solution)/shard_map/ppermute | solution.py:17
  166.9 5.5 %collective-permute-start.35 = (f32[6,1,64]{2,1,0:T(1,128)S(1)}, f32[6,1,64]{2,1,0:T(1,128)S(1)}, u32[]{:S(2)}, u32[]{:S(2)}) collective-permute-start(f32[6,1,64]{2,1,0:T(1,128)S(1)} %get-tuple-element.51), channel_id=1, source_target_pairs={{1,0},{2,1},{3,2},{5,4},{6,5},{7,6},{9,8},{10,9},{11,10},{13,12},{... | collective-permute-start | bytes 4616 | tf_op jit(solution)/shard_map/ppermute | solution.py:18
  172.6 5.4 %collective-permute-start.36 = (f32[1,16,64]{2,1,0:T(8,128)S(1)}, f32[1,16,64]{2,1,0:T(8,128)S(1)}, u32[]{:S(2)}, u32[]{:S(2)}) collective-permute-start(f32[1,16,64]{2,1,0:T(8,128)S(1)} %get-tuple-element.60), channel_id=1, source_target_pairs={{0,4},{4,8},{8,12},{12,16},{16,20},{20,24},{24,28},{1,5},{5,9},{9,... | collective-permute-start | bytes 12296 | tf_op jit(solution)/shard_map/ppermute | solution.py:17
  180.6 5.1 %collective-permute-start.38 = (f32[6,1,64]{2,1,0:T(1,128)S(1)}, f32[6,1,64]{2,1,0:T(1,128)S(1)}, u32[]{:S(2)}, u32[]{:S(2)}) collective-permute-start(f32[6,1,64]{2,1,0:T(1,128)S(1)} %get-tuple-element.48), channel_id=1, source_target_pairs={{0,1},{1,2},{2,3},{4,5},{5,6},{6,7},{8,9},{9,10},{10,11},{12,13},{... | collective-permute-start | bytes 4616 | tf_op jit(solution)/shard_map/ppermute | solution.py:17
  184.5 5.5 %collective-permute-start.39 = (f32[6,1,64]{2,1,0:T(1,128)S(1)}, f32[6,1,64]{2,1,0:T(1,128)S(1)}, u32[]{:S(2)}, u32[]{:S(2)}) collective-permute-start(f32[6,1,64]{2,1,0:T(1,128)S(1)} %get-tuple-element.49), channel_id=1, source_target_pairs={{1,0},{2,1},{3,2},{5,4},{6,5},{7,6},{9,8},{10,9},{11,10},{13,12},{... | collective-permute-start | bytes 4616 | tf_op jit(solution)/shard_map/ppermute | solution.py:18
  194.5 4.8 %collective-permute-start.49 = (f32[1,8,32]{2,1,0:T(8,128)S(1)}, f32[1,8,32]{2,1,0:T(8,128)S(1)}, u32[]{:S(2)}, u32[]{:S(2)}) collective-permute-start(f32[1,8,32]{2,1,0:T(8,128)S(1)} %get-tuple-element.91), channel_id=1, source_target_pairs={{4,0},{8,4},{12,8},{16,12},{20,16},{24,20},{28,24},{5,1},{9,5},{13... | collective-permute-start | bytes 3080 | tf_op jit(solution)/shard_map/ppermute | solution.py:18
  201.2 5.5 %collective-permute-start.51 = (f32[4,1,32]{2,1,0:T(1,128)S(1)}, f32[4,1,32]{2,1,0:T(1,128)S(1)}, u32[]{:S(2)}, u32[]{:S(2)}) collective-permute-start(f32[4,1,32]{2,1,0:T(1,128)S(1)} %get-tuple-element.75), channel_id=1, source_target_pairs={{1,0},{2,1},{3,2},{5,4},{6,5},{7,6},{9,8},{10,9},{11,10},{13,12},{... | collective-permute-start | bytes 1544 | tf_op jit(solution)/shard_map/ppermute | solution.py:18
  216.6 5.5 %collective-permute-start.55 = (f32[4,1,32]{2,1,0:T(1,128)S(1)}, f32[4,1,32]{2,1,0:T(1,128)S(1)}, u32[]{:S(2)}, u32[]{:S(2)}) collective-permute-start(f32[4,1,32]{2,1,0:T(1,128)S(1)} %get-tuple-element.73), channel_id=1, source_target_pairs={{1,0},{2,1},{3,2},{5,4},{6,5},{7,6},{9,8},{10,9},{11,10},{13,12},{... | collective-permute-start | bytes 1544 | tf_op jit(solution)/shard_map/ppermute | solution.py:18
  224.7 5.3 %collective-permute-start.57 = (f32[2,2,4,16]{3,2,1,0:T(4,128)S(1)}, f32[2,2,4,16]{3,2,1,0:T(4,128)S(1)}, u32[]{:S(2)}, u32[]{:S(2)}) collective-permute-start(f32[2,2,4,16]{3,2,1,0:T(4,128)S(1)} %maximum_select_fusion.2), channel_id=1, source_target_pairs={{0,8},{4,12},{8,0},{12,4},{16,24},{20,28},{24,16},{28,20},{1,9},{5... | collective-permute-start | bytes 3080 | tf_op jit(solution)/shard_map/ppermute | solution.py:26
  263.1 5.1 %collective-permute-start.60 = (f32[1,8,32]{2,1,0:T(8,128)S(1)}, f32[1,8,32]{2,1,0:T(8,128)S(1)}, u32[]{:S(2)}, u32[]{:S(2)}) collective-permute-start(f32[1,8,32]{2,1,0:T(8,128)S(1)} %get-tuple-element.83), channel_id=1, source_target_pairs={{4,0},{8,4},{12,8},{16,12},{20,16},{24,20},{28,24},{5,1},{9,5},{13... | collective-permute-start | bytes 3080 | tf_op jit(solution)/shard_map/ppermute | solution.py:18
  269.6 5.5 %collective-permute-start.62 = (f32[4,1,32]{2,1,0:T(1,128)S(1)}, f32[4,1,32]{2,1,0:T(1,128)S(1)}, u32[]{:S(2)}, u32[]{:S(2)}) collective-permute-start(f32[4,1,32]{2,1,0:T(1,128)S(1)} %get-tuple-element.71), channel_id=1, source_target_pairs={{1,0},{2,1},{3,2},{5,4},{6,5},{7,6},{9,8},{10,9},{11,10},{13,12},{... | collective-permute-start | bytes 1544 | tf_op jit(solution)/shard_map/ppermute | solution.py:18
  282.5 5.0 %collective-permute-start.65 = (f32[6,1,64]{2,1,0:T(1,128)S(1)}, f32[6,1,64]{2,1,0:T(1,128)S(1)}, u32[]{:S(2)}, u32[]{:S(2)}) collective-permute-start(f32[6,1,64]{2,1,0:T(1,128)S(1)} %get-tuple-element.46), channel_id=1, source_target_pairs={{0,1},{1,2},{2,3},{4,5},{5,6},{6,7},{8,9},{9,10},{10,11},{12,13},{... | collective-permute-start | bytes 4616 | tf_op jit(solution)/shard_map/ppermute | solution.py:17
  286.2 5.5 %collective-permute-start.66 = (f32[6,1,64]{2,1,0:T(1,128)S(1)}, f32[6,1,64]{2,1,0:T(1,128)S(1)}, u32[]{:S(2)}, u32[]{:S(2)}) collective-permute-start(f32[6,1,64]{2,1,0:T(1,128)S(1)} %get-tuple-element.47), channel_id=1, source_target_pairs={{1,0},{2,1},{3,2},{5,4},{6,5},{7,6},{9,8},{10,9},{11,10},{13,12},{... | collective-permute-start | bytes 4616 | tf_op jit(solution)/shard_map/ppermute | solution.py:18
  (22 other events, 172.2 us)
where the time goes:
time: 297 us; the launch traced here: 293 us
  starting transfers between devices  159 us (54%)
  waiting for transfers between devices  66.8 us (22%)
  local copies, waits for them, and re-layouts  24.6 us (8%)
  other arithmetic  19.1 us (6%)
  blocking collectives  13.4 us (5%)
  between operations  10.5 us (4%)
    ppermute x32, starting transfers between devices, with_halo(): before = lax.ppermute(last, axis, up)  110 us
    ppermute x32, waiting for transfers between devices, with_halo(): after = lax.ppermute(initial, axis, down)  62.5 us
    ppermute x32, starting transfers between devices, with_halo(): after = lax.ppermute(initial, axis, down)  41.5 us
    reshape x3, local copies, waits for them, and re-layouts, restrict(): field.reshape(size_x // 2, 2, size_y // 2, 2, size_z // 2, 2)  21.4 us
    all_gather x1, blocking collectives, agglomerate(): merged = lax.all_gather(merged, 'gy', axis=2, tiled=True)  13.4 us
    reduce_sum x8, other arithmetic, restrict(): field.reshape(size_x // 2, 2, size_y // 2, 2, size_z // 2, 2)  8.64 us
    ppermute x3, starting transfers between devices, swapped(): return lax.ppermute(value, axis, pairs)  7.4 us
  transfers between devices with their start and end apart: 67, of which 23 were waited for; matrix products, arithmetic and copies ran while one was open for 12% of the time, Pallas kernels for 0%

commit v1 on v0

v1 whole, which is shorter than its diff:
```python
import functools
import jax
import jax.numpy as jnp
from jax import lax
from jax.experimental import pallas as pl
from jax.experimental.pallas import tpu as pltpu
from jax.sharding import PartitionSpec as P

CSWEEPS = 4
REACH = 9
ORIGIN = 16
VMEM_LIMIT = 48 * 1024 * 1024


def y_rows(distance):
    return REACH if distance <= 2 else REACH + 2 - distance


def y_plan(cells_x):
    pieces = []
    start = 0
    for array in range(3):
        for plane in range(cells_x + 2 * REACH):
            x = plane - REACH
            distance = max(0, -x, x - cells_x + 1)
            if array == 1 and distance == REACH:
                continue
            rows = y_rows(distance)
            pieces.append((array, plane, start, rows))
            start += rows
    return pieces, -(-start // 8) * 8


def shifts(axis, step):
    count = lax.axis_size(axis)
    return [(i, i + step) for i in range(count) if 0 <= i + step < count]


def plane_source(array, plane, cells_x, own, low, high, low2, high2):
    x = plane - REACH
    far = 0 if array == 0 else 1
    if x < -cells_x:
        return low2, far
    if x < 0:
        return low, array * cells_x + cells_x + x
    if x < cells_x:
        return own[array], x
    if x < 2 * cells_x:
        return high, array * cells_x + x - cells_x
    return high2, far


def pack_kernel(p, f, k, low, high, low2, high2, to_up, to_down):
    cells_x, cells_y, _ = p.shape
    pieces, _ = y_plan(cells_x)
    for array, plane, start, rows in pieces:
        ref, index = plane_source(array, plane, cells_x, (p, f, k), low, high, low2, high2)
        to_up[pl.ds(start, rows), :] = ref[index, pl.ds(cells_y - rows, rows), :]
        to_down[pl.ds(start, rows), :] = ref[index, pl.ds(0, rows), :]


def fine_halo(pressure, source, coefficient):
    cells_x, _, depth = pressure.shape
    block = jnp.concatenate([pressure, source, coefficient], 0)
    far_up = jnp.concatenate([pressure[-1:], coefficient[-1:]], 0)
    far_down = jnp.concatenate([pressure[:1], coefficient[:1]], 0)
    low = lax.ppermute(block, "gx", shifts("gx", 1))
    high = lax.ppermute(block, "gx", shifts("gx", -1))
    low2 = lax.ppermute(far_up, "gx", shifts("gx", 2))
    high2 = lax.ppermute(far_down, "gx", shifts("gx", -2))
    _, length = y_plan(cells_x)
    packed = jax.ShapeDtypeStruct((length, depth), jnp.float32)
    to_up, to_down = pl.pallas_call(
        pack_kernel,
        out_shape=(packed, packed),
        compiler_params=pltpu.CompilerParams(vmem_limit_bytes=VMEM_LIMIT),
        name="pack_halo",
    )(pressure, source, coefficient, low, high, low2, high2)
    below = lax.ppermute(to_up, "gy", shifts("gy", 1))
    above = lax.ppermute(to_down, "gy", shifts("gy", -1))
    return low, high, low2, high2, below, above


def smooth_kernel(
    p, f, k, low, high, low2, high2, below, above,
    out, error_one, tiles,
    vp, vf, vk, wx, wy, zl, zh, dg, inv, va, vb,
    t0, t1, f1, k1, inv1, g1, h1, q2,
):
    cells_x, cells_y, depth = p.shape
    planes = cells_x + 2 * REACH
    own_rows = pl.ds(ORIGIN, cells_y)
    top = ORIGIN - REACH + 1
    rows = cells_y + 2 * (REACH - 1)
    body = pl.ds(top, rows)

    for array, window in ((0, vp), (1, vf), (2, vk)):
        for plane in range(planes):
            if array == 1 and plane in (0, planes - 1):
                continue
            ref, index = plane_source(array, plane, cells_x, (p, f, k), low, high, low2, high2)
            value = ref[index]
            window[plane, own_rows, :] = value + value if array == 1 else value
    pieces, _ = y_plan(cells_x)
    for array, plane, start, count in pieces:
        window = (vp, vf, vk)[array]
        before = below[pl.ds(start, count), :]
        after = above[pl.ds(start, count), :]
        if array == 1:
            before = before + before
            after = after + after
        window[plane, pl.ds(ORIGIN - count, count), :] = before
        window[plane, pl.ds(ORIGIN + cells_y, count), :] = after

    def lanes(count):
        return lax.broadcasted_iota(jnp.int32, (count, depth), 1)

    def rows_of(first, count):
        return lax.broadcasted_iota(jnp.int32, (count, depth), 0) + (first - ORIGIN)

    lane = lanes(rows)

    def weigh(plane, _):
        centre = vk[plane, body, :]
        west = centre + vk[plane - 1, body, :]
        wx[plane, body, :] = west
        east = centre + vk[plane + 1, body, :]
        south = centre + vk[plane, pl.ds(top - 1, rows), :]
        north = centre + vk[plane, pl.ds(top + 1, rows), :]
        wy[plane, body, :] = south
        wy[plane, pl.ds(top + rows, 1), :] = north[rows - 1:, :]
        down = jnp.where(lane > 0, pltpu.roll(centre, 1, 1), 0.0)
        up = jnp.where(lane < depth - 1, pltpu.roll(centre, depth - 1, 1), 0.0)
        total = west + east + south + north + (centre + down) + (centre + up)
        zl[plane, body, :] = jnp.where(lane > 0, centre + down, 0.0)
        zh[plane, body, :] = jnp.where(lane < depth - 1, centre + up, 0.0)
        dg[plane, body, :] = total
        inside = centre > 0.0
        inv[plane, body, :] = jnp.where(inside, 1.0 / jnp.where(inside, total, 1.0), 0.0)
        return 0

    lax.fori_loop(1, planes - 1, weigh, 0)
    wx[planes - 1, body, :] = vk[planes - 1, body, :] + vk[planes - 2, body, :]

    def stencil(v, plane, first, count):
        here = pl.ds(first, count)
        centre = v[plane, here, :]
        total = wx[plane, here, :] * v[plane - 1, here, :] + wx[plane + 1, here, :] * v[plane + 1, here, :]
        total += wy[plane, here, :] * v[plane, pl.ds(first - 1, count), :]
        total += wy[plane, pl.ds(first + 1, count), :] * v[plane, pl.ds(first + 1, count), :]
        total += zl[plane, here, :] * pltpu.roll(centre, 1, 1)
        total += zh[plane, here, :] * pltpu.roll(centre, depth - 1, 1)
        return total

    def relax(source_ref, target, reach):
        def one(plane, _):
            total = stencil(source_ref, plane, top, rows)
            target[plane, body, :] = inv[plane, body, :] * (vf[plane, body, :] + total)
            return 0

        lax.fori_loop(REACH - reach, REACH + cells_x + reach, one, 0)

    relax(vp, va, REACH - 1)
    relax(va, vb, REACH - 2)
    relax(vb, va, REACH - 3)
    relax(va, vb, REACH - 4)

    own_lane = lanes(cells_y)
    own_row = rows_of(ORIGIN, cells_y)
    for x in range(cells_x):
        even = ((own_row + own_lane + x) & 1) == 0
        out[x] = jnp.where(even, va[REACH + x, own_rows, :], vb[REACH + x, own_rows, :])

    planes_one = cells_x // 2
    first = ORIGIN - 4
    count = cells_y + 8
    lane = lanes(count)
    row = rows_of(first, count)

    def pair_lane(value, stride, lane):
        up = pltpu.roll(value, depth - stride, 1)
        down = pltpu.roll(value, stride, 1)
        return value + jnp.where((lane & stride) == 0, up, down)

    def pair_row(ref, index, first, count, stride, row):
        centre = ref[index, pl.ds(first, count), :]
        up = ref[index, pl.ds(first + stride, count), :]
        down = ref[index, pl.ds(first - stride, count), :]
        return centre + jnp.where((row & stride) == 0, up, down)

    def residual(plane_one, _):
        total = jnp.zeros((count, depth), jnp.float32)
        for half in range(2):
            plane = 2 * plane_one + REACH - 4 + half
            here = pl.ds(first, count)
            twice = vf[plane, here, :] - dg[plane, here, :] * va[plane, here, :] + stencil(vb, plane, first, count)
            even = ((row + lane + half) & 1) == 0
            total += jnp.where(even, twice, 0.0)
        t0[plane_one, pl.ds(first, count), :] = pair_lane(total, 1, lane)
        return 0

    lax.fori_loop(0, planes_one + 4, residual, 0)
    for x in range(planes_one + 4):
        f1[x, pl.ds(first, count), :] = 0.5 * pair_row(t0, x, first, count, 1, row)

    first_k = ORIGIN - 6
    count_k = cells_y + 16
    lane_k = lanes(count_k)
    row_k = rows_of(first_k, count_k)
    for x in range(planes_one + 6):
        plane = 2 * x + REACH - 6
        here = pl.ds(first_k, count_k)
        t1[x, here, :] = pair_lane(vk[plane, here, :] + vk[plane + 1, here, :], 1, lane_k)
    for x in range(planes_one + 6):
        k1[x, pl.ds(first_k, count_k), :] = 0.125 * pair_row(t1, x, first_k, count_k, 1, row_k)

    def down2(value, lane):
        return jnp.where(lane >= 2, pltpu.roll(value, 2, 1), 0.0)

    def up2(value, lane):
        return jnp.where(lane < depth - 2, pltpu.roll(value, depth - 2, 1), 0.0)

    here = pl.ds(first, count)
    for x in range(planes_one + 4):
        centre = k1[x + 1, here, :]
        total = 6.0 * centre + (k1[x, here, :] + k1[x + 2, here, :])
        total += k1[x + 1, pl.ds(first - 2, count), :] + k1[x + 1, pl.ds(first + 2, count), :]
        total += down2(centre, lane) + up2(centre, lane)
        inside = centre > 0.0
        inverse = jnp.where(inside, 1.0 / jnp.where(inside, total, 1.0), 0.0)
        inv1[x, here, :] = inverse
        g1[x, here, :] = inverse * f1[x, here, :]

    def stencil_one(v, x, v_x, first, count, lane):
        here = pl.ds(first, count)
        south = pl.ds(first - 2, count)
        north = pl.ds(first + 2, count)
        kc = k1[x, here, :]
        vc = v[v_x, here, :]
        total = (kc + k1[x - 1, here, :]) * v[v_x - 1, here, :] + (kc + k1[x + 1, here, :]) * v[v_x + 1, here, :]
        total += (kc + k1[x, south, :]) * v[v_x, south, :] + (kc + k1[x, north, :]) * v[v_x, north, :]
        total += (kc + down2(kc, lane)) * down2(vc, lane) + (kc + up2(kc, lane)) * up2(vc, lane)
        return total

    first_h = ORIGIN - 2
    count_h = cells_y + 8
    lane_h = lanes(count_h)
    row_h = rows_of(first_h, count_h)
    for x in range(planes_one + 2):
        here = pl.ds(first_h, count_h)
        total = stencil_one(g1, x + 2, x + 1, first_h, count_h, lane_h)
        odd = inv1[x + 1, here, :] * (f1[x + 1, here, :] + total)
        h1[x, here, :] = odd
        even_cell = ((x - 1 + (row_h >> 1) + (lane_h >> 1)) & 1) == 0
        error_one[x, pl.ds(first_h - 8, count_h), :] = jnp.where(even_cell, g1[x + 1, here, :], odd)

    own2 = own_lane
    row2 = own_row
    for x in range(planes_one // 2):
        sum_r = jnp.zeros((cells_y, depth), jnp.float32)
        for half in range(2):
            x1 = 2 * x + half
            total = stencil_one(h1, x1 + 3, x1 + 1, ORIGIN, cells_y, own2)
            even_cell = ((x1 + (row2 >> 1) + (own2 >> 1)) & 1) == 0
            sum_r += jnp.where(even_cell, total, 0.0)
        sum_k = k1[2 * x + 3, own_rows, :] + k1[2 * x + 4, own_rows, :]
        t0[x, own_rows, :] = pair_lane(sum_r, 2, own2)
        t1[x, own_rows, :] = pair_lane(sum_k, 2, own2)
    lane8 = lanes(cells_y // 4)
    tile = jnp.zeros((cells_y // 4, depth), jnp.float32)
    for x in range(planes_one // 2):
        q2[0] = (1.0 / 64.0) * pair_row(t0, x, ORIGIN, cells_y, 2, row2)
        q2[1] = 0.125 * pair_row(t1, x, ORIGIN, cells_y, 2, row2)
        for field in range(2):
            kept = q2[field, pl.ds(0, cells_y // 4, stride=4), :]
            tile = jnp.where((lane8 & 3) == 2 * field + x, kept, tile)
    tiles[...] = jnp.broadcast_to(tile[None], tiles.shape)


def smooth(copies, pressure, source, coefficient, halo):
    cells_x, cells_y, depth = pressure.shape
    planes = cells_x + 2 * REACH
    tall = cells_y + 2 * ORIGIN
    planes_one = cells_x // 2
    window = pltpu.VMEM((planes, tall, depth), jnp.float32)

    def level_one(count):
        return pltpu.VMEM((count, tall, depth), jnp.float32)

    return pl.pallas_call(
        smooth_kernel,
        out_shape=(
            jax.ShapeDtypeStruct((cells_x, cells_y, depth), jnp.float32),
            jax.ShapeDtypeStruct((planes_one + 2, cells_y + 16, depth), jnp.float32),
            jax.ShapeDtypeStruct((copies, cells_y // 4, depth), jnp.float32),
        ),
        scratch_shapes=[window] * 11
        + [
            level_one(planes_one + 4),
            level_one(planes_one + 6),
            level_one(planes_one + 4),
            level_one(planes_one + 6),
            level_one(planes_one + 4),
            level_one(planes_one + 4),
            level_one(planes_one + 2),
            pltpu.VMEM((2, cells_y, depth), jnp.float32),
        ],
        compiler_params=pltpu.CompilerParams(vmem_limit_bytes=VMEM_LIMIT),
        name="smooth",
    )(pressure, source, coefficient, *halo)


def ring(value, shift, axis):
    return pltpu.roll(value, shift % value.shape[axis], axis)


def before_x(v):
    return jnp.concatenate([jnp.zeros_like(v[:1]), v[:-1]], 0)


def after_x(v):
    return jnp.concatenate([v[1:], jnp.zeros_like(v[:1])], 0)


class Places:
    def __init__(self, shape):
        self.row = lax.broadcasted_iota(jnp.int32, shape, 1)
        self.lane = lax.broadcasted_iota(jnp.int32, shape, 2)
        self.part = self.lane & 3
        self.depth = shape[2]

    def before_y(self, v, stride):
        turned = ring(v, stride, 1)
        return jnp.where(self.row >= stride, turned, ring(turned, 1, 2))

    def after_y(self, v, stride):
        turned = ring(v, -stride, 1)
        return jnp.where(self.row < 8 - stride, turned, ring(turned, -1, 2))

    def has_before_y(self, stride):
        return (self.row >= stride) | (self.part > 0)

    def has_after_y(self, stride):
        return (self.row < 8 - stride) | (self.part < 3)

    def has_before_z(self, stride):
        return self.lane >= 4 * stride

    def has_after_z(self, stride):
        return self.lane < self.depth - 4 * stride


def whole_weights(k, places, stride):
    west = k + before_x(k)
    east = k + after_x(k)
    masks = (
        places.has_before_y(stride),
        places.has_after_y(stride),
        places.has_before_z(stride),
        places.has_after_z(stride),
    )
    near = (
        places.before_y(k, stride),
        places.after_y(k, stride),
        ring(k, 4 * stride, 2),
        ring(k, -4 * stride, 2),
    )
    diagonal = west + east
    weights = [west, east]
    for mask, value in zip(masks, near):
        diagonal += k + jnp.where(mask, value, 0.0)
        weights.append(jnp.where(mask, k + value, 0.0))
    return weights, diagonal


def whole_sum(v, weights, places, stride):
    total = weights[0] * before_x(v) + weights[1] * after_x(v)
    total += weights[2] * places.before_y(v, stride) + weights[3] * places.after_y(v, stride)
    total += weights[4] * ring(v, 4 * stride, 2) + weights[5] * ring(v, -4 * stride, 2)
    return total


def whole_solve(k2, rhs2):
    planes = k2.shape[0]
    places = Places(k2.shape)
    weights, diagonal = whole_weights(k2, places, 1)
    parity = lax.broadcasted_iota(jnp.int32, k2.shape, 0) + places.row + (places.lane >> 2)
    even = (parity & 1) == 0
    inverse = 1.0 / diagonal
    scaled = 32.0 * rhs2
    even_values = inverse * scaled
    odd_values = inverse * (scaled + whole_sum(even_values, weights, places, 1))
    error_two = jnp.where(even, even_values, odd_values)
    left = jnp.where(even, whole_sum(odd_values, weights, places, 1), 0.0)

    half = places.row[: planes // 2] , places.lane[: planes // 2]
    first_row = (half[0] & 1) == 0
    first_lane = (half[1] & 4) == 0

    def coarse(v):
        v = v.reshape(planes // 2, 2, *v.shape[1:])
        v = v[:, 0] + v[:, 1]
        v = v + jnp.where(first_row, ring(v, -1, 1), ring(v, 1, 1))
        return v + jnp.where(first_lane, ring(v, -4, 2), ring(v, 4, 2))

    remain = (1.0 / 256.0) * coarse(left)
    k3 = 0.125 * coarse(k2)
    places3 = Places(k3.shape)
    weights3, diagonal3 = whole_weights(k3, places3, 2)

    def total(v):
        return jnp.sum(jnp.sum(v, axis=0, keepdims=True), axis=(1, 2), keepdims=True)

    error = jnp.zeros_like(remain)
    direction = remain
    norm_now = total(remain * remain)
    for repeat in range(CSWEEPS):
        image = (diagonal3 * direction - whole_sum(direction, weights3, places3, 2)) * (1.0 / 128.0)
        alpha = norm_now / total(direction * image)
        error = error + alpha * direction
        if repeat == CSWEEPS - 1:
            break
        remain = remain - alpha * image
        norm_next = total(remain * remain)
        direction = remain + norm_next / norm_now * direction
        norm_now = norm_next

    lower = 0.75 * error + 0.25 * before_x(error)
    upper = 0.75 * error + 0.25 * after_x(error)
    fine = jnp.stack([lower, upper], 1).reshape(k2.shape)
    near = jnp.where(
        (places.row & 1) == 0,
        jnp.where(places.has_before_y(1), places.before_y(fine, 1), 0.0),
        jnp.where(places.has_after_y(1), places.after_y(fine, 1), 0.0),
    )
    fine = 0.75 * fine + 0.25 * near
    near = jnp.where(
        (places.lane & 4) == 0,
        jnp.where(places.has_before_z(1), ring(fine, 4, 2), 0.0),
        jnp.where(places.has_after_z(1), ring(fine, -4, 2), 0.0),
    )
    return error_two + (0.75 * fine + 0.25 * near)


def finish(grid, wide, smoothed, error_one, out, e1, e0):
    cells_x, cells_y, depth = smoothed.shape
    i, j = lax.axis_index("gx"), lax.axis_index("gy")
    first = 8 - 2
    count = cells_y + 8
    lane = lax.broadcasted_iota(jnp.int32, (count, depth), 1)
    row = lax.broadcasted_iota(jnp.int32, (count, depth), 0) - 2

    def widen_z(value, stride, lane):
        down = jnp.where(lane >= stride, pltpu.roll(value, stride, 1), 0.0)
        up = jnp.where(lane < depth - stride, pltpu.roll(value, depth - stride, 1), 0.0)
        return 0.75 * value + 0.25 * jnp.where((lane & stride) == 0, down, up)

    def widen_y(ref, index, first, count, stride, row):
        centre = ref[index, pl.ds(first, count), :]
        down = ref[index, pl.ds(first - stride, count), :]
        up = ref[index, pl.ds(first + stride, count), :]
        return 0.75 * centre + 0.25 * jnp.where((row & stride) == 0, down, up)

    low_row = jnp.where(j > 0, -cells_y, 0)
    high_row = jnp.where(j < grid[1] - 1, 2 * cells_y, cells_y)
    inside = (row >= low_row) & (row < high_row)
    planes_two = cells_x // 4 + 2
    mid = [widen_z(widen_y(wide, x, first, count, 2, row), 2, lane) for x in range(planes_two)]
    for x in range(cells_x // 2 + 2):
        centre = (x + 1) // 2
        near = centre + (1 if x % 2 == 0 else -1)
        value = jnp.where(inside, 0.75 * mid[centre] + 0.25 * mid[near], 0.0)
        if x == 0:
            value = jnp.where(i > 0, value, 0.0)
        if x == cells_x // 2 + 1:
            value = jnp.where(i < grid[0] - 1, value, 0.0)
        here = pl.ds(first, count)
        e1[x, here, :] = error_one[x, here, :] + value

    lane = lax.broadcasted_iota(jnp.int32, (cells_y, depth), 1)
    row = lax.broadcasted_iota(jnp.int32, (cells_y, depth), 0)
    for x in range(cells_x // 2 + 2):
        e0[x] = widen_z(widen_y(e1, x, 8, cells_y, 1, row), 1, lane)
    for x in range(cells_x):
        centre = x // 2 + 1
        near = centre + (-1 if x % 2 == 0 else 1)
        out[x] = smoothed[x] + (0.75 * e0[centre] + 0.25 * e0[near])


def correct_kernel(grid, gathered, smoothed, error_one, out, whole, strip, wide, e1, e0):
    cells_y = smoothed.shape[1]
    nx, ny = grid
    i, j = lax.axis_index("gx"), lax.axis_index("gy")
    lane = lax.broadcasted_iota(jnp.int32, (8, 128), 1) & 3
    fields = [[], []]
    for column in range(nx):
        parts = [gathered[column * ny + part] for part in range(ny)]
        for field in range(2):
            for x in range(2):
                place = 2 * field + x
                plane = None
                for part in range(ny):
                    turned = parts[part] if part == place else ring(parts[part], part - place, 1)
                    plane = turned if plane is None else jnp.where(lane == part, turned, plane)
                fields[field].append(plane)
    rhs2 = jnp.stack(fields[0], 0)
    k2 = jnp.stack(fields[1], 0)
    planes = 2 * nx
    whole[0] = jnp.zeros((8, 128), jnp.float32)
    whole[planes + 1] = jnp.zeros((8, 128), jnp.float32)
    whole[pl.ds(1, planes)] = whole_solve(k2, rhs2)

    for x in range(4):
        centre = pltpu.roll(whole[2 * i + x], lax.rem(128 - j, 128), 1)
        below = jnp.where(j > 0, ring(centre, 1, 1), 0.0)
        above = jnp.where(j < ny - 1, ring(centre, -1, 1), 0.0)
        for index, value in enumerate((below, centre, above)):
            value = jnp.where(lane == 0, value, 0.0)
            value = value + ring(value, 1, 1)
            strip[x, pl.ds(8 * index, 8), :] = value + ring(value, 2, 1)
        for place in range(4):
            wide[x, pl.ds(4 + place, 8, stride=4), :] = strip[x, pl.ds(7, 8), :]
            wide[x, pl.ds(36 + place, 2, stride=4), :] = strip[x, pl.ds(15, 2), :]
    finish(grid, wide, smoothed, error_one, out, e1, e0)


def finish_kernel(grid, wide, smoothed, error_one, out, e1, e0):
    finish(grid, wide, smoothed, error_one, out, e1, e0)


def last_scratch(cells_x, cells_y, depth):
    count = cells_x // 2 + 2
    return [
        pltpu.VMEM((count, cells_y + 16, depth), jnp.float32),
        pltpu.VMEM((count, cells_y, depth), jnp.float32),
    ]


def correct_whole(grid, tiles, smoothed, error_one):
    gathered = lax.all_to_all(tiles, ("gx", "gy"), 0, 0, tiled=False)
    cells_x, cells_y, depth = smoothed.shape
    return pl.pallas_call(
        functools.partial(correct_kernel, grid),
        out_shape=jax.ShapeDtypeStruct(smoothed.shape, jnp.float32),
        scratch_shapes=[
            pltpu.VMEM((2 * grid[0] + 2, 8, depth), jnp.float32),
            pltpu.VMEM((4, 24, depth), jnp.float32),
            pltpu.VMEM((4, cells_y + 16, depth), jnp.float32),
        ]
        + last_scratch(cells_x, cells_y, depth),
        compiler_params=pltpu.CompilerParams(vmem_limit_bytes=VMEM_LIMIT),
        name="correct",
    )(gathered, smoothed, error_one)


def with_faces(shard):
    for axis, dim in (("gx", 0), ("gy", 1)):
        length = shard.shape[dim]
        last = lax.slice_in_dim(shard, length - 1, length, axis=dim)
        initial = lax.slice_in_dim(shard, 0, 1, axis=dim)
        before = lax.ppermute(last, axis, shifts(axis, 1))
        after = lax.ppermute(initial, axis, shifts(axis, -1))
        shard = jnp.concatenate([before, shard, after], axis=dim)
    return shard


def with_zeros(field):
    return jnp.pad(field, ((1, 1), (1, 1), (0, 0)))


def pad_depth(field):
    return jnp.pad(field, ((0, 0), (0, 0), (1, 1)))


def restrict(field):
    size_x, size_y, size_z = field.shape
    return field.reshape(size_x // 2, 2, size_y // 2, 2, size_z // 2, 2).mean(axis=(1, 3, 5))


def level_weights(coef_pad):
    c = pad_depth(coef_pad)
    wx = (c[1:, 1:-1, 1:-1] + c[:-1, 1:-1, 1:-1]) * 0.5
    wy = (c[1:-1, 1:, 1:-1] + c[1:-1, :-1, 1:-1]) * 0.5
    wz = (c[1:-1, 1:-1, 1:] + c[1:-1, 1:-1, :-1]) * 0.5
    diagonal = wx[1:] + wx[:-1] + wy[:, 1:] + wy[:, :-1] + wz[:, :, 1:] + wz[:, :, :-1]
    return (wx, wy, wz), diagonal


def neighbour_sum(field_pad, weights):
    wx, wy, wz = weights
    v = pad_depth(field_pad)
    total = wx[:-1] * v[:-2, 1:-1, 1:-1] + wx[1:] * v[2:, 1:-1, 1:-1]
    total = total + wy[:, :-1] * v[1:-1, :-2, 1:-1] + wy[:, 1:] * v[1:-1, 2:, 1:-1]
    return total + wz[:, :, :-1] * v[1:-1, 1:-1, :-2] + wz[:, :, 1:] * v[1:-1, 1:-1, 2:]


def prolong_axis(padded, axis):
    length = padded.shape[axis]
    middle = lax.slice_in_dim(padded, 1, length - 1, axis=axis)
    before = lax.slice_in_dim(padded, 0, length - 2, axis=axis)
    after = lax.slice_in_dim(padded, 2, length, axis=axis)
    joined = jnp.stack([0.75 * middle + 0.25 * before, 0.75 * middle + 0.25 * after], axis=axis + 1)
    shape = list(middle.shape)
    shape[axis] = 2 * shape[axis]
    return joined.reshape(shape)


def coarse_solve(rhs, weights, diagonal):
    error = jnp.zeros_like(rhs)
    remain = rhs
    direction = rhs
    norm_now = jnp.sum(remain * remain)
    for _ in range(CSWEEPS):
        image = (diagonal * direction - neighbour_sum(with_zeros(direction), weights)) * 4.0**-3
        alpha = norm_now / jnp.sum(direction * image)
        error = error + alpha * direction
        remain = remain - alpha * image
        norm_next = jnp.sum(remain * remain)
        direction = remain + norm_next / norm_now * direction
        norm_now = norm_next
    return error


def correct_spread(grid, tiles, smoothed, error_one):
    cells_x, cells_y, depth = smoothed.shape
    shape2 = (cells_x // 4, cells_y // 4, depth // 4)
    own = tiles[0].reshape(shape2[1], shape2[2], 2, shape2[0]).transpose(2, 3, 0, 1)
    rhs2, k2 = own[0], own[1]
    weights, diagonal = level_weights(with_faces(k2))
    parity = sum(lax.broadcasted_iota(jnp.int32, shape2, d) for d in range(3)) % 2
    error_two = jnp.where(parity == 0, rhs2 * 16.0 / diagonal, 0.0)
    total = neighbour_sum(with_faces(error_two), weights)
    error_two = jnp.where(parity == 1, (rhs2 * 16.0 + total) / diagonal, error_two)
    total = neighbour_sum(with_faces(error_two), weights)
    rhs3 = restrict(rhs2 - (diagonal * error_two - total) * 4.0**-2)
    merged = jnp.stack([rhs3, restrict(k2)])
    merged = lax.all_gather(merged, "gx", axis=1, tiled=True)
    merged = lax.all_gather(merged, "gy", axis=2, tiled=True)
    weights3, diagonal3 = level_weights(with_zeros(merged[1]))
    error_three = coarse_solve(merged[0], weights3, diagonal3)
    start_x = lax.axis_index("gx") * rhs3.shape[0]
    start_y = lax.axis_index("gy") * rhs3.shape[1]
    window = lax.dynamic_slice(
        with_zeros(error_three),
        (start_x, start_y, jnp.int32(0)),
        (rhs3.shape[0] + 2, rhs3.shape[1] + 2, rhs3.shape[2]),
    )
    finer = pad_depth(window)
    for axis in range(3):
        finer = prolong_axis(finer, axis)
    wide = with_faces(error_two + finer)
    wide = jnp.repeat(jnp.repeat(wide, 4, axis=1), 4, axis=2)
    wide = jnp.pad(wide, ((0, 0), (4, 4), (0, 0)))
    return pl.pallas_call(
        functools.partial(finish_kernel, grid),
        out_shape=jax.ShapeDtypeStruct(smoothed.shape, jnp.float32),
        scratch_shapes=last_scratch(cells_x, cells_y, depth),
        compiler_params=pltpu.CompilerParams(vmem_limit_bytes=VMEM_LIMIT),
        name="finish",
    )(wide, smoothed, error_one)


def on_device(pressure, source, coefficient):
    grid = (lax.axis_size("gx"), lax.axis_size("gy"))
    _, cells_y, depth = pressure.shape
    fits = grid[1] == 4 and cells_y == 32 and depth == 128
    halo = fine_halo(pressure, source, coefficient)
    copies = grid[0] * grid[1] if fits else 1
    smoothed, error_one, tiles = smooth(copies, pressure, source, coefficient, halo)
    correct = correct_whole if fits else correct_spread
    return correct(grid, tiles, smoothed, error_one)


def solution(mesh):
    spec = P("gx", "gy", None)
    return jax.shard_map(on_device, mesh=mesh, in_specs=(spec, spec, spec), out_specs=spec, check_vma=False)
```

time: 297 us -> 59.4 us (0.20); the launches traced: 293 us -> 59.1 us
  starting transfers between devices: 159 us -> 15.4 us
  waiting for transfers between devices: 66.8 us -> 14.3 us
  local copies, waits for them, and re-layouts: 24.6 us -> 1.87 us
  other arithmetic: 19.1 us -> 0.01 us
  Pallas kernels: 0 us -> 14.5 us
  between operations: 10.5 us -> 0.12 us
    ppermute x67 -> x6, starting transfers between devices: 159 us -> 15.4 us  [the longest x1 4.82 us: fine_halo(): low2 = lax.ppermute(far_up, 'gx', shifts('gx', 2))]
    ppermute x67 -> x6, waiting for transfers between devices: 66.8 us -> 14.3 us  [the longest x1 5.22 us: fine_halo(): below = lax.ppermute(to_up, 'gy', shifts('gy', 1))]
    reshape x6 -> x0, local copies, waits for them, and re-layouts: 21.7 us -> none  [the longest x3 21.4 us: restrict(): field.reshape(size_x // 2, 2, size_y // 2, 2, size_z // 2, 2)]
    pallas_call x0 -> x3, Pallas kernels: none -> 14.5 us  [the longest x1 11.4 us: smooth(): pl.pallas_call(smooth_kernel, out_shape=(jax.ShapeDtypeStruct((cells_x, c...]
    all_gather x1 -> x0, blocking collectives: 13.4 us -> none  [agglomerate(): merged = lax.all_gather(merged, 'gy', axis=2, tiled=True)]
    reduce_sum x15 -> x0, other arithmetic: 13.3 us -> none  [the longest x8 8.64 us: restrict(): field.reshape(size_x // 2, 2, size_y // 2, 2, size_z // 2, 2)]
    all_to_all x0 -> x1, blocking collectives: none -> 12.9 us  [correct_whole(): gathered = lax.all_to_all(tiles, ('gx', 'gy'), 0, 0, tiled=False)]
  transfers between devices with their start and end apart: 67 -> 6, of which waited for: 23 -> 4; matrix products, arithmetic and copies ran while one was open for 12% -> 0% of each run, Pallas kernels for 0% -> 0%
where the time goes in v1:
time: 59.4 us; the launch traced here: 59.1 us
  starting transfers between devices  15.4 us (26%)
  Pallas kernels  14.5 us (24%)
  waiting for transfers between devices  14.3 us (24%)
  blocking collectives  12.9 us (22%)
  local copies, waits for them, and re-layouts  1.87 us (3%)
    all_to_all x1, blocking collectives, correct_whole(): gathered = lax.all_to_all(tiles, ('gx', 'gy'), 0, 0, tiled=False)  12.9 us
    pallas_call x1, Pallas kernels, smooth(): pl.pallas_call(smooth_kernel, out_shape=(jax.ShapeDtypeStruct((cells_x, c...  11.4 us
    ppermute x1, waiting for transfers between devices, fine_halo(): below = lax.ppermute(to_up, 'gy', shifts('gy', 1))  5.22 us
    ppermute x1, starting transfers between devices, fine_halo(): low2 = lax.ppermute(far_up, 'gx', shifts('gx', 2))  4.82 us
    ppermute x1, waiting for transfers between devices, fine_halo(): high2 = lax.ppermute(far_down, 'gx', shifts('gx', -2))  4.41 us
    ppermute x1, waiting for transfers between devices, fine_halo(): above = lax.ppermute(to_down, 'gy', shifts('gy', -1))  4.13 us
    ppermute x1, starting transfers between devices, fine_halo(): below = lax.ppermute(to_up, 'gy', shifts('gy', 1))  3.5 us
    ppermute x1, starting transfers between devices, fine_halo(): low = lax.ppermute(block, 'gx', shifts('gx', 1))  3.05 us
  transfers between devices with their start and end apart: 6, of which 4 were waited for; matrix products, arithmetic and copies ran while one was open for 0% of the time, Pallas kernels for 0%

profile of v1, /device:TPU:0, one launch (start us, length us, event | category | flops | bytes accessed | tf_op | source)
XLA Modules:
  0.0 59.1 jit_solution(8549165646329280136)
XLA Ops:
  0.0 0.0 copy-start.2
  0.0 0.9 %constant_dynamic-update-slice_fusion.2 = f32[24,32,128]{2,1,0:T(8,128)S(1)} fusion(f32[8,32,128]{2,1,0:T(8,128)} %p.3), kind=kLoop, calls=%fused_computation.4 | loop fusion | bytes 262144
  1.0 0.0 copy-done.2
  1.0 0.0 copy-start.1
  1.0 0.9 %copy-done.1 = f32[8,32,128]{2,1,0:T(8,128)S(1)} copy-done((f32[8,32,128]{2,1,0:T(8,128)S(1)}, f32[8,32,128]{2,1,0:T(8,128)}, u32[]{:S(2)}) %copy-start.1) | copy-done | bytes 131096
  1.9 0.0 copy-start
  1.9 1.4 %collective-permute-start.1 = (f32[24,32,128]{2,1,0:T(8,128)S(1)}, f32[24,32,128]{2,1,0:T(8,128)S(1)}, u32[]{:S(2)}, u32[]{:S(2)}) collective-permute-start(f32[24,32,128]{2,1,0:T(8,128)S(1)} %constant_dynamic-update-slice_fusion), channel_id=1, source_target_pairs={{4,0},{8,4},{12,8},{16,12},{20,16},{24,20},{28,24},{5,1},{9,5},{13... | collective-permute-start | bytes 1179656 | tf_op jit(solution)/shard_map/ppermute | solution.py:68
  3.3 3.1 %collective-permute-start = (f32[24,32,128]{2,1,0:T(8,128)S(1)}, f32[24,32,128]{2,1,0:T(8,128)S(1)}, u32[]{:S(2)}, u32[]{:S(2)}) collective-permute-start(f32[24,32,128]{2,1,0:T(8,128)S(1)} %constant_dynamic-update-slice_fusion), channel_id=1, source_target_pairs={{0,4},{4,8},{8,12},{12,16},{16,20},{20,24},{24,28},{1,5},{5,9},{9,... | collective-permute-start | bytes 1179656 | tf_op jit(solution)/shard_map/ppermute | solution.py:67
  6.4 0.0 copy-done
  6.4 4.8 %collective-permute-start.2 = (f32[2,32,128]{2,1,0:T(8,128)S(1)}, f32[2,32,128]{2,1,0:T(8,128)S(1)}, u32[]{:S(2)}, u32[]{:S(2)}) collective-permute-start(f32[2,32,128]{2,1,0:T(8,128)S(1)} %pad_maximum_fusion), channel_id=1, source_target_pairs={{0,8},{4,12},{8,16},{12,20},{16,24},{20,28},{1,9},{5,13},{9,17},{1... | collective-permute-start | bytes 98312 | tf_op jit(solution)/shard_map/ppermute | solution.py:69
  11.3 1.3 %collective-permute-start.3 = (f32[2,32,128]{2,1,0:T(8,128)S(1)}, f32[2,32,128]{2,1,0:T(8,128)S(1)}, u32[]{:S(2)}, u32[]{:S(2)}) collective-permute-start(f32[2,32,128]{2,1,0:T(8,128)S(1)} %pad_maximum_fusion.1), channel_id=1, source_target_pairs={{8,0},{12,4},{16,8},{20,12},{24,16},{28,20},{9,1},{13,5},{17,9},{2... | collective-permute-start | bytes 98312 | tf_op jit(solution)/shard_map/ppermute | solution.py:70
  12.6 0.5 collective-permute-done.2.low2
  13.1 4.4 %collective-permute-done.3.high2 = f32[2,32,128]{2,1,0:T(8,128)S(1)} collective-permute-done((f32[2,32,128]{2,1,0:T(8,128)S(1)}, f32[2,32,128]{2,1,0:T(8,128)S(1)}, u32[]{:S(2)}, u32[]{:S(2)}) %collective-permute-start.3) | collective-permute-done | bytes 32800 | tf_op jit(solution)/shard_map/ppermute | solution.py:70
  17.5 0.0 collective-permute-done.1.high
  17.5 0.0 collective-permute-done.low
  17.5 0.1 pack_halo.1
  17.6 3.5 %collective-permute-start.4 = (f32[536,128]{1,0:T(8,128)S(1)}, f32[536,128]{1,0:T(8,128)S(1)}, u32[]{:S(2)}, u32[]{:S(2)}) collective-permute-start(f32[536,128]{1,0:T(8,128)S(1)} %get-tuple-element.10), channel_id=1, source_target_pairs={{0,1},{1,2},{2,3},{4,5},{5,6},{6,7},{8,9},{9,10},{10,11},{12,13},{... | collective-permute-start | bytes 823304 | tf_op jit(solution)/shard_map/ppermute | solution.py:79
  21.1 1.3 %collective-permute-start.5 = (f32[536,128]{1,0:T(8,128)S(1)}, f32[536,128]{1,0:T(8,128)S(1)}, u32[]{:S(2)}, u32[]{:S(2)}) collective-permute-start(f32[536,128]{1,0:T(8,128)S(1)} %get-tuple-element.11), channel_id=1, source_target_pairs={{1,0},{2,1},{3,2},{5,4},{6,5},{7,6},{9,8},{10,9},{11,10},{13,12},{... | collective-permute-start | bytes 823304 | tf_op jit(solution)/shard_map/ppermute | solution.py:80
  22.4 5.2 %collective-permute-done.4.below = f32[536,128]{1,0:T(8,128)S(1)} collective-permute-done((f32[536,128]{1,0:T(8,128)S(1)}, f32[536,128]{1,0:T(8,128)S(1)}, u32[]{:S(2)}, u32[]{:S(2)}) %collective-permute-start.4) | collective-permute-done | bytes 274464 | tf_op jit(solution)/shard_map/ppermute | solution.py:79
  27.6 4.1 %collective-permute-done.5.above = f32[536,128]{1,0:T(8,128)S(1)} collective-permute-done((f32[536,128]{1,0:T(8,128)S(1)}, f32[536,128]{1,0:T(8,128)S(1)}, u32[]{:S(2)}, u32[]{:S(2)}) %collective-permute-start.5) | collective-permute-done | bytes 274464 | tf_op jit(solution)/shard_map/ppermute | solution.py:80
  31.7 11.4 %smooth.1 = (f32[8,32,128]{2,1,0:T(8,128)S(1)}, f32[6,48,128]{2,1,0:T(8,128)S(1)}, f32[32,8,128]{2,1,0:T(8,128)S(1)}) custom-call(f32[8,32,128]{2,1,0:T(8,128)S(1)} %copy-done, f32[8,32,128]{2,1,0:T(8,128)S(1)} %copy-done.2, f32[8,32,128]{2,1,0:T(8,128)S(1)} %copy-done.1, f32[24,32,128]{2,1,0:T(8,128)S(1)} %collective-permute-done.low, ...), custom_call_target="tpu_custom_call" | custom-call | tf_op jit(solution)/shard_map/smooth/pallas_call | solution.py:290
  43.1 12.9 %all_to_all.5.gathered = f32[32,8,128]{2,1,0:T(8,128)S(1)} all-to-all(f32[32,8,128]{2,1,0:T(8,128)S(1)} %get-tuple-element.12), channel_id=1, replica_groups=mesh['gx'=8,'gy'=4] {'gx','gy'}, dimensions={0} | all-to-all | bytes 262144 | tf_op jit(solution)/shard_map/all_to_all | solution.py:540
  56.1 3.0 %correct.1 = f32[8,32,128]{2,1,0:T(8,128)} custom-call(f32[32,8,128]{2,1,0:T(8,128)S(1)} %all_to_all.5.gathered, f32[8,32,128]{2,1,0:T(8,128)S(1)} %get-tuple-element.13.smoothed, f32[6,48,128]{2,1,0:T(8,128)S(1)} %get-tuple-element.14.error_one), custom_call_target="tpu_custom_call" | custom-call | tf_op jit(solution)/shard_map/correct/pallas_call | solution.py:542
  (5 shorter events, 0.0 us)
Async XLA Ops:
  0.0 1.0 %copy-start.2 = (f32[8,32,128]{2,1,0:T(8,128)S(1)}, f32[8,32,128]{2,1,0:T(8,128)}, u32[]{:S(2)}) copy-start(f32[8,32,128]{2,1,0:T(8,128)} %f.3) | copy-start | bytes 393220
  1.0 0.9 %copy-start.1 = (f32[8,32,128]{2,1,0:T(8,128)S(1)}, f32[8,32,128]{2,1,0:T(8,128)}, u32[]{:S(2)}) copy-start(f32[8,32,128]{2,1,0:T(8,128)} %k.3) | copy-start | bytes 393220
  1.9 4.5 %copy-start = (f32[8,32,128]{2,1,0:T(8,128)S(1)}, f32[8,32,128]{2,1,0:T(8,128)}, u32[]{:S(2)}) copy-start(f32[8,32,128]{2,1,0:T(8,128)} %p.3) | copy-start | bytes 393220
  1.9 15.6 %collective-permute-start.1 = (f32[24,32,128]{2,1,0:T(8,128)S(1)}, f32[24,32,128]{2,1,0:T(8,128)S(1)}, u32[]{:S(2)}, u32[]{:S(2)}) collective-permute-start(f32[24,32,128]{2,1,0:T(8,128)S(1)} %constant_dynamic-update-slice_fusion), channel_id=1, source_target_pairs={{4,0},{8,4},{12,8},{16,12},{20,16},{24,20},{28,24},{5,1},{9,5},{13... | collective-permute-start | bytes 1179656 | tf_op jit(solution)/shard_map/ppermute | solution.py:68
  3.3 14.2 %collective-permute-start = (f32[24,32,128]{2,1,0:T(8,128)S(1)}, f32[24,32,128]{2,1,0:T(8,128)S(1)}, u32[]{:S(2)}, u32[]{:S(2)}) collective-permute-start(f32[24,32,128]{2,1,0:T(8,128)S(1)} %constant_dynamic-update-slice_fusion), channel_id=1, source_target_pairs={{0,4},{4,8},{8,12},{12,16},{16,20},{20,24},{24,28},{1,5},{5,9},{9,... | collective-permute-start | bytes 1179656 | tf_op jit(solution)/shard_map/ppermute | solution.py:67
  6.4 6.7 %collective-permute-start.2 = (f32[2,32,128]{2,1,0:T(8,128)S(1)}, f32[2,32,128]{2,1,0:T(8,128)S(1)}, u32[]{:S(2)}, u32[]{:S(2)}) collective-permute-start(f32[2,32,128]{2,1,0:T(8,128)S(1)} %pad_maximum_fusion), channel_id=1, source_target_pairs={{0,8},{4,12},{8,16},{12,20},{16,24},{20,28},{1,9},{5,13},{9,17},{1... | collective-permute-start | bytes 98312 | tf_op jit(solution)/shard_map/ppermute | solution.py:69
  11.3 6.2 %collective-permute-start.3 = (f32[2,32,128]{2,1,0:T(8,128)S(1)}, f32[2,32,128]{2,1,0:T(8,128)S(1)}, u32[]{:S(2)}, u32[]{:S(2)}) collective-permute-start(f32[2,32,128]{2,1,0:T(8,128)S(1)} %pad_maximum_fusion.1), channel_id=1, source_target_pairs={{8,0},{12,4},{16,8},{20,12},{24,16},{28,20},{9,1},{13,5},{17,9},{2... | collective-permute-start | bytes 98312 | tf_op jit(solution)/shard_map/ppermute | solution.py:70
  17.6 10.0 %collective-permute-start.4 = (f32[536,128]{1,0:T(8,128)S(1)}, f32[536,128]{1,0:T(8,128)S(1)}, u32[]{:S(2)}, u32[]{:S(2)}) collective-permute-start(f32[536,128]{1,0:T(8,128)S(1)} %get-tuple-element.10), channel_id=1, source_target_pairs={{0,1},{1,2},{2,3},{4,5},{5,6},{6,7},{8,9},{9,10},{10,11},{12,13},{... | collective-permute-start | bytes 823304 | tf_op jit(solution)/shard_map/ppermute | solution.py:79
  21.1 10.7 %collective-permute-start.5 = (f32[536,128]{1,0:T(8,128)S(1)}, f32[536,128]{1,0:T(8,128)S(1)}, u32[]{:S(2)}, u32[]{:S(2)}) collective-permute-start(f32[536,128]{1,0:T(8,128)S(1)} %get-tuple-element.11), channel_id=1, source_target_pairs={{1,0},{2,1},{3,2},{5,4},{6,5},{7,6},{9,8},{10,9},{11,10},{13,12},{... | collective-permute-start | bytes 823304 | tf_op jit(solution)/shard_map/ppermute | solution.py:80

commit v2 on v1

--- a/solution.py
+++ b/solution.py
@@ -139,7 +139,7 @@
         inv[plane, body, :] = jnp.where(inside, 1.0 / jnp.where(inside, total, 1.0), 0.0)
         return 0
 
-    lax.fori_loop(1, planes - 1, weigh, 0)
+    lax.fori_loop(1, planes - 1, weigh, 0, unroll=True)
     wx[planes - 1, body, :] = vk[planes - 1, body, :] + vk[planes - 2, body, :]
 
     def stencil(v, plane, first, count):
@@ -158,7 +158,7 @@
             target[plane, body, :] = inv[plane, body, :] * (vf[plane, body, :] + total)
             return 0
 
-        lax.fori_loop(REACH - reach, REACH + cells_x + reach, one, 0)
+        lax.fori_loop(REACH - reach, REACH + cells_x + reach, one, 0, unroll=True)
 
     relax(vp, va, REACH - 1)
     relax(va, vb, REACH - 2)
@@ -199,7 +199,7 @@
         t0[plane_one, pl.ds(first, count), :] = pair_lane(total, 1, lane)
         return 0
 
-    lax.fori_loop(0, planes_one + 4, residual, 0)
+    lax.fori_loop(0, planes_one + 4, residual, 0, unroll=True)
     for x in range(planes_one + 4):
         f1[x, pl.ds(first, count), :] = 0.5 * pair_row(t0, x, first, count, 1, row)
 

time: 59.4 us -> 51.2 us (0.86)
  Pallas kernels: 14.5 us -> 6.26 us
    pallas_call x1, Pallas kernels: 11.4 us -> 3.19 us  [smooth(): pl.pallas_call(smooth_kernel, out_shape=(jax.ShapeDtypeStruct((cells_x, c...]
where the time goes in v2:
time: 51.2 us; the launch traced here: 50.9 us
  starting transfers between devices  15.4 us (30%)
  waiting for transfers between devices  14.3 us (28%)
  blocking collectives  12.9 us (25%)
  Pallas kernels  6.26 us (12%)
  local copies, waits for them, and re-layouts  1.87 us (4%)
    all_to_all x1, blocking collectives, correct_whole(): gathered = lax.all_to_all(tiles, ('gx', 'gy'), 0, 0, tiled=False)  12.9 us
    ppermute x1, waiting for transfers between devices, fine_halo(): below = lax.ppermute(to_up, 'gy', shifts('gy', 1))  5.22 us
    ppermute x1, starting transfers between devices, fine_halo(): low2 = lax.ppermute(far_up, 'gx', shifts('gx', 2))  4.82 us
    ppermute x1, waiting for transfers between devices, fine_halo(): high2 = lax.ppermute(far_down, 'gx', shifts('gx', -2))  4.41 us
    ppermute x1, waiting for transfers between devices, fine_halo(): above = lax.ppermute(to_down, 'gy', shifts('gy', -1))  4.13 us
    ppermute x1, starting transfers between devices, fine_halo(): below = lax.ppermute(to_up, 'gy', shifts('gy', 1))  3.5 us
    pallas_call x1, Pallas kernels, smooth(): pl.pallas_call(smooth_kernel, out_shape=(jax.ShapeDtypeStruct((cells_x, c...  3.19 us
    ppermute x1, starting transfers between devices, fine_halo(): low = lax.ppermute(block, 'gx', shifts('gx', 1))  3.05 us
  transfers between devices with their start and end apart: 6, of which 4 were waited for; matrix products, arithmetic and copies ran while one was open for 0% of the time, Pallas kernels for 0%

profile of v2, /device:TPU:0, one launch (start us, length us, event | category | flops | bytes accessed | tf_op | source)
XLA Modules:
  0.0 50.9 jit_solution(10550456616483142647)
XLA Ops:
  0.0 0.0 copy-start.2
  0.0 0.9 %constant_dynamic-update-slice_fusion.2 = f32[24,32,128]{2,1,0:T(8,128)S(1)} fusion(f32[8,32,128]{2,1,0:T(8,128)} %p.3), kind=kLoop, calls=%fused_computation.4 | loop fusion | bytes 262144
  1.0 0.0 copy-done.2
  1.0 0.0 copy-start.1
  1.0 0.9 %copy-done.1 = f32[8,32,128]{2,1,0:T(8,128)S(1)} copy-done((f32[8,32,128]{2,1,0:T(8,128)S(1)}, f32[8,32,128]{2,1,0:T(8,128)}, u32[]{:S(2)}) %copy-start.1) | copy-done | bytes 131096
  1.9 0.0 copy-start
  1.9 1.4 %collective-permute-start.1 = (f32[24,32,128]{2,1,0:T(8,128)S(1)}, f32[24,32,128]{2,1,0:T(8,128)S(1)}, u32[]{:S(2)}, u32[]{:S(2)}) collective-permute-start(f32[24,32,128]{2,1,0:T(8,128)S(1)} %constant_dynamic-update-slice_fusion), channel_id=1, source_target_pairs={{4,0},{8,4},{12,8},{16,12},{20,16},{24,20},{28,24},{5,1},{9,5},{13... | collective-permute-start | bytes 1179656 | tf_op jit(solution)/shard_map/ppermute | solution.py:68
  3.3 3.1 %collective-permute-start = (f32[24,32,128]{2,1,0:T(8,128)S(1)}, f32[24,32,128]{2,1,0:T(8,128)S(1)}, u32[]{:S(2)}, u32[]{:S(2)}) collective-permute-start(f32[24,32,128]{2,1,0:T(8,128)S(1)} %constant_dynamic-update-slice_fusion), channel_id=1, source_target_pairs={{0,4},{4,8},{8,12},{12,16},{16,20},{20,24},{24,28},{1,5},{5,9},{9,... | collective-permute-start | bytes 1179656 | tf_op jit(solution)/shard_map/ppermute | solution.py:67
  6.4 0.0 copy-done
  6.4 4.8 %collective-permute-start.2 = (f32[2,32,128]{2,1,0:T(8,128)S(1)}, f32[2,32,128]{2,1,0:T(8,128)S(1)}, u32[]{:S(2)}, u32[]{:S(2)}) collective-permute-start(f32[2,32,128]{2,1,0:T(8,128)S(1)} %pad_maximum_fusion), channel_id=1, source_target_pairs={{0,8},{4,12},{8,16},{12,20},{16,24},{20,28},{1,9},{5,13},{9,17},{1... | collective-permute-start | bytes 98312 | tf_op jit(solution)/shard_map/ppermute | solution.py:69
  11.3 1.3 %collective-permute-start.3 = (f32[2,32,128]{2,1,0:T(8,128)S(1)}, f32[2,32,128]{2,1,0:T(8,128)S(1)}, u32[]{:S(2)}, u32[]{:S(2)}) collective-permute-start(f32[2,32,128]{2,1,0:T(8,128)S(1)} %pad_maximum_fusion.1), channel_id=1, source_target_pairs={{8,0},{12,4},{16,8},{20,12},{24,16},{28,20},{9,1},{13,5},{17,9},{2... | collective-permute-start | bytes 98312 | tf_op jit(solution)/shard_map/ppermute | solution.py:70
  12.6 0.5 %collective-permute-done.2.low2 = f32[2,32,128]{2,1,0:T(8,128)S(1)} collective-permute-done((f32[2,32,128]{2,1,0:T(8,128)S(1)}, f32[2,32,128]{2,1,0:T(8,128)S(1)}, u32[]{:S(2)}, u32[]{:S(2)}) %collective-permute-start.2) | collective-permute-done | bytes 32800 | tf_op jit(solution)/shard_map/ppermute | solution.py:69
  13.1 4.4 %collective-permute-done.3.high2 = f32[2,32,128]{2,1,0:T(8,128)S(1)} collective-permute-done((f32[2,32,128]{2,1,0:T(8,128)S(1)}, f32[2,32,128]{2,1,0:T(8,128)S(1)}, u32[]{:S(2)}, u32[]{:S(2)}) %collective-permute-start.3) | collective-permute-done | bytes 32800 | tf_op jit(solution)/shard_map/ppermute | solution.py:70
  17.5 0.0 collective-permute-done.1.high
  17.5 0.0 collective-permute-done.low
  17.5 0.1 pack_halo.1
  17.6 3.5 %collective-permute-start.4 = (f32[536,128]{1,0:T(8,128)S(1)}, f32[536,128]{1,0:T(8,128)S(1)}, u32[]{:S(2)}, u32[]{:S(2)}) collective-permute-start(f32[536,128]{1,0:T(8,128)S(1)} %get-tuple-element.10), channel_id=1, source_target_pairs={{0,1},{1,2},{2,3},{4,5},{5,6},{6,7},{8,9},{9,10},{10,11},{12,13},{... | collective-permute-start | bytes 823304 | tf_op jit(solution)/shard_map/ppermute | solution.py:79
  21.1 1.3 %collective-permute-start.5 = (f32[536,128]{1,0:T(8,128)S(1)}, f32[536,128]{1,0:T(8,128)S(1)}, u32[]{:S(2)}, u32[]{:S(2)}) collective-permute-start(f32[536,128]{1,0:T(8,128)S(1)} %get-tuple-element.11), channel_id=1, source_target_pairs={{1,0},{2,1},{3,2},{5,4},{6,5},{7,6},{9,8},{10,9},{11,10},{13,12},{... | collective-permute-start | bytes 823304 | tf_op jit(solution)/shard_map/ppermute | solution.py:80
  22.4 5.2 %collective-permute-done.4.below = f32[536,128]{1,0:T(8,128)S(1)} collective-permute-done((f32[536,128]{1,0:T(8,128)S(1)}, f32[536,128]{1,0:T(8,128)S(1)}, u32[]{:S(2)}, u32[]{:S(2)}) %collective-permute-start.4) | collective-permute-done | bytes 274464 | tf_op jit(solution)/shard_map/ppermute | solution.py:79
  27.6 4.1 %collective-permute-done.5.above = f32[536,128]{1,0:T(8,128)S(1)} collective-permute-done((f32[536,128]{1,0:T(8,128)S(1)}, f32[536,128]{1,0:T(8,128)S(1)}, u32[]{:S(2)}, u32[]{:S(2)}) %collective-permute-start.5) | collective-permute-done | bytes 274464 | tf_op jit(solution)/shard_map/ppermute | solution.py:80
  31.7 3.2 %smooth.1 = (f32[8,32,128]{2,1,0:T(8,128)S(1)}, f32[6,48,128]{2,1,0:T(8,128)S(1)}, f32[32,8,128]{2,1,0:T(8,128)S(1)}) custom-call(f32[8,32,128]{2,1,0:T(8,128)S(1)} %copy-done, f32[8,32,128]{2,1,0:T(8,128)S(1)} %copy-done.2, f32[8,32,128]{2,1,0:T(8,128)S(1)} %copy-done.1, f32[24,32,128]{2,1,0:T(8,128)S(1)} %collective-permute-done.low, ...), custom_call_target="tpu_custom_call" | custom-call | tf_op jit(solution)/shard_map/smooth/pallas_call | solution.py:290
  34.9 12.9 %all_to_all.5.gathered = f32[32,8,128]{2,1,0:T(8,128)S(1)} all-to-all(f32[32,8,128]{2,1,0:T(8,128)S(1)} %get-tuple-element.12), channel_id=1, replica_groups=mesh['gx'=8,'gy'=4] {'gx','gy'}, dimensions={0} | all-to-all | bytes 262144 | tf_op jit(solution)/shard_map/all_to_all | solution.py:540
  47.9 3.0 %correct.1 = f32[8,32,128]{2,1,0:T(8,128)} custom-call(f32[32,8,128]{2,1,0:T(8,128)S(1)} %all_to_all.5.gathered, f32[8,32,128]{2,1,0:T(8,128)S(1)} %get-tuple-element.13.smoothed, f32[6,48,128]{2,1,0:T(8,128)S(1)} %get-tuple-element.14.error_one), custom_call_target="tpu_custom_call" | custom-call | tf_op jit(solution)/shard_map/correct/pallas_call | solution.py:542
  (5 shorter events, 0.0 us)
Async XLA Ops:
  0.0 1.0 %copy-start.2 = (f32[8,32,128]{2,1,0:T(8,128)S(1)}, f32[8,32,128]{2,1,0:T(8,128)}, u32[]{:S(2)}) copy-start(f32[8,32,128]{2,1,0:T(8,128)} %f.3) | copy-start | bytes 393220
  1.0 0.9 %copy-start.1 = (f32[8,32,128]{2,1,0:T(8,128)S(1)}, f32[8,32,128]{2,1,0:T(8,128)}, u32[]{:S(2)}) copy-start(f32[8,32,128]{2,1,0:T(8,128)} %k.3) | copy-start | bytes 393220
  1.9 4.5 %copy-start = (f32[8,32,128]{2,1,0:T(8,128)S(1)}, f32[8,32,128]{2,1,0:T(8,128)}, u32[]{:S(2)}) copy-start(f32[8,32,128]{2,1,0:T(8,128)} %p.3) | copy-start | bytes 393220
  1.9 15.6 %collective-permute-start.1 = (f32[24,32,128]{2,1,0:T(8,128)S(1)}, f32[24,32,128]{2,1,0:T(8,128)S(1)}, u32[]{:S(2)}, u32[]{:S(2)}) collective-permute-start(f32[24,32,128]{2,1,0:T(8,128)S(1)} %constant_dynamic-update-slice_fusion), channel_id=1, source_target_pairs={{4,0},{8,4},{12,8},{16,12},{20,16},{24,20},{28,24},{5,1},{9,5},{13... | collective-permute-start | bytes 1179656 | tf_op jit(solution)/shard_map/ppermute | solution.py:68
  3.3 14.2 %collective-permute-start = (f32[24,32,128]{2,1,0:T(8,128)S(1)}, f32[24,32,128]{2,1,0:T(8,128)S(1)}, u32[]{:S(2)}, u32[]{:S(2)}) collective-permute-start(f32[24,32,128]{2,1,0:T(8,128)S(1)} %constant_dynamic-update-slice_fusion), channel_id=1, source_target_pairs={{0,4},{4,8},{8,12},{12,16},{16,20},{20,24},{24,28},{1,5},{5,9},{9,... | collective-permute-start | bytes 1179656 | tf_op jit(solution)/shard_map/ppermute | solution.py:67
  6.4 6.7 %collective-permute-start.2 = (f32[2,32,128]{2,1,0:T(8,128)S(1)}, f32[2,32,128]{2,1,0:T(8,128)S(1)}, u32[]{:S(2)}, u32[]{:S(2)}) collective-permute-start(f32[2,32,128]{2,1,0:T(8,128)S(1)} %pad_maximum_fusion), channel_id=1, source_target_pairs={{0,8},{4,12},{8,16},{12,20},{16,24},{20,28},{1,9},{5,13},{9,17},{1... | collective-permute-start | bytes 98312 | tf_op jit(solution)/shard_map/ppermute | solution.py:69
  11.3 6.2 %collective-permute-start.3 = (f32[2,32,128]{2,1,0:T(8,128)S(1)}, f32[2,32,128]{2,1,0:T(8,128)S(1)}, u32[]{:S(2)}, u32[]{:S(2)}) collective-permute-start(f32[2,32,128]{2,1,0:T(8,128)S(1)} %pad_maximum_fusion.1), channel_id=1, source_target_pairs={{8,0},{12,4},{16,8},{20,12},{24,16},{28,20},{9,1},{13,5},{17,9},{2... | collective-permute-start | bytes 98312 | tf_op jit(solution)/shard_map/ppermute | solution.py:70
  17.6 10.0 %collective-permute-start.4 = (f32[536,128]{1,0:T(8,128)S(1)}, f32[536,128]{1,0:T(8,128)S(1)}, u32[]{:S(2)}, u32[]{:S(2)}) collective-permute-start(f32[536,128]{1,0:T(8,128)S(1)} %get-tuple-element.10), channel_id=1, source_target_pairs={{0,1},{1,2},{2,3},{4,5},{5,6},{6,7},{8,9},{9,10},{10,11},{12,13},{... | collective-permute-start | bytes 823304 | tf_op jit(solution)/shard_map/ppermute | solution.py:79
  21.1 10.7 %collective-permute-start.5 = (f32[536,128]{1,0:T(8,128)S(1)}, f32[536,128]{1,0:T(8,128)S(1)}, u32[]{:S(2)}, u32[]{:S(2)}) collective-permute-start(f32[536,128]{1,0:T(8,128)S(1)} %get-tuple-element.11), channel_id=1, source_target_pairs={{1,0},{2,1},{3,2},{5,4},{6,5},{7,6},{9,8},{10,9},{11,10},{13,12},{... | collective-permute-start | bytes 823304 | tf_op jit(solution)/shard_map/ppermute | solution.py:80

commit v3 on v2

--- a/solution.py
+++ b/solution.py
@@ -16,18 +16,41 @@
     return REACH if distance <= 2 else REACH + 2 - distance
 
 
+def side_entries():
+    pairs = [(0, d, (d, d + 1)) for d in range(1, REACH - 1, 2)] + [(0, REACH, (REACH,))]
+    return pairs + [(1, d, (d,)) for d in range(1, REACH)] + [(2, d, (d,)) for d in range(1, REACH + 1)]
+
+
+def x_plan(cells_y):
+    first, second = {}, {}
+    lengths = [0, 0]
+
+    def put(message, plan, key, row, rows):
+        plan.setdefault(key, []).append((row, rows, lengths[message]))
+        lengths[message] += rows
+
+    for array, distance, _ in side_entries():
+        key = (array, distance)
+        ends = y_rows(distance)
+        if array != 1 and distance in (1, REACH):
+            put(0, first, key, 0, cells_y)
+        else:
+            put(0, first, key, 0, ends)
+            put(0, first, key, cells_y - ends, ends)
+            put(1, second, key, ends, cells_y - 2 * ends)
+    return first, second, [-(-length // 8) * 8 for length in lengths]
+
+
 def y_plan(cells_x):
     pieces = []
     start = 0
-    for array in range(3):
-        for plane in range(cells_x + 2 * REACH):
-            x = plane - REACH
-            distance = max(0, -x, x - cells_x + 1)
-            if array == 1 and distance == REACH:
-                continue
-            rows = y_rows(distance)
-            pieces.append((array, plane, start, rows))
-            start += rows
+    inside = [(0, m) for m in range(cells_x)] + [(a, x) for a in (1, 2) for x in range(2 * cells_x)]
+    chosen = [("inside", array, index, REACH) for array, index in inside]
+    for side in ("low", "high"):
+        chosen += [(side, array, distance, y_rows(distance)) for array, distance, _ in side_entries()]
+    for side, array, index, rows in chosen:
+        pieces.append((side, array, index, rows, start))
+        start += rows
     return pieces, -(-start // 8) * 8
 
 
@@ -36,81 +59,180 @@
     return [(i, i + step) for i in range(count) if 0 <= i + step < count]
 
 
-def plane_source(array, plane, cells_x, own, low, high, low2, high2):
-    x = plane - REACH
-    far = 0 if array == 0 else 1
-    if x < -cells_x:
-        return low2, far
-    if x < 0:
-        return low, array * cells_x + cells_x + x
-    if x < cells_x:
-        return own[array], x
-    if x < 2 * cells_x:
-        return high, array * cells_x + x - cells_x
-    return high2, far
-
-
-def pack_kernel(p, f, k, low, high, low2, high2, to_up, to_down):
-    cells_x, cells_y, _ = p.shape
-    pieces, _ = y_plan(cells_x)
-    for array, plane, start, rows in pieces:
-        ref, index = plane_source(array, plane, cells_x, (p, f, k), low, high, low2, high2)
-        to_up[pl.ds(start, rows), :] = ref[index, pl.ds(cells_y - rows, rows), :]
-        to_down[pl.ds(start, rows), :] = ref[index, pl.ds(0, rows), :]
-
-
-def fine_halo(pressure, source, coefficient):
-    cells_x, _, depth = pressure.shape
+def swap_pairs():
+    return [(i, i ^ 1) for i in range(lax.axis_size("gx"))]
+
+
+def x_pairs():
+    count = lax.axis_size("gx")
+    pairs = [(i, i + 1) for i in range(1, count - 1, 2)]
+    return pairs + [(j, i) for i, j in pairs]
+
+
+def y_pairs():
+    nx, ny = lax.axis_size("gx"), lax.axis_size("gy")
+    pairs = [((i + 1) * ny + j, i * ny + j + 1) for i in range(0, nx, 2) for j in range(ny - 1)]
+    return pairs + [(j, i) for i, j in pairs]
+
+
+def inside_rows(member, own, partner, array, index, first, rows):
+    cells_x = own[0].shape[0]
+    here = pl.ds(first, rows)
+
+    def plane(x):
+        if x // cells_x == member:
+            return own[array][x % cells_x, here, :]
+        value = partner[array][x % cells_x, here, :]
+        return value + value if array == 1 else value
+
+    if array != 0:
+        return plane(index)
+    depth = own[0].shape[2]
+    row = lax.broadcasted_iota(jnp.int32, (rows, depth), 0) + first
+    lane = lax.broadcasted_iota(jnp.int32, (rows, depth), 1)
+    return jnp.where(((row + lane) & 1) == 1, plane(2 * index), plane(2 * index + 1))
+
+
+def for_member(body):
+    me = lax.axis_index("gx") & 1
+    for member in range(2):
+        pl.when(me == member)(functools.partial(body, member))
+
+
+def split_kernel(block, pp, pf, pk, first, second):
+    cells_x, cells_y, _ = pp.shape
+    p, f, k = views(block, cells_x)
+    plans = x_plan(cells_y)
+
+    def body(member):
+        for plan, target in zip(plans, (first, second)):
+            for (array, distance), pieces in plan.items():
+                plane = 2 * cells_x - distance if member == 1 else distance - 1
+                index = plane // 2 if array == 0 else plane
+                for row, rows, start in pieces:
+                    value = inside_rows(member, (p, f, k), (pp, pf, pk), array, index, row, rows)
+                    target[pl.ds(start, rows), :] = value
+
+    for_member(body)
+
+
+def pack_kernel(block, pp, pf, pk, received, passed, message):
+    cells_x, cells_y, _ = pp.shape
+    p, f, k = views(block, cells_x)
+    plan = x_plan(cells_y)[0]
+
+    def body(member):
+        sides = {"low": (received, passed)[member], "high": (passed, received)[member]}
+        for side, array, index, rows, start in y_plan(cells_x)[0]:
+            row = cells_y - rows if member == 1 else 0
+            if side == "inside":
+                value = inside_rows(member, (p, f, k), (pp, pf, pk), array, index, row, rows)
+            else:
+                place = [s + row - r for r, count, s in plan[array, index] if r <= row and row + rows <= r + count][0]
+                value = sides[side][pl.ds(place, rows), :]
+            message[pl.ds(start, rows), :] = value
+
+    for_member(body)
+
+
+def stacked(pressure, source, coefficient):
     block = jnp.concatenate([pressure, source, coefficient], 0)
-    far_up = jnp.concatenate([pressure[-1:], coefficient[-1:]], 0)
-    far_down = jnp.concatenate([pressure[:1], coefficient[:1]], 0)
-    low = lax.ppermute(block, "gx", shifts("gx", 1))
-    high = lax.ppermute(block, "gx", shifts("gx", -1))
-    low2 = lax.ppermute(far_up, "gx", shifts("gx", 2))
-    high2 = lax.ppermute(far_down, "gx", shifts("gx", -2))
-    _, length = y_plan(cells_x)
-    packed = jax.ShapeDtypeStruct((length, depth), jnp.float32)
-    to_up, to_down = pl.pallas_call(
-        pack_kernel,
-        out_shape=(packed, packed),
-        compiler_params=pltpu.CompilerParams(vmem_limit_bytes=VMEM_LIMIT),
-        name="pack_halo",
-    )(pressure, source, coefficient, low, high, low2, high2)
-    below = lax.ppermute(to_up, "gy", shifts("gy", 1))
-    above = lax.ppermute(to_down, "gy", shifts("gy", -1))
-    return low, high, low2, high2, below, above
+    cells_x = pressure.shape[0]
+    plane = lax.broadcasted_iota(jnp.int32, block.shape, 0)
+    return block * jnp.where((plane >= cells_x) & (plane < 2 * cells_x), 2.0, 1.0)
+
+
+def views(block, cells_x):
+    return tuple(block.at[pl.ds(n * cells_x, cells_x)] for n in range(3))
+
+
+def fine_halo(own, block):
+    cells_x, cells_y, depth = own[0].shape
+    params = pltpu.CompilerParams(vmem_limit_bytes=VMEM_LIMIT)
+
+    def packed(length):
+        return jax.ShapeDtypeStruct((length, depth), jnp.float32)
+
+    partner = tuple(lax.ppermute(v, "gx", swap_pairs()) for v in own)
+    lengths = x_plan(cells_y)[2]
+    first, second = pl.pallas_call(
+        split_kernel, out_shape=[packed(n) for n in lengths], compiler_params=params, name="split_block"
+    )(block, *partner)
+    received = lax.ppermute(first, "gx", x_pairs())
+    passed = lax.ppermute(received, "gx", swap_pairs())
+    message = pl.pallas_call(
+        pack_kernel, out_shape=packed(y_plan(cells_x)[1]), compiler_params=params, name="pack_halo"
+    )(block, *partner, received, passed)
+    second, message = lax.optimization_barrier((second, message))
+    along_y = lax.ppermute(message, ("gx", "gy"), y_pairs())
+    rest = lax.ppermute(second, "gx", x_pairs())
+    along_y, rest = lax.optimization_barrier((along_y, rest))
+    other_y = lax.ppermute(along_y, "gx", swap_pairs())
+    return *partner, received, passed, rest, along_y, other_y
 
 
 def smooth_kernel(
-    p, f, k, low, high, low2, high2, below, above,
+    block, pp, pf, pk, received, passed, rest, along_y, other_y,
     out, error_one, tiles,
     vp, vf, vk, wx, wy, zl, zh, dg, inv, va, vb,
     t0, t1, f1, k1, inv1, g1, h1, q2,
 ):
-    cells_x, cells_y, depth = p.shape
+    cells_x, cells_y, depth = pp.shape
     planes = cells_x + 2 * REACH
     own_rows = pl.ds(ORIGIN, cells_y)
     top = ORIGIN - REACH + 1
     rows = cells_y + 2 * (REACH - 1)
     body = pl.ds(top, rows)
 
-    for array, window in ((0, vp), (1, vf), (2, vk)):
-        for plane in range(planes):
-            if array == 1 and plane in (0, planes - 1):
+    windows = (vp, vf, vk)
+    first_plan, second_plan, _ = x_plan(cells_y)
+
+    def fill(array, x, first, value):
+        if x < -REACH or x >= cells_x + REACH or (array == 1 and (x == -REACH or x == cells_x + REACH - 1)):
+            return
+        windows[array][REACH + x, pl.ds(ORIGIN + first, value.shape[0]), :] = value
+
+    for x in range(cells_x):
+        for array, ref in enumerate(views(block, cells_x)):
+            fill(array, x, 0, ref[x])
+
+    def fill_member(member):
+        offset = cells_x * member
+
+        def outside(side, distance):
+            return (-distance if side == "low" else 2 * cells_x - 1 + distance) - offset
+
+        for x in range(cells_x):
+            for array, ref in enumerate((pp, pf, pk)):
+                value = ref[x]
+                fill(array, x + cells_x * (1 - member) - offset, 0, value + value if array == 1 else value)
+        away, near = (("low", "high"), ("high", "low"))[member]
+        for array, distance, distances in side_entries():
+            key = (array, distance)
+            for plan, ref in ((first_plan, received), (second_plan, rest)):
+                for row, count, start in plan.get(key, []):
+                    value = ref[pl.ds(start, count), :]
+                    for each in distances:
+                        fill(array, outside(away, each), row, value)
+            if array != 1 and distance == 1:
+                (row, count, start), = first_plan[key]
+                fill(array, outside(near, 1), row, passed[pl.ds(start, count), :])
+        below, above = ((along_y, other_y), (other_y, along_y))[member]
+        spans = {(array, distance): distances for array, distance, distances in side_entries()}
+        for side, array, index, count, start in y_plan(cells_x)[0]:
+            if side == "inside":
+                xs = [x - offset for x in ((2 * index, 2 * index + 1) if array == 0 else (index,))]
+            else:
+                xs = [outside(side, each) for each in spans[array, index]]
+            if not any(-REACH <= x < cells_x + REACH for x in xs):
                 continue
-            ref, index = plane_source(array, plane, cells_x, (p, f, k), low, high, low2, high2)
-            value = ref[index]
-            window[plane, own_rows, :] = value + value if array == 1 else value
-    pieces, _ = y_plan(cells_x)
-    for array, plane, start, count in pieces:
-        window = (vp, vf, vk)[array]
-        before = below[pl.ds(start, count), :]
-        after = above[pl.ds(start, count), :]
-        if array == 1:
-            before = before + before
-            after = after + after
-        window[plane, pl.ds(ORIGIN - count, count), :] = before
-        window[plane, pl.ds(ORIGIN + cells_y, count), :] = after
+            before = below[pl.ds(start, count), :]
+            after = above[pl.ds(start, count), :]
+            for x in xs:
+                fill(array, x, -count, before)
+                fill(array, x, cells_y, after)
+
+    for_member(fill_member)
 
     def lanes(count):
         return lax.broadcasted_iota(jnp.int32, (count, depth), 1)
@@ -277,8 +399,8 @@
     tiles[...] = jnp.broadcast_to(tile[None], tiles.shape)
 
 
-def smooth(copies, pressure, source, coefficient, halo):
-    cells_x, cells_y, depth = pressure.shape
+def smooth(copies, block, halo):
+    cells_x, cells_y, depth = halo[0].shape
     planes = cells_x + 2 * REACH
     tall = cells_y + 2 * ORIGIN
     planes_one = cells_x // 2
@@ -307,7 +429,7 @@
         ],
         compiler_params=pltpu.CompilerParams(vmem_limit_bytes=VMEM_LIMIT),
         name="smooth",
-    )(pressure, source, coefficient, *halo)
+    )(block, *halo)
 
 
 def ring(value, shift, axis):
@@ -664,9 +786,11 @@
     grid = (lax.axis_size("gx"), lax.axis_size("gy"))
     _, cells_y, depth = pressure.shape
     fits = grid[1] == 4 and cells_y == 32 and depth == 128
-    halo = fine_halo(pressure, source, coefficient)
+    own = (pressure, source, coefficient)
+    block = stacked(*own)
+    halo = fine_halo(own, block)
     copies = grid[0] * grid[1] if fits else 1
-    smoothed, error_one, tiles = smooth(copies, pressure, source, coefficient, halo)
+    smoothed, error_one, tiles = smooth(copies, block, halo)
     correct = correct_whole if fits else correct_spread
     return correct(grid, tiles, smoothed, error_one)
 

time: 51.2 us -> 46.5 us (0.908)
  waiting for transfers between devices: 14.3 us -> 2.39 us
  starting transfers between devices: 15.4 us -> 22.7 us
  local copies, waits for them, and re-layouts: 1.87 us -> 0 us
  other arithmetic: 0.01 us -> 1.12 us
  blocking collectives: 12.9 us -> 13.7 us
    ppermute x6 -> x8, waiting for transfers between devices: 14.3 us -> 2.39 us  [the longest x1 1.25 us: fine_halo(): other_y = lax.ppermute(along_y, 'gx', swap_pairs())]
    ppermute x6 -> x8, starting transfers between devices: 15.4 us -> 22.7 us  [the longest x1 11.4 us: fine_halo(): other_y = lax.ppermute(along_y, 'gx', swap_pairs())]
    unnamed x8 -> x0, local copies, waits for them, and re-layouts: 1.86 us -> none
    mul x0 -> x1, other arithmetic: none -> 1.12 us  [stacked(): block * jnp.where((plane >= cells_x) & (plane < 2 * cells_x), 2.0, 1.0)]
    all_to_all x1, blocking collectives: 12.9 us -> 13.7 us  [correct_whole(): gathered = lax.all_to_all(tiles, ('gx', 'gy'), 0, 0, tiled=False)]
  transfers between devices with their start and end apart: 6 -> 8, of which waited for: 4 -> 3; matrix products, arithmetic and copies ran while one was open for 0% -> 2% of each run, Pallas kernels for 0% -> 0%
where the time goes in v3:
time: 46.5 us; the launch traced here: 46.4 us
  starting transfers between devices  22.7 us (49%)
  blocking collectives  13.7 us (29%)
  Pallas kernels  6.31 us (14%)
  waiting for transfers between devices  2.39 us (5%)
  other arithmetic  1.12 us (2%)
    all_to_all x1, blocking collectives, correct_whole(): gathered = lax.all_to_all(tiles, ('gx', 'gy'), 0, 0, tiled=False)  13.7 us
    ppermute x1, starting transfers between devices, fine_halo(): other_y = lax.ppermute(along_y, 'gx', swap_pairs())  11.4 us
    ppermute x1, starting transfers between devices, fine_halo(): passed = lax.ppermute(received, 'gx', swap_pairs())  8.36 us
    pallas_call x1, Pallas kernels, smooth(): pl.pallas_call(smooth_kernel, out_shape=(jax.ShapeDtypeStruct((cells_x, c...  3.22 us
    pallas_call x1, Pallas kernels, correct_whole(): pl.pallas_call(functools.partial(correct_kernel, grid), out_shape=jax.Sha...  3.01 us
    ppermute x1, waiting for transfers between devices, fine_halo(): other_y = lax.ppermute(along_y, 'gx', swap_pairs())  1.25 us
    mul x1, other arithmetic, stacked(): block * jnp.where((plane >= cells_x) & (plane < 2 * cells_x), 2.0, 1.0)  1.12 us
    ppermute x1, waiting for transfers between devices, fine_halo(): passed = lax.ppermute(received, 'gx', swap_pairs())  1.05 us
  transfers between devices with their start and end apart: 8, of which 3 were waited for; matrix products, arithmetic and copies ran while one was open for 2% of the time, Pallas kernels for 0%

profile of v3, /device:TPU:0, one launch (start us, length us, event | category | flops | bytes accessed | tf_op | source)
XLA Modules:
  0.0 46.4 jit_solution(8273825083276889008)
XLA Ops:
  0.0 0.5 collective-permute-start
  0.5 0.1 collective-permute-start.1
  0.5 0.5 collective-permute-start.2
  1.0 1.1 %maximum_multiply_fusion.block = f32[24,32,128]{2,1,0:T(8,128)S(1)} fusion(f32[8,32,128]{2,1,0:T(8,128)} %param.5, f32[8,32,128]{2,1,0:T(8,128)} %param.4, f32[8,32,128]{2,1,0:T(8,128)} %param.3, f32[24]{0:T(128)S(1)} %and_select_fusion), kind=kLoop, calls=%fused_computation | loop fusion | flops 294912 | bytes 786528 | tf_op jit(solution)/shard_map/mul | solution.py:142
  2.1 0.0 collective-permute-done.pp
  2.1 0.0 collective-permute-done.1.pf
  2.1 0.1 collective-permute-done.2.pk
  2.2 0.7 %collective-permute-start.3 = (f32[352,128]{1,0:T(8,128)S(1)}, f32[352,128]{1,0:T(8,128)S(1)}, u32[]{:S(2)}, u32[]{:S(2)}) collective-permute-start(f32[352,128]{1,0:T(8,128)S(1)} %get-tuple-element.14), channel_id=1, source_target_pairs={{4,8},{12,16},{20,24},{8,4},{16,12},{24,20},{5,9},{13,17},{21,25},... | collective-permute-start | bytes 540680 | tf_op jit(solution)/shard_map/ppermute | solution.py:161
  2.9 0.0 collective-permute-done.3.received
  2.9 8.4 %collective-permute-start.4 = (f32[352,128]{1,0:T(8,128)S(1)}, f32[352,128]{1,0:T(8,128)S(1)}, u32[]{:S(2)}, u32[]{:S(2)}) collective-permute-start(f32[352,128]{1,0:T(8,128)S(1)} %collective-permute-done.3.received), channel_id=1, source_target_pairs={{0,4},{4,0},{8,12},{12,8},{16,20},{20,16},{24,28},{28,24},{1,5},{5... | collective-permute-start | bytes 540680 | tf_op jit(solution)/shard_map/ppermute | solution.py:162
  11.3 1.0 %collective-permute-done.4.passed = f32[352,128]{1,0:T(8,128)S(1)} collective-permute-done((f32[352,128]{1,0:T(8,128)S(1)}, f32[352,128]{1,0:T(8,128)S(1)}, u32[]{:S(2)}, u32[]{:S(2)}) %collective-permute-start.4) | collective-permute-done | bytes 180256 | tf_op jit(solution)/shard_map/ppermute | solution.py:162
  12.4 0.7 %collective-permute-start.5 = (f32[632,128]{1,0:T(8,128)S(1)}, f32[632,128]{1,0:T(8,128)S(1)}, u32[]{:S(2)}, u32[]{:S(2)}) collective-permute-start(f32[632,128]{1,0:T(8,128)S(1)} %pack_halo.1), channel_id=1, source_target_pairs={{4,1},{5,2},{6,3},{12,9},{13,10},{14,11},{20,17},{21,18},{22,19},{... | collective-permute-start | bytes 970760 | tf_op jit(solution)/shard_map/ppermute | solution.py:167
  13.1 0.7 %collective-permute-start.6 = (f32[360,128]{1,0:T(8,128)S(1)}, f32[360,128]{1,0:T(8,128)S(1)}, u32[]{:S(2)}, u32[]{:S(2)}) collective-permute-start(f32[360,128]{1,0:T(8,128)S(1)} %get-tuple-element.17), channel_id=1, source_target_pairs={{4,8},{12,16},{20,24},{8,4},{16,12},{24,20},{5,9},{13,17},{21,25},... | collective-permute-start | bytes 552968 | tf_op jit(solution)/shard_map/ppermute | solution.py:168
  13.8 0.0 collective-permute-done.6.rest
  13.8 0.0 collective-permute-done.5.along_y
  13.8 11.4 %collective-permute-start.7 = (f32[632,128]{1,0:T(8,128)S(1)}, f32[632,128]{1,0:T(8,128)S(1)}, u32[]{:S(2)}, u32[]{:S(2)}) collective-permute-start(f32[632,128]{1,0:T(8,128)S(1)} %collective-permute-done.5.along_y), channel_id=1, source_target_pairs={{0,4},{4,0},{8,12},{12,8},{16,20},{20,16},{24,28},{28,24},{1,5},{5... | collective-permute-start | bytes 970760 | tf_op jit(solution)/shard_map/ppermute | solution.py:170
  25.2 1.2 %collective-permute-done.7.other_y = f32[632,128]{1,0:T(8,128)S(1)} collective-permute-done((f32[632,128]{1,0:T(8,128)S(1)}, f32[632,128]{1,0:T(8,128)S(1)}, u32[]{:S(2)}, u32[]{:S(2)}) %collective-permute-start.7) | collective-permute-done | bytes 323616 | tf_op jit(solution)/shard_map/ppermute | solution.py:170
  26.4 3.2 %smooth.1 = (f32[8,32,128]{2,1,0:T(8,128)S(1)}, f32[6,48,128]{2,1,0:T(8,128)S(1)}, f32[32,8,128]{2,1,0:T(8,128)S(1)}) custom-call(f32[24,32,128]{2,1,0:T(8,128)S(1)} %maximum_multiply_fusion.block, f32[8,32,128]{2,1,0:T(8,128)S(1)} %collective-permute-done.pp, f32[8,32,128]{2,1,0:T(8,128)S(1)} %collective-permute-done.1.pf, ...), custom_call_target="tpu_custom_call" | custom-call | tf_op jit(solution)/shard_map/smooth/pallas_call | solution.py:412
  29.7 13.7 %all_to_all.5.gathered = f32[32,8,128]{2,1,0:T(8,128)S(1)} all-to-all(f32[32,8,128]{2,1,0:T(8,128)S(1)} %get-tuple-element.20), channel_id=1, replica_groups=mesh['gx'=8,'gy'=4] {'gx','gy'}, dimensions={0} | all-to-all | bytes 262144 | tf_op jit(solution)/shard_map/all_to_all | solution.py:662
  43.3 3.0 %correct.1 = f32[8,32,128]{2,1,0:T(8,128)} custom-call(f32[32,8,128]{2,1,0:T(8,128)S(1)} %all_to_all.5.gathered, f32[8,32,128]{2,1,0:T(8,128)S(1)} %get-tuple-element.21.smoothed, f32[6,48,128]{2,1,0:T(8,128)S(1)} %get-tuple-element.22.error_one), custom_call_target="tpu_custom_call" | custom-call | tf_op jit(solution)/shard_map/correct/pallas_call | solution.py:664
  (3 shorter events, 0.1 us)
Async XLA Ops:
  0.0 2.1 %collective-permute-start = (f32[8,32,128]{2,1,0:T(8,128)}, f32[8,32,128]{2,1,0:T(8,128)S(1)}, u32[]{:S(2)}, u32[]{:S(2)}) collective-permute-start(f32[8,32,128]{2,1,0:T(8,128)} %param.3), channel_id=1, source_target_pairs={{0,4},{4,0},{8,12},{12,8},{16,20},{20,16},{24,28},{28,24},{1,5},{5... | collective-permute-start | bytes 393224 | tf_op jit(solution)/shard_map/ppermute | solution.py:156
  0.5 1.7 %collective-permute-start.1 = (f32[8,32,128]{2,1,0:T(8,128)}, f32[8,32,128]{2,1,0:T(8,128)S(1)}, u32[]{:S(2)}, u32[]{:S(2)}) collective-permute-start(f32[8,32,128]{2,1,0:T(8,128)} %param.4), channel_id=1, source_target_pairs={{0,4},{4,0},{8,12},{12,8},{16,20},{20,16},{24,28},{28,24},{1,5},{5... | collective-permute-start | bytes 393224 | tf_op jit(solution)/shard_map/ppermute | solution.py:156
  0.5 1.7 %collective-permute-start.2 = (f32[8,32,128]{2,1,0:T(8,128)}, f32[8,32,128]{2,1,0:T(8,128)S(1)}, u32[]{:S(2)}, u32[]{:S(2)}) collective-permute-start(f32[8,32,128]{2,1,0:T(8,128)} %param.5), channel_id=1, source_target_pairs={{0,4},{4,0},{8,12},{12,8},{16,20},{20,16},{24,28},{28,24},{1,5},{5... | collective-permute-start | bytes 393224 | tf_op jit(solution)/shard_map/ppermute | solution.py:156
  2.2 0.7 %collective-permute-start.3 = (f32[352,128]{1,0:T(8,128)S(1)}, f32[352,128]{1,0:T(8,128)S(1)}, u32[]{:S(2)}, u32[]{:S(2)}) collective-permute-start(f32[352,128]{1,0:T(8,128)S(1)} %get-tuple-element.14), channel_id=1, source_target_pairs={{4,8},{12,16},{20,24},{8,4},{16,12},{24,20},{5,9},{13,17},{21,25},... | collective-permute-start | bytes 540680 | tf_op jit(solution)/shard_map/ppermute | solution.py:161
  2.9 9.4 %collective-permute-start.4 = (f32[352,128]{1,0:T(8,128)S(1)}, f32[352,128]{1,0:T(8,128)S(1)}, u32[]{:S(2)}, u32[]{:S(2)}) collective-permute-start(f32[352,128]{1,0:T(8,128)S(1)} %collective-permute-done.3.received), channel_id=1, source_target_pairs={{0,4},{4,0},{8,12},{12,8},{16,20},{20,16},{24,28},{28,24},{1,5},{5... | collective-permute-start | bytes 540680 | tf_op jit(solution)/shard_map/ppermute | solution.py:162
  12.4 1.4 %collective-permute-start.5 = (f32[632,128]{1,0:T(8,128)S(1)}, f32[632,128]{1,0:T(8,128)S(1)}, u32[]{:S(2)}, u32[]{:S(2)}) collective-permute-start(f32[632,128]{1,0:T(8,128)S(1)} %pack_halo.1), channel_id=1, source_target_pairs={{4,1},{5,2},{6,3},{12,9},{13,10},{14,11},{20,17},{21,18},{22,19},{... | collective-permute-start | bytes 970760 | tf_op jit(solution)/shard_map/ppermute | solution.py:167
  13.1 0.7 %collective-permute-start.6 = (f32[360,128]{1,0:T(8,128)S(1)}, f32[360,128]{1,0:T(8,128)S(1)}, u32[]{:S(2)}, u32[]{:S(2)}) collective-permute-start(f32[360,128]{1,0:T(8,128)S(1)} %get-tuple-element.17), channel_id=1, source_target_pairs={{4,8},{12,16},{20,24},{8,4},{16,12},{24,20},{5,9},{13,17},{21,25},... | collective-permute-start | bytes 552968 | tf_op jit(solution)/shard_map/ppermute | solution.py:168
  13.8 12.6 %collective-permute-start.7 = (f32[632,128]{1,0:T(8,128)S(1)}, f32[632,128]{1,0:T(8,128)S(1)}, u32[]{:S(2)}, u32[]{:S(2)}) collective-permute-start(f32[632,128]{1,0:T(8,128)S(1)} %collective-permute-done.5.along_y), channel_id=1, source_target_pairs={{0,4},{4,0},{8,12},{12,8},{16,20},{20,16},{24,28},{28,24},{1,5},{5... | collective-permute-start | bytes 970760 | tf_op jit(solution)/shard_map/ppermute | solution.py:170

commit v4 on v3

--- a/solution.py
+++ b/solution.py
@@ -12,8 +12,9 @@
 VMEM_LIMIT = 48 * 1024 * 1024
 
 
-def y_rows(distance):
-    return REACH if distance <= 2 else REACH + 2 - distance
+def y_rows(distance, array):
+    rows = REACH if distance <= 2 else REACH + 2 - distance
+    return rows - 1 if array == 1 else rows
 
 
 def side_entries():
@@ -31,23 +32,20 @@
 
     for array, distance, _ in side_entries():
         key = (array, distance)
-        ends = y_rows(distance)
-        if array != 1 and distance in (1, REACH):
-            put(0, first, key, 0, cells_y)
-        else:
-            put(0, first, key, 0, ends)
-            put(0, first, key, cells_y - ends, ends)
-            put(1, second, key, ends, cells_y - 2 * ends)
+        ends = y_rows(distance, array)
+        put(0, first, key, 0, ends)
+        put(0, first, key, cells_y - ends, ends)
+        put(1, second, key, ends, cells_y - 2 * ends)
     return first, second, [-(-length // 8) * 8 for length in lengths]
 
 
 def y_plan(cells_x):
     pieces = []
     start = 0
-    inside = [(0, m) for m in range(cells_x)] + [(a, x) for a in (1, 2) for x in range(2 * cells_x)]
-    chosen = [("inside", array, index, REACH) for array, index in inside]
+    inside = [(0, m) for m in range(cells_x // 2)] + [(a, x) for a in (1, 2) for x in range(cells_x)]
+    chosen = [("inside", array, index, y_rows(0, array)) for array, index in inside]
     for side in ("low", "high"):
-        chosen += [(side, array, distance, y_rows(distance)) for array, distance, _ in side_entries()]
+        chosen += [(side, array, distance, y_rows(distance, array)) for array, distance, _ in side_entries()]
     for side, array, index, rows in chosen:
         pieces.append((side, array, index, rows, start))
         start += rows
@@ -69,10 +67,9 @@
     return pairs + [(j, i) for i, j in pairs]
 
 
-def y_pairs():
-    nx, ny = lax.axis_size("gx"), lax.axis_size("gy")
-    pairs = [((i + 1) * ny + j, i * ny + j + 1) for i in range(0, nx, 2) for j in range(ny - 1)]
-    return pairs + [(j, i) for i, j in pairs]
+def far_pairs():
+    count = lax.axis_size("gx")
+    return [(i, i - 2) for i in range(2, count, 2)] + [(i, i + 2) for i in range(1, count - 2, 2)]
 
 
 def inside_rows(member, own, partner, array, index, first, rows):
@@ -99,7 +96,7 @@
         pl.when(me == member)(functools.partial(body, member))
 
 
-def split_kernel(block, pp, pf, pk, first, second):
+def split_kernel(block, pp, pf, pk, first, second, far):
     cells_x, cells_y, _ = pp.shape
     p, f, k = views(block, cells_x)
     plans = x_plan(cells_y)
@@ -112,25 +109,37 @@
                 for row, rows, start in pieces:
                     value = inside_rows(member, (p, f, k), (pp, pf, pk), array, index, row, rows)
                     target[pl.ds(start, rows), :] = value
+        outermost = (cells_x - 1) * member
+        far[0] = p[outermost]
+        far[1] = k[outermost]
 
     for_member(body)
 
 
-def pack_kernel(block, pp, pf, pk, received, passed, message):
+def pack_kernel(block, pp, pf, pk, received, far, to_up, to_down):
     cells_x, cells_y, _ = pp.shape
     p, f, k = views(block, cells_x)
     plan = x_plan(cells_y)[0]
 
     def body(member):
-        sides = {"low": (received, passed)[member], "high": (passed, received)[member]}
+        away = ("low", "high")[member]
+
+        def piece(side, array, index, rows, row):
+            if side == away:
+                place = [s for r, _, s in plan[array, index] if r == row][0]
+                return received[pl.ds(place, rows), :]
+            if side != "inside" and index == REACH:
+                return far[0 if array == 0 else 1, pl.ds(row, rows), :]
+            if side == "inside":
+                index += (cells_x // 2 if array == 0 else cells_x) * member
+            else:
+                plane = cells_x - index if member == 1 else cells_x - 1 + index
+                index = plane // 2 if array == 0 else plane
+            return inside_rows(member, (p, f, k), (pp, pf, pk), array, index, row, rows)
+
         for side, array, index, rows, start in y_plan(cells_x)[0]:
-            row = cells_y - rows if member == 1 else 0
-            if side == "inside":
-                value = inside_rows(member, (p, f, k), (pp, pf, pk), array, index, row, rows)
-            else:
-                place = [s + row - r for r, count, s in plan[array, index] if r <= row and row + rows <= r + count][0]
-                value = sides[side][pl.ds(place, rows), :]
-            message[pl.ds(start, rows), :] = value
+            to_up[pl.ds(start, rows), :] = piece(side, array, index, rows, cells_y - rows)
+            to_down[pl.ds(start, rows), :] = piece(side, array, index, rows, 0)
 
     for_member(body)
 
@@ -155,24 +164,24 @@
 
     partner = tuple(lax.ppermute(v, "gx", swap_pairs()) for v in own)
     lengths = x_plan(cells_y)[2]
-    first, second = pl.pallas_call(
-        split_kernel, out_shape=[packed(n) for n in lengths], compiler_params=params, name="split_block"
+    planes = jax.ShapeDtypeStruct((2, cells_y, depth), jnp.float32)
+    first, second, outermost = pl.pallas_call(
+        split_kernel, out_shape=[packed(n) for n in lengths] + [planes], compiler_params=params, name="split_block"
     )(block, *partner)
+    far = lax.ppermute(outermost, "gx", far_pairs())
     received = lax.ppermute(first, "gx", x_pairs())
-    passed = lax.ppermute(received, "gx", swap_pairs())
-    message = pl.pallas_call(
-        pack_kernel, out_shape=packed(y_plan(cells_x)[1]), compiler_params=params, name="pack_halo"
-    )(block, *partner, received, passed)
-    second, message = lax.optimization_barrier((second, message))
-    along_y = lax.ppermute(message, ("gx", "gy"), y_pairs())
+    length = y_plan(cells_x)[1]
+    to_up, to_down = pl.pallas_call(
+        pack_kernel, out_shape=[packed(length)] * 2, compiler_params=params, name="pack_halo"
+    )(block, *partner, received, far)
+    below = lax.ppermute(to_up, "gy", shifts("gy", 1))
+    above = lax.ppermute(to_down, "gy", shifts("gy", -1))
     rest = lax.ppermute(second, "gx", x_pairs())
-    along_y, rest = lax.optimization_barrier((along_y, rest))
-    other_y = lax.ppermute(along_y, "gx", swap_pairs())
-    return *partner, received, passed, rest, along_y, other_y
+    return *partner, received, rest, far, below, above
 
 
 def smooth_kernel(
-    block, pp, pf, pk, received, passed, rest, along_y, other_y,
+    block, pp, pf, pk, received, rest, far, below, above,
     out, error_one, tiles,
     vp, vf, vk, wx, wy, zl, zh, dg, inv, va, vb,
     t0, t1, f1, k1, inv1, g1, h1, q2,
@@ -196,43 +205,37 @@
         for array, ref in enumerate(views(block, cells_x)):
             fill(array, x, 0, ref[x])
 
+    spans = {(array, distance): distances for array, distance, distances in side_entries()}
+
+    def outside(side, distance):
+        return -distance if side == "low" else cells_x - 1 + distance
+
     def fill_member(member):
-        offset = cells_x * member
-
-        def outside(side, distance):
-            return (-distance if side == "low" else 2 * cells_x - 1 + distance) - offset
-
+        away, near = (("low", "high"), ("high", "low"))[member]
         for x in range(cells_x):
             for array, ref in enumerate((pp, pf, pk)):
                 value = ref[x]
-                fill(array, x + cells_x * (1 - member) - offset, 0, value + value if array == 1 else value)
-        away, near = (("low", "high"), ("high", "low"))[member]
-        for array, distance, distances in side_entries():
-            key = (array, distance)
-            for plan, ref in ((first_plan, received), (second_plan, rest)):
-                for row, count, start in plan.get(key, []):
+                fill(array, x + cells_x * (1 - 2 * member), 0, value + value if array == 1 else value)
+        fill(0, outside(near, REACH), 0, far[0])
+        fill(2, outside(near, REACH), 0, far[1])
+        for plan, ref in ((first_plan, received), (second_plan, rest)):
+            for (array, distance), pieces in plan.items():
+                for row, count, start in pieces:
                     value = ref[pl.ds(start, count), :]
-                    for each in distances:
+                    for each in spans[array, distance]:
                         fill(array, outside(away, each), row, value)
-            if array != 1 and distance == 1:
-                (row, count, start), = first_plan[key]
-                fill(array, outside(near, 1), row, passed[pl.ds(start, count), :])
-        below, above = ((along_y, other_y), (other_y, along_y))[member]
-        spans = {(array, distance): distances for array, distance, distances in side_entries()}
-        for side, array, index, count, start in y_plan(cells_x)[0]:
-            if side == "inside":
-                xs = [x - offset for x in ((2 * index, 2 * index + 1) if array == 0 else (index,))]
-            else:
-                xs = [outside(side, each) for each in spans[array, index]]
-            if not any(-REACH <= x < cells_x + REACH for x in xs):
-                continue
-            before = below[pl.ds(start, count), :]
-            after = above[pl.ds(start, count), :]
-            for x in xs:
-                fill(array, x, -count, before)
-                fill(array, x, cells_y, after)
 
     for_member(fill_member)
+    for side, array, index, count, start in y_plan(cells_x)[0]:
+        before = below[pl.ds(start, count), :]
+        after = above[pl.ds(start, count), :]
+        if side == "inside":
+            xs = (2 * index, 2 * index + 1) if array == 0 else (index,)
+        else:
+            xs = [outside(side, each) for each in spans[array, index]]
+        for x in xs:
+            fill(array, x, -count, before)
+            fill(array, x, cells_y, after)
 
     def lanes(count):
         return lax.broadcasted_iota(jnp.int32, (count, depth), 1)

time: 46.5 us -> 43.7 us (0.940)
  starting transfers between devices: 22.7 us -> 9.07 us
  waiting for transfers between devices: 2.39 us -> 14.2 us
  blocking collectives: 13.7 us -> 12.6 us
    ppermute x3, starting transfers between devices: 20.4 us -> 6.76 us  [the longest x1 4.18 us: fine_halo(): below = lax.ppermute(to_up, 'gy', shifts('gy', 1))]
    ppermute x3, waiting for transfers between devices: 2.3 us -> 14.1 us  [the longest x1 6.22 us: fine_halo(): far = lax.ppermute(outermost, 'gx', far_pairs())]
    all_to_all x1, blocking collectives: 13.7 us -> 12.6 us  [correct_whole(): gathered = lax.all_to_all(tiles, ('gx', 'gy'), 0, 0, tiled=False)]
  transfers between devices with their start and end apart: 8 -> 8, of which waited for: 3 -> 4; matrix products, arithmetic and copies ran while one was open for 2% -> 3% of each run, Pallas kernels for 0% -> 0%
where the time goes in v4:
time: 43.7 us; the launch traced here: 43.5 us
  waiting for transfers between devices  14.2 us (32%)
  blocking collectives  12.6 us (29%)
  starting transfers between devices  9.07 us (21%)
  Pallas kernels  6.3 us (14%)
  other arithmetic  1.12 us (3%)
    all_to_all x1, blocking collectives, correct_whole(): gathered = lax.all_to_all(tiles, ('gx', 'gy'), 0, 0, tiled=False)  12.6 us
    ppermute x1, waiting for transfers between devices, fine_halo(): far = lax.ppermute(outermost, 'gx', far_pairs())  6.22 us
    ppermute x1, starting transfers between devices, fine_halo(): below = lax.ppermute(to_up, 'gy', shifts('gy', 1))  4.18 us
    ppermute x1, waiting for transfers between devices, fine_halo(): above = lax.ppermute(to_down, 'gy', shifts('gy', -1))  4.13 us
    ppermute x1, waiting for transfers between devices, fine_halo(): below = lax.ppermute(to_up, 'gy', shifts('gy', 1))  3.78 us
    pallas_call x1, Pallas kernels, smooth(): pl.pallas_call(smooth_kernel, out_shape=(jax.ShapeDtypeStruct((cells_x, c...  3.18 us
    pallas_call x1, Pallas kernels, correct_whole(): pl.pallas_call(functools.partial(correct_kernel, grid), out_shape=jax.Sha...  3.01 us
    ppermute x1, starting transfers between devices, fine_halo(): far = lax.ppermute(outermost, 'gx', far_pairs())  1.29 us
  transfers between devices with their start and end apart: 8, of which 4 were waited for; matrix products, arithmetic and copies ran while one was open for 3% of the time, Pallas kernels for 0%

profile of v4, /device:TPU:0, one launch (start us, length us, event | category | flops | bytes accessed | tf_op | source)
XLA Modules:
  0.0 43.5 jit_solution(8961428690268643559)
XLA Ops:
  0.0 0.5 %collective-permute-start = (f32[8,32,128]{2,1,0:T(8,128)}, f32[8,32,128]{2,1,0:T(8,128)S(1)}, u32[]{:S(2)}, u32[]{:S(2)}) collective-permute-start(f32[8,32,128]{2,1,0:T(8,128)} %param.3), channel_id=1, source_target_pairs={{0,4},{4,0},{8,12},{12,8},{16,20},{20,16},{24,28},{28,24},{1,5},{5... | collective-permute-start | bytes 393224 | tf_op jit(solution)/shard_map/ppermute | solution.py:165
  0.5 0.1 collective-permute-start.1
  0.5 0.5 %collective-permute-start.2 = (f32[8,32,128]{2,1,0:T(8,128)}, f32[8,32,128]{2,1,0:T(8,128)S(1)}, u32[]{:S(2)}, u32[]{:S(2)}) collective-permute-start(f32[8,32,128]{2,1,0:T(8,128)} %param.5), channel_id=1, source_target_pairs={{0,4},{4,0},{8,12},{12,8},{16,20},{20,16},{24,28},{28,24},{1,5},{5... | collective-permute-start | bytes 393224 | tf_op jit(solution)/shard_map/ppermute | solution.py:165
  1.0 1.1 %maximum_multiply_fusion.block = f32[24,32,128]{2,1,0:T(8,128)S(1)} fusion(f32[8,32,128]{2,1,0:T(8,128)} %param.5, f32[8,32,128]{2,1,0:T(8,128)} %param.4, f32[8,32,128]{2,1,0:T(8,128)} %param.3, f32[24]{0:T(128)S(1)} %and_select_fusion), kind=kLoop, calls=%fused_computation | loop fusion | flops 294912 | bytes 786528 | tf_op jit(solution)/shard_map/mul | solution.py:151
  2.1 0.0 collective-permute-done.pp
  2.1 0.0 collective-permute-done.1.pf
  2.1 0.1 collective-permute-done.2.pk
  2.3 0.7 %collective-permute-start.3 = (f32[256,128]{1,0:T(8,128)S(1)}, f32[256,128]{1,0:T(8,128)S(1)}, u32[]{:S(2)}, u32[]{:S(2)}) collective-permute-start(f32[256,128]{1,0:T(8,128)S(1)} %get-tuple-element.13), channel_id=1, source_target_pairs={{4,8},{12,16},{20,24},{8,4},{16,12},{24,20},{5,9},{13,17},{21,25},... | collective-permute-start | bytes 393224 | tf_op jit(solution)/shard_map/ppermute | solution.py:172
  2.9 1.3 %collective-permute-start.5 = (f32[2,32,128]{2,1,0:T(8,128)S(1)}, f32[2,32,128]{2,1,0:T(8,128)S(1)}, u32[]{:S(2)}, u32[]{:S(2)}) collective-permute-start(f32[2,32,128]{2,1,0:T(8,128)S(1)} %get-tuple-element.15), channel_id=1, source_target_pairs={{8,0},{16,8},{24,16},{4,12},{12,20},{20,28},{9,1},{17,9},{25,17},{... | collective-permute-start | bytes 98312 | tf_op jit(solution)/shard_map/ppermute | solution.py:171
  4.2 0.7 %collective-permute-start.4 = (f32[456,128]{1,0:T(8,128)S(1)}, f32[456,128]{1,0:T(8,128)S(1)}, u32[]{:S(2)}, u32[]{:S(2)}) collective-permute-start(f32[456,128]{1,0:T(8,128)S(1)} %get-tuple-element.14), channel_id=1, source_target_pairs={{4,8},{12,16},{20,24},{8,4},{16,12},{24,20},{5,9},{13,17},{21,25},... | collective-permute-start | bytes 700424 | tf_op jit(solution)/shard_map/ppermute | solution.py:179
  4.9 6.2 %collective-permute-done.5.far = f32[2,32,128]{2,1,0:T(8,128)S(1)} collective-permute-done((f32[2,32,128]{2,1,0:T(8,128)S(1)}, f32[2,32,128]{2,1,0:T(8,128)S(1)}, u32[]{:S(2)}, u32[]{:S(2)}) %collective-permute-start.5) | collective-permute-done | bytes 32800 | tf_op jit(solution)/shard_map/ppermute | solution.py:171
  11.1 0.0 collective-permute-done.3.received
  11.1 0.1 pack_halo.1
  11.2 4.2 %collective-permute-start.6 = (f32[424,128]{1,0:T(8,128)S(1)}, f32[424,128]{1,0:T(8,128)S(1)}, u32[]{:S(2)}, u32[]{:S(2)}) collective-permute-start(f32[424,128]{1,0:T(8,128)S(1)} %get-tuple-element.16), channel_id=1, source_target_pairs={{0,1},{1,2},{2,3},{4,5},{5,6},{6,7},{8,9},{9,10},{10,11},{12,13},{... | collective-permute-start | bytes 651272 | tf_op jit(solution)/shard_map/ppermute | solution.py:177
  15.4 1.3 %collective-permute-start.7 = (f32[424,128]{1,0:T(8,128)S(1)}, f32[424,128]{1,0:T(8,128)S(1)}, u32[]{:S(2)}, u32[]{:S(2)}) collective-permute-start(f32[424,128]{1,0:T(8,128)S(1)} %get-tuple-element.17), channel_id=1, source_target_pairs={{1,0},{2,1},{3,2},{5,4},{6,5},{7,6},{9,8},{10,9},{11,10},{13,12},{... | collective-permute-start | bytes 651272 | tf_op jit(solution)/shard_map/ppermute | solution.py:178
  16.7 0.0 collective-permute-done.4.rest
  16.7 3.8 %collective-permute-done.6.below = f32[424,128]{1,0:T(8,128)S(1)} collective-permute-done((f32[424,128]{1,0:T(8,128)S(1)}, f32[424,128]{1,0:T(8,128)S(1)}, u32[]{:S(2)}, u32[]{:S(2)}) %collective-permute-start.6) | collective-permute-done | bytes 217120 | tf_op jit(solution)/shard_map/ppermute | solution.py:177
  20.5 4.1 %collective-permute-done.7.above = f32[424,128]{1,0:T(8,128)S(1)} collective-permute-done((f32[424,128]{1,0:T(8,128)S(1)}, f32[424,128]{1,0:T(8,128)S(1)}, u32[]{:S(2)}, u32[]{:S(2)}) %collective-permute-start.7) | collective-permute-done | bytes 217120 | tf_op jit(solution)/shard_map/ppermute | solution.py:178
  24.6 3.2 %smooth.1 = (f32[8,32,128]{2,1,0:T(8,128)S(1)}, f32[6,48,128]{2,1,0:T(8,128)S(1)}, f32[32,8,128]{2,1,0:T(8,128)S(1)}) custom-call(f32[24,32,128]{2,1,0:T(8,128)S(1)} %maximum_multiply_fusion.block, f32[8,32,128]{2,1,0:T(8,128)S(1)} %collective-permute-done.pp, f32[8,32,128]{2,1,0:T(8,128)S(1)} %collective-permute-done.1.pf, ...), custom_call_target="tpu_custom_call" | custom-call | tf_op jit(solution)/shard_map/smooth/pallas_call | solution.py:415
  27.8 12.6 %all_to_all.5.gathered = f32[32,8,128]{2,1,0:T(8,128)S(1)} all-to-all(f32[32,8,128]{2,1,0:T(8,128)S(1)} %get-tuple-element.18), channel_id=1, replica_groups=mesh['gx'=8,'gy'=4] {'gx','gy'}, dimensions={0} | all-to-all | bytes 262144 | tf_op jit(solution)/shard_map/all_to_all | solution.py:665
  40.4 3.0 %correct.1 = f32[8,32,128]{2,1,0:T(8,128)} custom-call(f32[32,8,128]{2,1,0:T(8,128)S(1)} %all_to_all.5.gathered, f32[8,32,128]{2,1,0:T(8,128)S(1)} %get-tuple-element.19.smoothed, f32[6,48,128]{2,1,0:T(8,128)S(1)} %get-tuple-element.20.error_one), custom_call_target="tpu_custom_call" | custom-call | tf_op jit(solution)/shard_map/correct/pallas_call | solution.py:667
  (2 shorter events, 0.0 us)
Async XLA Ops:
  0.0 2.1 %collective-permute-start = (f32[8,32,128]{2,1,0:T(8,128)}, f32[8,32,128]{2,1,0:T(8,128)S(1)}, u32[]{:S(2)}, u32[]{:S(2)}) collective-permute-start(f32[8,32,128]{2,1,0:T(8,128)} %param.3), channel_id=1, source_target_pairs={{0,4},{4,0},{8,12},{12,8},{16,20},{20,16},{24,28},{28,24},{1,5},{5... | collective-permute-start | bytes 393224 | tf_op jit(solution)/shard_map/ppermute | solution.py:165
  0.5 1.7 %collective-permute-start.1 = (f32[8,32,128]{2,1,0:T(8,128)}, f32[8,32,128]{2,1,0:T(8,128)S(1)}, u32[]{:S(2)}, u32[]{:S(2)}) collective-permute-start(f32[8,32,128]{2,1,0:T(8,128)} %param.4), channel_id=1, source_target_pairs={{0,4},{4,0},{8,12},{12,8},{16,20},{20,16},{24,28},{28,24},{1,5},{5... | collective-permute-start | bytes 393224 | tf_op jit(solution)/shard_map/ppermute | solution.py:165
  0.5 1.7 %collective-permute-start.2 = (f32[8,32,128]{2,1,0:T(8,128)}, f32[8,32,128]{2,1,0:T(8,128)S(1)}, u32[]{:S(2)}, u32[]{:S(2)}) collective-permute-start(f32[8,32,128]{2,1,0:T(8,128)} %param.5), channel_id=1, source_target_pairs={{0,4},{4,0},{8,12},{12,8},{16,20},{20,16},{24,28},{28,24},{1,5},{5... | collective-permute-start | bytes 393224 | tf_op jit(solution)/shard_map/ppermute | solution.py:165
  2.3 8.9 %collective-permute-start.3 = (f32[256,128]{1,0:T(8,128)S(1)}, f32[256,128]{1,0:T(8,128)S(1)}, u32[]{:S(2)}, u32[]{:S(2)}) collective-permute-start(f32[256,128]{1,0:T(8,128)S(1)} %get-tuple-element.13), channel_id=1, source_target_pairs={{4,8},{12,16},{20,24},{8,4},{16,12},{24,20},{5,9},{13,17},{21,25},... | collective-permute-start | bytes 393224 | tf_op jit(solution)/shard_map/ppermute | solution.py:172
  2.9 8.2 %collective-permute-start.5 = (f32[2,32,128]{2,1,0:T(8,128)S(1)}, f32[2,32,128]{2,1,0:T(8,128)S(1)}, u32[]{:S(2)}, u32[]{:S(2)}) collective-permute-start(f32[2,32,128]{2,1,0:T(8,128)S(1)} %get-tuple-element.15), channel_id=1, source_target_pairs={{8,0},{16,8},{24,16},{4,12},{12,20},{20,28},{9,1},{17,9},{25,17},{... | collective-permute-start | bytes 98312 | tf_op jit(solution)/shard_map/ppermute | solution.py:171
  4.2 12.5 %collective-permute-start.4 = (f32[456,128]{1,0:T(8,128)S(1)}, f32[456,128]{1,0:T(8,128)S(1)}, u32[]{:S(2)}, u32[]{:S(2)}) collective-permute-start(f32[456,128]{1,0:T(8,128)S(1)} %get-tuple-element.14), channel_id=1, source_target_pairs={{4,8},{12,16},{20,24},{8,4},{16,12},{24,20},{5,9},{13,17},{21,25},... | collective-permute-start | bytes 700424 | tf_op jit(solution)/shard_map/ppermute | solution.py:179
  11.2 9.3 %collective-permute-start.6 = (f32[424,128]{1,0:T(8,128)S(1)}, f32[424,128]{1,0:T(8,128)S(1)}, u32[]{:S(2)}, u32[]{:S(2)}) collective-permute-start(f32[424,128]{1,0:T(8,128)S(1)} %get-tuple-element.16), channel_id=1, source_target_pairs={{0,1},{1,2},{2,3},{4,5},{5,6},{6,7},{8,9},{9,10},{10,11},{12,13},{... | collective-permute-start | bytes 651272 | tf_op jit(solution)/shard_map/ppermute | solution.py:177
  15.4 9.2 %collective-permute-start.7 = (f32[424,128]{1,0:T(8,128)S(1)}, f32[424,128]{1,0:T(8,128)S(1)}, u32[]{:S(2)}, u32[]{:S(2)}) collective-permute-start(f32[424,128]{1,0:T(8,128)S(1)} %get-tuple-element.17), channel_id=1, source_target_pairs={{1,0},{2,1},{3,2},{5,4},{6,5},{7,6},{9,8},{10,9},{11,10},{13,12},{... | collective-permute-start | bytes 651272 | tf_op jit(solution)/shard_map/ppermute | solution.py:178

commit v5 on v4

--- a/solution.py
+++ b/solution.py
@@ -33,9 +33,12 @@
     for array, distance, _ in side_entries():
         key = (array, distance)
         ends = y_rows(distance, array)
-        put(0, first, key, 0, ends)
-        put(0, first, key, cells_y - ends, ends)
-        put(1, second, key, ends, cells_y - 2 * ends)
+        if array != 1 and distance == 1:
+            put(0, first, key, 0, cells_y)
+        else:
+            put(0, first, key, 0, ends)
+            put(0, first, key, cells_y - ends, ends)
+            put(1, second, key, ends, cells_y - 2 * ends)
     return first, second, [-(-length // 8) * 8 for length in lengths]
 
 
@@ -44,8 +47,7 @@
     start = 0
     inside = [(0, m) for m in range(cells_x // 2)] + [(a, x) for a in (1, 2) for x in range(cells_x)]
     chosen = [("inside", array, index, y_rows(0, array)) for array, index in inside]
-    for side in ("low", "high"):
-        chosen += [(side, array, distance, y_rows(distance, array)) for array, distance, _ in side_entries()]
+    chosen += [("away", array, distance, y_rows(distance, array)) for array, distance, _ in side_entries()]
     for side, array, index, rows in chosen:
         pieces.append((side, array, index, rows, start))
         start += rows
@@ -65,11 +67,6 @@
     count = lax.axis_size("gx")
     pairs = [(i, i + 1) for i in range(1, count - 1, 2)]
     return pairs + [(j, i) for i, j in pairs]
-
-
-def far_pairs():
-    count = lax.axis_size("gx")
-    return [(i, i - 2) for i in range(2, count, 2)] + [(i, i + 2) for i in range(1, count - 2, 2)]
 
 
 def inside_rows(member, own, partner, array, index, first, rows):
@@ -96,7 +93,7 @@
         pl.when(me == member)(functools.partial(body, member))
 
 
-def split_kernel(block, pp, pf, pk, first, second, far):
+def split_kernel(block, pp, pf, pk, first, second):
     cells_x, cells_y, _ = pp.shape
     p, f, k = views(block, cells_x)
     plans = x_plan(cells_y)
@@ -109,39 +106,26 @@
                 for row, rows, start in pieces:
                     value = inside_rows(member, (p, f, k), (pp, pf, pk), array, index, row, rows)
                     target[pl.ds(start, rows), :] = value
-        outermost = (cells_x - 1) * member
-        far[0] = p[outermost]
-        far[1] = k[outermost]
 
     for_member(body)
 
 
-def pack_kernel(block, pp, pf, pk, received, far, to_up, to_down):
-    cells_x, cells_y, _ = pp.shape
-    p, f, k = views(block, cells_x)
+def pack_kernel(block, received, to_up, to_down, far):
+    cells_x, cells_y = block.shape[0] // 3, block.shape[1]
+    own = views(block, cells_x)
     plan = x_plan(cells_y)[0]
 
-    def body(member):
-        away = ("low", "high")[member]
-
-        def piece(side, array, index, rows, row):
-            if side == away:
-                place = [s for r, _, s in plan[array, index] if r == row][0]
-                return received[pl.ds(place, rows), :]
-            if side != "inside" and index == REACH:
-                return far[0 if array == 0 else 1, pl.ds(row, rows), :]
-            if side == "inside":
-                index += (cells_x // 2 if array == 0 else cells_x) * member
-            else:
-                plane = cells_x - index if member == 1 else cells_x - 1 + index
-                index = plane // 2 if array == 0 else plane
-            return inside_rows(member, (p, f, k), (pp, pf, pk), array, index, row, rows)
-
-        for side, array, index, rows, start in y_plan(cells_x)[0]:
-            to_up[pl.ds(start, rows), :] = piece(side, array, index, rows, cells_y - rows)
-            to_down[pl.ds(start, rows), :] = piece(side, array, index, rows, 0)
-
-    for_member(body)
+    def piece(side, array, index, rows, row):
+        if side == "inside":
+            return inside_rows(0, own, None, array, index, row, rows)
+        place = [s + row - r for r, count, s in plan[array, index] if r <= row and row + rows <= r + count][0]
+        return received[pl.ds(place, rows), :]
+
+    for side, array, index, rows, start in y_plan(cells_x)[0]:
+        to_up[pl.ds(start, rows), :] = piece(side, array, index, rows, cells_y - rows)
+        to_down[pl.ds(start, rows), :] = piece(side, array, index, rows, 0)
+    far[0] = piece("away", 0, 1, cells_y, 0)
+    far[1] = piece("away", 2, 1, cells_y, 0)
 
 
 def stacked(pressure, source, coefficient):
@@ -164,24 +148,27 @@
 
     partner = tuple(lax.ppermute(v, "gx", swap_pairs()) for v in own)
     lengths = x_plan(cells_y)[2]
-    planes = jax.ShapeDtypeStruct((2, cells_y, depth), jnp.float32)
-    first, second, outermost = pl.pallas_call(
-        split_kernel, out_shape=[packed(n) for n in lengths] + [planes], compiler_params=params, name="split_block"
+    first, second = pl.pallas_call(
+        split_kernel, out_shape=[packed(n) for n in lengths], compiler_params=params, name="split_block"
     )(block, *partner)
-    far = lax.ppermute(outermost, "gx", far_pairs())
     received = lax.ppermute(first, "gx", x_pairs())
     length = y_plan(cells_x)[1]
-    to_up, to_down = pl.pallas_call(
-        pack_kernel, out_shape=[packed(length)] * 2, compiler_params=params, name="pack_halo"
-    )(block, *partner, received, far)
+    planes = jax.ShapeDtypeStruct((2, cells_y, depth), jnp.float32)
+    to_up, to_down, outermost = pl.pallas_call(
+        pack_kernel, out_shape=[packed(length), packed(length), planes], compiler_params=params, name="pack_halo"
+    )(block, received)
     below = lax.ppermute(to_up, "gy", shifts("gy", 1))
     above = lax.ppermute(to_down, "gy", shifts("gy", -1))
+    far = lax.ppermute(outermost, "gx", swap_pairs())
     rest = lax.ppermute(second, "gx", x_pairs())
-    return *partner, received, rest, far, below, above
+    below, above, far, rest = lax.optimization_barrier((below, above, far, rest))
+    p_below = lax.ppermute(below, "gx", swap_pairs())
+    p_above = lax.ppermute(above, "gx", swap_pairs())
+    return *partner, received, rest, far, below, above, p_below, p_above
 
 
 def smooth_kernel(
-    block, pp, pf, pk, received, rest, far, below, above,
+    block, pp, pf, pk, received, rest, far, below, above, p_below, p_above,
     out, error_one, tiles,
     vp, vf, vk, wx, wy, zl, zh, dg, inv, va, vb,
     t0, t1, f1, k1, inv1, g1, h1, q2,
@@ -225,17 +212,21 @@
                     for each in spans[array, distance]:
                         fill(array, outside(away, each), row, value)
 
+        towards_partner = cells_x * (1 - 2 * member)
+        for before, after, is_partner in ((below, above, False), (p_below, p_above, True)):
+            for side, array, index, count, start in y_plan(cells_x)[0]:
+                if side == "inside":
+                    xs = (2 * index, 2 * index + 1) if array == 0 else (index,)
+                    xs = [x + towards_partner * is_partner for x in xs]
+                elif is_partner:
+                    xs = [outside(near, cells_x + each) for each in spans[array, index]]
+                else:
+                    xs = [outside(away, each) for each in spans[array, index]]
+                for x in xs:
+                    fill(array, x, -count, before[pl.ds(start, count), :])
+                    fill(array, x, cells_y, after[pl.ds(start, count), :])
+
     for_member(fill_member)
-    for side, array, index, count, start in y_plan(cells_x)[0]:
-        before = below[pl.ds(start, count), :]
-        after = above[pl.ds(start, count), :]
-        if side == "inside":
-            xs = (2 * index, 2 * index + 1) if array == 0 else (index,)
-        else:
-            xs = [outside(side, each) for each in spans[array, index]]
-        for x in xs:
-            fill(array, x, -count, before)
-            fill(array, x, cells_y, after)
 
     def lanes(count):
         return lax.broadcasted_iota(jnp.int32, (count, depth), 1)

time: 43.7 us -> 43 us (0.984)
  waiting for transfers between devices: 14.2 us -> 2.34 us
  starting transfers between devices: 9.07 us -> 18.4 us
  blocking collectives: 12.6 us -> 14.4 us
    ppermute x1 -> x3, starting transfers between devices: 1.29 us -> 10 us  [the longest x1 6.3 us: fine_halo(): far = lax.ppermute(outermost, 'gx', swap_pairs())]
    ppermute x1, waiting for transfers between devices: 4.13 us -> 0.01 us  [fine_halo(): above = lax.ppermute(to_down, 'gy', shifts('gy', -1))]
    ppermute x1 -> x3, waiting for transfers between devices: 6.22 us -> 2.24 us  [the longest x1 1.01 us: fine_halo(): p_below = lax.ppermute(below, 'gx', swap_pairs())]
    ppermute x1, waiting for transfers between devices: 3.78 us -> 0.01 us  [fine_halo(): below = lax.ppermute(to_up, 'gy', shifts('gy', 1))]
    all_to_all x1, blocking collectives: 12.6 us -> 14.4 us  [correct_whole(): gathered = lax.all_to_all(tiles, ('gx', 'gy'), 0, 0, tiled=False)]
    ppermute x1, starting transfers between devices: 4.18 us -> 4.81 us  [fine_halo(): below = lax.ppermute(to_up, 'gy', shifts('gy', 1))]
  transfers between devices with their start and end apart: 8 -> 10, of which waited for: 4 -> 4; matrix products, arithmetic and copies ran while one was open for 3% -> 3% of each run, Pallas kernels for 0% -> 0%
where the time goes in v5:
time: 43 us; the launch traced here: 42.8 us
  starting transfers between devices  18.4 us (43%)
  blocking collectives  14.4 us (33%)
  Pallas kernels  6.3 us (15%)
  waiting for transfers between devices  2.34 us (5%)
  other arithmetic  1.12 us (3%)
    all_to_all x1, blocking collectives, correct_whole(): gathered = lax.all_to_all(tiles, ('gx', 'gy'), 0, 0, tiled=False)  14.4 us
    ppermute x1, starting transfers between devices, fine_halo(): far = lax.ppermute(outermost, 'gx', swap_pairs())  6.3 us
    ppermute x1, starting transfers between devices, fine_halo(): below = lax.ppermute(to_up, 'gy', shifts('gy', 1))  4.81 us
    ppermute x1, starting transfers between devices, fine_halo(): p_below = lax.ppermute(below, 'gx', swap_pairs())  3.74 us
    pallas_call x1, Pallas kernels, smooth(): pl.pallas_call(smooth_kernel, out_shape=(jax.ShapeDtypeStruct((cells_x, c...  3.21 us
    pallas_call x1, Pallas kernels, correct_whole(): pl.pallas_call(functools.partial(correct_kernel, grid), out_shape=jax.Sha...  3.01 us
    ppermute x1, starting transfers between devices, fine_halo(): above = lax.ppermute(to_down, 'gy', shifts('gy', -1))  1.29 us
    mul x1, other arithmetic, stacked(): block * jnp.where((plane >= cells_x) & (plane < 2 * cells_x), 2.0, 1.0)  1.12 us
  transfers between devices with their start and end apart: 10, of which 4 were waited for; matrix products, arithmetic and copies ran while one was open for 3% of the time, Pallas kernels for 0%

profile of v5, /device:TPU:0, one launch (start us, length us, event | category | flops | bytes accessed | tf_op | source)
XLA Modules:
  0.0 42.8 jit_solution(304299122863845345)
XLA Ops:
  0.0 0.5 %collective-permute-start = (f32[8,32,128]{2,1,0:T(8,128)}, f32[8,32,128]{2,1,0:T(8,128)S(1)}, u32[]{:S(2)}, u32[]{:S(2)}) collective-permute-start(f32[8,32,128]{2,1,0:T(8,128)} %param.3), channel_id=1, source_target_pairs={{0,4},{4,0},{8,12},{12,8},{16,20},{20,16},{24,28},{28,24},{1,5},{5... | collective-permute-start | bytes 393224 | tf_op jit(solution)/shard_map/ppermute | solution.py:149
  0.5 0.1 collective-permute-start.1
  0.5 0.5 %collective-permute-start.2 = (f32[8,32,128]{2,1,0:T(8,128)}, f32[8,32,128]{2,1,0:T(8,128)S(1)}, u32[]{:S(2)}, u32[]{:S(2)}) collective-permute-start(f32[8,32,128]{2,1,0:T(8,128)} %param.5), channel_id=1, source_target_pairs={{0,4},{4,0},{8,12},{12,8},{16,20},{20,16},{24,28},{28,24},{1,5},{5... | collective-permute-start | bytes 393224 | tf_op jit(solution)/shard_map/ppermute | solution.py:149
  1.0 1.1 %maximum_multiply_fusion.block = f32[24,32,128]{2,1,0:T(8,128)S(1)} fusion(f32[8,32,128]{2,1,0:T(8,128)} %param.5, f32[8,32,128]{2,1,0:T(8,128)} %param.4, f32[8,32,128]{2,1,0:T(8,128)} %param.3, f32[24]{0:T(128)S(1)} %and_select_fusion), kind=kLoop, calls=%fused_computation | loop fusion | flops 294912 | bytes 786528 | tf_op jit(solution)/shard_map/mul | solution.py:135
  2.1 0.0 collective-permute-done.pp
  2.1 0.0 collective-permute-done.1.pf
  2.1 0.1 collective-permute-done.2.pk
  2.2 0.7 %collective-permute-start.3 = (f32[280,128]{1,0:T(8,128)S(1)}, f32[280,128]{1,0:T(8,128)S(1)}, u32[]{:S(2)}, u32[]{:S(2)}) collective-permute-start(f32[280,128]{1,0:T(8,128)S(1)} %get-tuple-element.17), channel_id=1, source_target_pairs={{4,8},{12,16},{20,24},{8,4},{16,12},{24,20},{5,9},{13,17},{21,25},... | collective-permute-start | bytes 430088 | tf_op jit(solution)/shard_map/ppermute | solution.py:154
  2.9 0.7 %collective-permute-start.7 = (f32[432,128]{1,0:T(8,128)S(1)}, f32[432,128]{1,0:T(8,128)S(1)}, u32[]{:S(2)}, u32[]{:S(2)}) collective-permute-start(f32[432,128]{1,0:T(8,128)S(1)} %get-tuple-element.21), channel_id=1, source_target_pairs={{4,8},{12,16},{20,24},{8,4},{16,12},{24,20},{5,9},{13,17},{21,25},... | collective-permute-start | bytes 663560 | tf_op jit(solution)/shard_map/ppermute | solution.py:163
  3.6 0.0 collective-permute-done.3.received
  3.7 4.8 %collective-permute-start.4 = (f32[304,128]{1,0:T(8,128)S(1)}, f32[304,128]{1,0:T(8,128)S(1)}, u32[]{:S(2)}, u32[]{:S(2)}) collective-permute-start(f32[304,128]{1,0:T(8,128)S(1)} %get-tuple-element.18), channel_id=1, source_target_pairs={{0,1},{1,2},{2,3},{4,5},{5,6},{6,7},{8,9},{9,10},{10,11},{12,13},{... | collective-permute-start | bytes 466952 | tf_op jit(solution)/shard_map/ppermute | solution.py:160
  8.5 1.3 %collective-permute-start.5 = (f32[304,128]{1,0:T(8,128)S(1)}, f32[304,128]{1,0:T(8,128)S(1)}, u32[]{:S(2)}, u32[]{:S(2)}) collective-permute-start(f32[304,128]{1,0:T(8,128)S(1)} %get-tuple-element.19), channel_id=1, source_target_pairs={{1,0},{2,1},{3,2},{5,4},{6,5},{7,6},{9,8},{10,9},{11,10},{13,12},{... | collective-permute-start | bytes 466952 | tf_op jit(solution)/shard_map/ppermute | solution.py:161
  9.8 6.3 %collective-permute-start.6 = (f32[2,32,128]{2,1,0:T(8,128)S(1)}, f32[2,32,128]{2,1,0:T(8,128)S(1)}, u32[]{:S(2)}, u32[]{:S(2)}) collective-permute-start(f32[2,32,128]{2,1,0:T(8,128)S(1)} %get-tuple-element.20), channel_id=1, source_target_pairs={{0,4},{4,0},{8,12},{12,8},{16,20},{20,16},{24,28},{28,24},{1,5},{5... | collective-permute-start | bytes 98312 | tf_op jit(solution)/shard_map/ppermute | solution.py:162
  16.1 0.9 %collective-permute-done.6.far = f32[2,32,128]{2,1,0:T(8,128)S(1)} collective-permute-done((f32[2,32,128]{2,1,0:T(8,128)S(1)}, f32[2,32,128]{2,1,0:T(8,128)S(1)}, u32[]{:S(2)}, u32[]{:S(2)}) %collective-permute-start.6) | collective-permute-done | bytes 32800 | tf_op jit(solution)/shard_map/ppermute | solution.py:162
  16.9 0.0 collective-permute-done.7.rest
  17.0 0.0 collective-permute-done.4.below
  17.0 0.0 collective-permute-done.5.above
  17.0 3.7 %collective-permute-start.8 = (f32[304,128]{1,0:T(8,128)S(1)}, f32[304,128]{1,0:T(8,128)S(1)}, u32[]{:S(2)}, u32[]{:S(2)}) collective-permute-start(f32[304,128]{1,0:T(8,128)S(1)} %collective-permute-done.4.below), channel_id=1, source_target_pairs={{0,4},{4,0},{8,12},{12,8},{16,20},{20,16},{24,28},{28,24},{1,5},{5... | collective-permute-start | bytes 466952 | tf_op jit(solution)/shard_map/ppermute | solution.py:165
  20.7 0.0 collective-permute-start.9
  20.7 1.0 %collective-permute-done.8.p_below = f32[304,128]{1,0:T(8,128)S(1)} collective-permute-done((f32[304,128]{1,0:T(8,128)S(1)}, f32[304,128]{1,0:T(8,128)S(1)}, u32[]{:S(2)}, u32[]{:S(2)}) %collective-permute-start.8) | collective-permute-done | bytes 155680 | tf_op jit(solution)/shard_map/ppermute | solution.py:165
  21.7 0.4 collective-permute-done.9.p_above
  22.1 3.2 %smooth.1 = (f32[8,32,128]{2,1,0:T(8,128)S(1)}, f32[6,48,128]{2,1,0:T(8,128)S(1)}, f32[32,8,128]{2,1,0:T(8,128)S(1)}) custom-call(f32[24,32,128]{2,1,0:T(8,128)S(1)} %maximum_multiply_fusion.block, f32[8,32,128]{2,1,0:T(8,128)S(1)} %collective-permute-done.pp, f32[8,32,128]{2,1,0:T(8,128)S(1)} %collective-permute-done.1.pf, ...), custom_call_target="tpu_custom_call" | custom-call | tf_op jit(solution)/shard_map/smooth/pallas_call | solution.py:406
  25.3 14.4 %all_to_all.5.gathered = f32[32,8,128]{2,1,0:T(8,128)S(1)} all-to-all(f32[32,8,128]{2,1,0:T(8,128)S(1)} %get-tuple-element.26), channel_id=1, replica_groups=mesh['gx'=8,'gy'=4] {'gx','gy'}, dimensions={0} | all-to-all | bytes 262144 | tf_op jit(solution)/shard_map/all_to_all | solution.py:656
  39.7 3.0 %correct.1 = f32[8,32,128]{2,1,0:T(8,128)} custom-call(f32[32,8,128]{2,1,0:T(8,128)S(1)} %all_to_all.5.gathered, f32[8,32,128]{2,1,0:T(8,128)S(1)} %get-tuple-element.27.smoothed, f32[6,48,128]{2,1,0:T(8,128)S(1)} %get-tuple-element.28.error_one), custom_call_target="tpu_custom_call" | custom-call | tf_op jit(solution)/shard_map/correct/pallas_call | solution.py:658
  (3 shorter events, 0.1 us)
Async XLA Ops:
  0.0 2.1 %collective-permute-start = (f32[8,32,128]{2,1,0:T(8,128)}, f32[8,32,128]{2,1,0:T(8,128)S(1)}, u32[]{:S(2)}, u32[]{:S(2)}) collective-permute-start(f32[8,32,128]{2,1,0:T(8,128)} %param.3), channel_id=1, source_target_pairs={{0,4},{4,0},{8,12},{12,8},{16,20},{20,16},{24,28},{28,24},{1,5},{5... | collective-permute-start | bytes 393224 | tf_op jit(solution)/shard_map/ppermute | solution.py:149
  0.5 1.7 %collective-permute-start.1 = (f32[8,32,128]{2,1,0:T(8,128)}, f32[8,32,128]{2,1,0:T(8,128)S(1)}, u32[]{:S(2)}, u32[]{:S(2)}) collective-permute-start(f32[8,32,128]{2,1,0:T(8,128)} %param.4), channel_id=1, source_target_pairs={{0,4},{4,0},{8,12},{12,8},{16,20},{20,16},{24,28},{28,24},{1,5},{5... | collective-permute-start | bytes 393224 | tf_op jit(solution)/shard_map/ppermute | solution.py:149
  0.5 1.7 %collective-permute-start.2 = (f32[8,32,128]{2,1,0:T(8,128)}, f32[8,32,128]{2,1,0:T(8,128)S(1)}, u32[]{:S(2)}, u32[]{:S(2)}) collective-permute-start(f32[8,32,128]{2,1,0:T(8,128)} %param.5), channel_id=1, source_target_pairs={{0,4},{4,0},{8,12},{12,8},{16,20},{20,16},{24,28},{28,24},{1,5},{5... | collective-permute-start | bytes 393224 | tf_op jit(solution)/shard_map/ppermute | solution.py:149
  2.2 1.4 %collective-permute-start.3 = (f32[280,128]{1,0:T(8,128)S(1)}, f32[280,128]{1,0:T(8,128)S(1)}, u32[]{:S(2)}, u32[]{:S(2)}) collective-permute-start(f32[280,128]{1,0:T(8,128)S(1)} %get-tuple-element.17), channel_id=1, source_target_pairs={{4,8},{12,16},{20,24},{8,4},{16,12},{24,20},{5,9},{13,17},{21,25},... | collective-permute-start | bytes 430088 | tf_op jit(solution)/shard_map/ppermute | solution.py:154
  2.9 14.0 %collective-permute-start.7 = (f32[432,128]{1,0:T(8,128)S(1)}, f32[432,128]{1,0:T(8,128)S(1)}, u32[]{:S(2)}, u32[]{:S(2)}) collective-permute-start(f32[432,128]{1,0:T(8,128)S(1)} %get-tuple-element.21), channel_id=1, source_target_pairs={{4,8},{12,16},{20,24},{8,4},{16,12},{24,20},{5,9},{13,17},{21,25},... | collective-permute-start | bytes 663560 | tf_op jit(solution)/shard_map/ppermute | solution.py:163
  3.7 13.3 %collective-permute-start.4 = (f32[304,128]{1,0:T(8,128)S(1)}, f32[304,128]{1,0:T(8,128)S(1)}, u32[]{:S(2)}, u32[]{:S(2)}) collective-permute-start(f32[304,128]{1,0:T(8,128)S(1)} %get-tuple-element.18), channel_id=1, source_target_pairs={{0,1},{1,2},{2,3},{4,5},{5,6},{6,7},{8,9},{9,10},{10,11},{12,13},{... | collective-permute-start | bytes 466952 | tf_op jit(solution)/shard_map/ppermute | solution.py:160
  8.5 8.5 %collective-permute-start.5 = (f32[304,128]{1,0:T(8,128)S(1)}, f32[304,128]{1,0:T(8,128)S(1)}, u32[]{:S(2)}, u32[]{:S(2)}) collective-permute-start(f32[304,128]{1,0:T(8,128)S(1)} %get-tuple-element.19), channel_id=1, source_target_pairs={{1,0},{2,1},{3,2},{5,4},{6,5},{7,6},{9,8},{10,9},{11,10},{13,12},{... | collective-permute-start | bytes 466952 | tf_op jit(solution)/shard_map/ppermute | solution.py:161
  9.8 7.2 %collective-permute-start.6 = (f32[2,32,128]{2,1,0:T(8,128)S(1)}, f32[2,32,128]{2,1,0:T(8,128)S(1)}, u32[]{:S(2)}, u32[]{:S(2)}) collective-permute-start(f32[2,32,128]{2,1,0:T(8,128)S(1)} %get-tuple-element.20), channel_id=1, source_target_pairs={{0,4},{4,0},{8,12},{12,8},{16,20},{20,16},{24,28},{28,24},{1,5},{5... | collective-permute-start | bytes 98312 | tf_op jit(solution)/shard_map/ppermute | solution.py:162
  17.0 4.8 %collective-permute-start.8 = (f32[304,128]{1,0:T(8,128)S(1)}, f32[304,128]{1,0:T(8,128)S(1)}, u32[]{:S(2)}, u32[]{:S(2)}) collective-permute-start(f32[304,128]{1,0:T(8,128)S(1)} %collective-permute-done.4.below), channel_id=1, source_target_pairs={{0,4},{4,0},{8,12},{12,8},{16,20},{20,16},{24,28},{28,24},{1,5},{5... | collective-permute-start | bytes 466952 | tf_op jit(solution)/shard_map/ppermute | solution.py:165
  20.7 1.4 %collective-permute-start.9 = (f32[304,128]{1,0:T(8,128)S(1)}, f32[304,128]{1,0:T(8,128)S(1)}, u32[]{:S(2)}, u32[]{:S(2)}) collective-permute-start(f32[304,128]{1,0:T(8,128)S(1)} %collective-permute-done.5.above), channel_id=1, source_target_pairs={{0,4},{4,0},{8,12},{12,8},{16,20},{20,16},{24,28},{28,24},{1,5},{5... | collective-permute-start | bytes 466952 | tf_op jit(solution)/shard_map/ppermute | solution.py:166

commit v6 on v5

--- a/solution.py
+++ b/solution.py
@@ -527,29 +527,44 @@
     def total(v):
         return jnp.sum(jnp.sum(v, axis=0, keepdims=True), axis=(1, 2), keepdims=True)
 
-    error = jnp.zeros_like(remain)
-    direction = remain
+    def around(v):
+        return (
+            places3.before_y(v, 2), places3.after_y(v, 2), ring(v, 8, 2), ring(v, -8, 2),
+        )
+
+    direction, sides = remain, around(remain)
+    remain_sides = sides
     norm_now = total(remain * remain)
+    error = error_before = error_after = jnp.zeros_like(remain)
     for repeat in range(CSWEEPS):
-        image = (diagonal3 * direction - whole_sum(direction, weights3, places3, 2)) * (1.0 / 128.0)
+        coupled = weights3[0] * before_x(direction) + weights3[1] * after_x(direction)
+        coupled += weights3[2] * sides[0] + weights3[3] * sides[1]
+        coupled += weights3[4] * sides[2] + weights3[5] * sides[3]
+        image = (diagonal3 * direction - coupled) * (1.0 / 128.0)
         alpha = norm_now / total(direction * image)
         error = error + alpha * direction
+        error_before = error_before + alpha * sides[0]
+        error_after = error_after + alpha * sides[1]
         if repeat == CSWEEPS - 1:
             break
+        image_sides = around(image)
         remain = remain - alpha * image
+        remain_sides = [r - alpha * q for r, q in zip(remain_sides, image_sides)]
         norm_next = total(remain * remain)
-        direction = remain + norm_next / norm_now * direction
+        beta = norm_next / norm_now
+        direction = remain + beta * direction
+        sides = [r + beta * p for r, p in zip(remain_sides, sides)]
         norm_now = norm_next
 
+    near = jnp.where(
+        first_row,
+        jnp.where(places3.has_before_y(2), error_before, 0.0),
+        jnp.where(places3.has_after_y(2), error_after, 0.0),
+    )
+    error = 0.75 * error + 0.25 * near
     lower = 0.75 * error + 0.25 * before_x(error)
     upper = 0.75 * error + 0.25 * after_x(error)
     fine = jnp.stack([lower, upper], 1).reshape(k2.shape)
-    near = jnp.where(
-        (places.row & 1) == 0,
-        jnp.where(places.has_before_y(1), places.before_y(fine, 1), 0.0),
-        jnp.where(places.has_after_y(1), places.after_y(fine, 1), 0.0),
-    )
-    fine = 0.75 * fine + 0.25 * near
     near = jnp.where(
         (places.lane & 4) == 0,
         jnp.where(places.has_before_z(1), ring(fine, 4, 2), 0.0),
@@ -626,14 +641,16 @@
     whole[planes + 1] = jnp.zeros((8, 128), jnp.float32)
     whole[pl.ds(1, planes)] = whole_solve(k2, rhs2)
 
+    masks = [[(j + side - lane) == shift for shift in range(-4, 5)] for side in (-1, 0, 1)]
+    inside = (j > 0, True, j < ny - 1)
     for x in range(4):
-        centre = pltpu.roll(whole[2 * i + x], lax.rem(128 - j, 128), 1)
-        below = jnp.where(j > 0, ring(centre, 1, 1), 0.0)
-        above = jnp.where(j < ny - 1, ring(centre, -1, 1), 0.0)
-        for index, value in enumerate((below, centre, above)):
-            value = jnp.where(lane == 0, value, 0.0)
-            value = value + ring(value, 1, 1)
-            strip[x, pl.ds(8 * index, 8), :] = value + ring(value, 2, 1)
+        plane = whole[2 * i + x]
+        turned = [plane if shift == 0 else ring(plane, -shift, 1) for shift in range(-4, 5)]
+        for index in range(3):
+            value = jnp.zeros_like(plane)
+            for mask, each in zip(masks[index], turned):
+                value = jnp.where(mask, each, value)
+            strip[x, pl.ds(8 * index, 8), :] = value if index == 1 else jnp.where(inside[index], value, 0.0)
         for place in range(4):
             wide[x, pl.ds(4 + place, 8, stride=4), :] = strip[x, pl.ds(7, 8), :]
             wide[x, pl.ds(36 + place, 2, stride=4), :] = strip[x, pl.ds(15, 2), :]

time: 43 us -> 42.5 us (0.988)
  Pallas kernels: 6.3 us -> 5.82 us
    pallas_call x1, Pallas kernels: 3.01 us -> 2.52 us  [correct_whole(): pl.pallas_call(functools.partial(correct_kernel, grid), out_shape=jax.Sha...]
where the time goes in v6:
time: 42.5 us; the launch traced here: 42.3 us
  starting transfers between devices  18.4 us (43%)
  blocking collectives  14.4 us (34%)
  Pallas kernels  5.82 us (14%)
  waiting for transfers between devices  2.34 us (6%)
  other arithmetic  1.12 us (3%)
    all_to_all x1, blocking collectives, correct_whole(): gathered = lax.all_to_all(tiles, ('gx', 'gy'), 0, 0, tiled=False)  14.4 us
    ppermute x1, starting transfers between devices, fine_halo(): far = lax.ppermute(outermost, 'gx', swap_pairs())  6.3 us
    ppermute x1, starting transfers between devices, fine_halo(): below = lax.ppermute(to_up, 'gy', shifts('gy', 1))  4.81 us
    ppermute x1, starting transfers between devices, fine_halo(): p_below = lax.ppermute(below, 'gx', swap_pairs())  3.74 us
    pallas_call x1, Pallas kernels, smooth(): pl.pallas_call(smooth_kernel, out_shape=(jax.ShapeDtypeStruct((cells_x, c...  3.21 us
    pallas_call x1, Pallas kernels, correct_whole(): pl.pallas_call(functools.partial(correct_kernel, grid), out_shape=jax.Sha...  2.52 us
    ppermute x1, starting transfers between devices, fine_halo(): above = lax.ppermute(to_down, 'gy', shifts('gy', -1))  1.29 us
    mul x1, other arithmetic, stacked(): block * jnp.where((plane >= cells_x) & (plane < 2 * cells_x), 2.0, 1.0)  1.12 us
  transfers between devices with their start and end apart: 10, of which 4 were waited for; matrix products, arithmetic and copies ran while one was open for 3% of the time, Pallas kernels for 0%

profile of v6, /device:TPU:0, one launch (start us, length us, event | category | flops | bytes accessed | tf_op | source)
XLA Modules:
  0.0 42.3 jit_solution(10602499367368725779)
XLA Ops:
  0.0 0.5 %collective-permute-start = (f32[8,32,128]{2,1,0:T(8,128)}, f32[8,32,128]{2,1,0:T(8,128)S(1)}, u32[]{:S(2)}, u32[]{:S(2)}) collective-permute-start(f32[8,32,128]{2,1,0:T(8,128)} %param.3), channel_id=1, source_target_pairs={{0,4},{4,0},{8,12},{12,8},{16,20},{20,16},{24,28},{28,24},{1,5},{5... | collective-permute-start | bytes 393224 | tf_op jit(solution)/shard_map/ppermute | solution.py:149
  0.5 0.1 collective-permute-start.1
  0.5 0.5 %collective-permute-start.2 = (f32[8,32,128]{2,1,0:T(8,128)}, f32[8,32,128]{2,1,0:T(8,128)S(1)}, u32[]{:S(2)}, u32[]{:S(2)}) collective-permute-start(f32[8,32,128]{2,1,0:T(8,128)} %param.5), channel_id=1, source_target_pairs={{0,4},{4,0},{8,12},{12,8},{16,20},{20,16},{24,28},{28,24},{1,5},{5... | collective-permute-start | bytes 393224 | tf_op jit(solution)/shard_map/ppermute | solution.py:149
  1.0 1.1 %maximum_multiply_fusion.block = f32[24,32,128]{2,1,0:T(8,128)S(1)} fusion(f32[8,32,128]{2,1,0:T(8,128)} %param.5, f32[8,32,128]{2,1,0:T(8,128)} %param.4, f32[8,32,128]{2,1,0:T(8,128)} %param.3, f32[24]{0:T(128)S(1)} %and_select_fusion), kind=kLoop, calls=%fused_computation | loop fusion | flops 294912 | bytes 786528 | tf_op jit(solution)/shard_map/mul | solution.py:135
  2.1 0.0 collective-permute-done.pp
  2.1 0.0 collective-permute-done.1.pf
  2.1 0.1 collective-permute-done.2.pk
  2.2 0.7 %collective-permute-start.3 = (f32[280,128]{1,0:T(8,128)S(1)}, f32[280,128]{1,0:T(8,128)S(1)}, u32[]{:S(2)}, u32[]{:S(2)}) collective-permute-start(f32[280,128]{1,0:T(8,128)S(1)} %get-tuple-element.17), channel_id=1, source_target_pairs={{4,8},{12,16},{20,24},{8,4},{16,12},{24,20},{5,9},{13,17},{21,25},... | collective-permute-start | bytes 430088 | tf_op jit(solution)/shard_map/ppermute | solution.py:154
  2.9 0.7 %collective-permute-start.7 = (f32[432,128]{1,0:T(8,128)S(1)}, f32[432,128]{1,0:T(8,128)S(1)}, u32[]{:S(2)}, u32[]{:S(2)}) collective-permute-start(f32[432,128]{1,0:T(8,128)S(1)} %get-tuple-element.21), channel_id=1, source_target_pairs={{4,8},{12,16},{20,24},{8,4},{16,12},{24,20},{5,9},{13,17},{21,25},... | collective-permute-start | bytes 663560 | tf_op jit(solution)/shard_map/ppermute | solution.py:163
  3.6 0.0 collective-permute-done.3.received
  3.7 4.8 %collective-permute-start.4 = (f32[304,128]{1,0:T(8,128)S(1)}, f32[304,128]{1,0:T(8,128)S(1)}, u32[]{:S(2)}, u32[]{:S(2)}) collective-permute-start(f32[304,128]{1,0:T(8,128)S(1)} %get-tuple-element.18), channel_id=1, source_target_pairs={{0,1},{1,2},{2,3},{4,5},{5,6},{6,7},{8,9},{9,10},{10,11},{12,13},{... | collective-permute-start | bytes 466952 | tf_op jit(solution)/shard_map/ppermute | solution.py:160
  8.5 1.3 %collective-permute-start.5 = (f32[304,128]{1,0:T(8,128)S(1)}, f32[304,128]{1,0:T(8,128)S(1)}, u32[]{:S(2)}, u32[]{:S(2)}) collective-permute-start(f32[304,128]{1,0:T(8,128)S(1)} %get-tuple-element.19), channel_id=1, source_target_pairs={{1,0},{2,1},{3,2},{5,4},{6,5},{7,6},{9,8},{10,9},{11,10},{13,12},{... | collective-permute-start | bytes 466952 | tf_op jit(solution)/shard_map/ppermute | solution.py:161
  9.8 6.3 %collective-permute-start.6 = (f32[2,32,128]{2,1,0:T(8,128)S(1)}, f32[2,32,128]{2,1,0:T(8,128)S(1)}, u32[]{:S(2)}, u32[]{:S(2)}) collective-permute-start(f32[2,32,128]{2,1,0:T(8,128)S(1)} %get-tuple-element.20), channel_id=1, source_target_pairs={{0,4},{4,0},{8,12},{12,8},{16,20},{20,16},{24,28},{28,24},{1,5},{5... | collective-permute-start | bytes 98312 | tf_op jit(solution)/shard_map/ppermute | solution.py:162
  16.1 0.9 %collective-permute-done.6.far = f32[2,32,128]{2,1,0:T(8,128)S(1)} collective-permute-done((f32[2,32,128]{2,1,0:T(8,128)S(1)}, f32[2,32,128]{2,1,0:T(8,128)S(1)}, u32[]{:S(2)}, u32[]{:S(2)}) %collective-permute-start.6) | collective-permute-done | bytes 32800 | tf_op jit(solution)/shard_map/ppermute | solution.py:162
  16.9 0.0 collective-permute-done.7.rest
  17.0 0.0 collective-permute-done.4.below
  17.0 0.0 collective-permute-done.5.above
  17.0 3.7 %collective-permute-start.8 = (f32[304,128]{1,0:T(8,128)S(1)}, f32[304,128]{1,0:T(8,128)S(1)}, u32[]{:S(2)}, u32[]{:S(2)}) collective-permute-start(f32[304,128]{1,0:T(8,128)S(1)} %collective-permute-done.4.below), channel_id=1, source_target_pairs={{0,4},{4,0},{8,12},{12,8},{16,20},{20,16},{24,28},{28,24},{1,5},{5... | collective-permute-start | bytes 466952 | tf_op jit(solution)/shard_map/ppermute | solution.py:165
  20.7 0.0 collective-permute-start.9
  20.7 1.0 %collective-permute-done.8.p_below = f32[304,128]{1,0:T(8,128)S(1)} collective-permute-done((f32[304,128]{1,0:T(8,128)S(1)}, f32[304,128]{1,0:T(8,128)S(1)}, u32[]{:S(2)}, u32[]{:S(2)}) %collective-permute-start.8) | collective-permute-done | bytes 155680 | tf_op jit(solution)/shard_map/ppermute | solution.py:165
  21.7 0.4 collective-permute-done.9.p_above
  22.1 3.2 %smooth.1 = (f32[8,32,128]{2,1,0:T(8,128)S(1)}, f32[6,48,128]{2,1,0:T(8,128)S(1)}, f32[32,8,128]{2,1,0:T(8,128)S(1)}) custom-call(f32[24,32,128]{2,1,0:T(8,128)S(1)} %maximum_multiply_fusion.block, f32[8,32,128]{2,1,0:T(8,128)S(1)} %collective-permute-done.pp, f32[8,32,128]{2,1,0:T(8,128)S(1)} %collective-permute-done.1.pf, ...), custom_call_target="tpu_custom_call" | custom-call | tf_op jit(solution)/shard_map/smooth/pallas_call | solution.py:406
  25.3 14.4 %all_to_all.5.gathered = f32[32,8,128]{2,1,0:T(8,128)S(1)} all-to-all(f32[32,8,128]{2,1,0:T(8,128)S(1)} %get-tuple-element.26), channel_id=1, replica_groups=mesh['gx'=8,'gy'=4] {'gx','gy'}, dimensions={0} | all-to-all | bytes 262144 | tf_op jit(solution)/shard_map/all_to_all | solution.py:673
  39.7 2.5 %correct.1 = f32[8,32,128]{2,1,0:T(8,128)} custom-call(f32[32,8,128]{2,1,0:T(8,128)S(1)} %all_to_all.5.gathered, f32[8,32,128]{2,1,0:T(8,128)S(1)} %get-tuple-element.27.smoothed, f32[6,48,128]{2,1,0:T(8,128)S(1)} %get-tuple-element.28.error_one), custom_call_target="tpu_custom_call" | custom-call | tf_op jit(solution)/shard_map/correct/pallas_call | solution.py:675
  (3 shorter events, 0.1 us)
Async XLA Ops:
  0.0 2.1 %collective-permute-start = (f32[8,32,128]{2,1,0:T(8,128)}, f32[8,32,128]{2,1,0:T(8,128)S(1)}, u32[]{:S(2)}, u32[]{:S(2)}) collective-permute-start(f32[8,32,128]{2,1,0:T(8,128)} %param.3), channel_id=1, source_target_pairs={{0,4},{4,0},{8,12},{12,8},{16,20},{20,16},{24,28},{28,24},{1,5},{5... | collective-permute-start | bytes 393224 | tf_op jit(solution)/shard_map/ppermute | solution.py:149
  0.5 1.7 %collective-permute-start.1 = (f32[8,32,128]{2,1,0:T(8,128)}, f32[8,32,128]{2,1,0:T(8,128)S(1)}, u32[]{:S(2)}, u32[]{:S(2)}) collective-permute-start(f32[8,32,128]{2,1,0:T(8,128)} %param.4), channel_id=1, source_target_pairs={{0,4},{4,0},{8,12},{12,8},{16,20},{20,16},{24,28},{28,24},{1,5},{5... | collective-permute-start | bytes 393224 | tf_op jit(solution)/shard_map/ppermute | solution.py:149
  0.5 1.7 %collective-permute-start.2 = (f32[8,32,128]{2,1,0:T(8,128)}, f32[8,32,128]{2,1,0:T(8,128)S(1)}, u32[]{:S(2)}, u32[]{:S(2)}) collective-permute-start(f32[8,32,128]{2,1,0:T(8,128)} %param.5), channel_id=1, source_target_pairs={{0,4},{4,0},{8,12},{12,8},{16,20},{20,16},{24,28},{28,24},{1,5},{5... | collective-permute-start | bytes 393224 | tf_op jit(solution)/shard_map/ppermute | solution.py:149
  2.2 1.4 %collective-permute-start.3 = (f32[280,128]{1,0:T(8,128)S(1)}, f32[280,128]{1,0:T(8,128)S(1)}, u32[]{:S(2)}, u32[]{:S(2)}) collective-permute-start(f32[280,128]{1,0:T(8,128)S(1)} %get-tuple-element.17), channel_id=1, source_target_pairs={{4,8},{12,16},{20,24},{8,4},{16,12},{24,20},{5,9},{13,17},{21,25},... | collective-permute-start | bytes 430088 | tf_op jit(solution)/shard_map/ppermute | solution.py:154
  2.9 14.0 %collective-permute-start.7 = (f32[432,128]{1,0:T(8,128)S(1)}, f32[432,128]{1,0:T(8,128)S(1)}, u32[]{:S(2)}, u32[]{:S(2)}) collective-permute-start(f32[432,128]{1,0:T(8,128)S(1)} %get-tuple-element.21), channel_id=1, source_target_pairs={{4,8},{12,16},{20,24},{8,4},{16,12},{24,20},{5,9},{13,17},{21,25},... | collective-permute-start | bytes 663560 | tf_op jit(solution)/shard_map/ppermute | solution.py:163
  3.7 13.3 %collective-permute-start.4 = (f32[304,128]{1,0:T(8,128)S(1)}, f32[304,128]{1,0:T(8,128)S(1)}, u32[]{:S(2)}, u32[]{:S(2)}) collective-permute-start(f32[304,128]{1,0:T(8,128)S(1)} %get-tuple-element.18), channel_id=1, source_target_pairs={{0,1},{1,2},{2,3},{4,5},{5,6},{6,7},{8,9},{9,10},{10,11},{12,13},{... | collective-permute-start | bytes 466952 | tf_op jit(solution)/shard_map/ppermute | solution.py:160
  8.5 8.5 %collective-permute-start.5 = (f32[304,128]{1,0:T(8,128)S(1)}, f32[304,128]{1,0:T(8,128)S(1)}, u32[]{:S(2)}, u32[]{:S(2)}) collective-permute-start(f32[304,128]{1,0:T(8,128)S(1)} %get-tuple-element.19), channel_id=1, source_target_pairs={{1,0},{2,1},{3,2},{5,4},{6,5},{7,6},{9,8},{10,9},{11,10},{13,12},{... | collective-permute-start | bytes 466952 | tf_op jit(solution)/shard_map/ppermute | solution.py:161
  9.8 7.2 %collective-permute-start.6 = (f32[2,32,128]{2,1,0:T(8,128)S(1)}, f32[2,32,128]{2,1,0:T(8,128)S(1)}, u32[]{:S(2)}, u32[]{:S(2)}) collective-permute-start(f32[2,32,128]{2,1,0:T(8,128)S(1)} %get-tuple-element.20), channel_id=1, source_target_pairs={{0,4},{4,0},{8,12},{12,8},{16,20},{20,16},{24,28},{28,24},{1,5},{5... | collective-permute-start | bytes 98312 | tf_op jit(solution)/shard_map/ppermute | solution.py:162
  17.0 4.8 %collective-permute-start.8 = (f32[304,128]{1,0:T(8,128)S(1)}, f32[304,128]{1,0:T(8,128)S(1)}, u32[]{:S(2)}, u32[]{:S(2)}) collective-permute-start(f32[304,128]{1,0:T(8,128)S(1)} %collective-permute-done.4.below), channel_id=1, source_target_pairs={{0,4},{4,0},{8,12},{12,8},{16,20},{20,16},{24,28},{28,24},{1,5},{5... | collective-permute-start | bytes 466952 | tf_op jit(solution)/shard_map/ppermute | solution.py:165
  20.7 1.4 %collective-permute-start.9 = (f32[304,128]{1,0:T(8,128)S(1)}, f32[304,128]{1,0:T(8,128)S(1)}, u32[]{:S(2)}, u32[]{:S(2)}) collective-permute-start(f32[304,128]{1,0:T(8,128)S(1)} %collective-permute-done.5.above), channel_id=1, source_target_pairs={{0,4},{4,0},{8,12},{12,8},{16,20},{20,16},{24,28},{28,24},{1,5},{5... | collective-permute-start | bytes 466952 | tf_op jit(solution)/shard_map/ppermute | solution.py:166

commit v7 on v6

--- a/solution.py
+++ b/solution.py
@@ -161,7 +161,7 @@
     above = lax.ppermute(to_down, "gy", shifts("gy", -1))
     far = lax.ppermute(outermost, "gx", swap_pairs())
     rest = lax.ppermute(second, "gx", x_pairs())
-    below, above, far, rest = lax.optimization_barrier((below, above, far, rest))
+    above, far, rest = lax.optimization_barrier((above, far, rest))
     p_below = lax.ppermute(below, "gx", swap_pairs())
     p_above = lax.ppermute(above, "gx", swap_pairs())
     return *partner, received, rest, far, below, above, p_below, p_above

time: 42.5 us -> 42.1 us (level)
  blocking collectives: 14.4 us -> 16.4 us
  starting transfers between devices: 18.4 us -> 16.6 us
    ppermute x1, starting transfers between devices: 3.74 us -> 0.87 us  [fine_halo(): p_below = lax.ppermute(below, 'gx', swap_pairs())]
    all_to_all x1, blocking collectives: 14.4 us -> 16.4 us  [correct_whole(): gathered = lax.all_to_all(tiles, ('gx', 'gy'), 0, 0, tiled=False)]
    ppermute x1, starting transfers between devices: 4.81 us -> 5.44 us  [fine_halo(): below = lax.ppermute(to_up, 'gy', shifts('gy', 1))]
where the time goes in v7:
time: 42.1 us; the launch traced here: 41.9 us
  starting transfers between devices  16.6 us (39%)
  blocking collectives  16.4 us (39%)
  Pallas kernels  5.81 us (14%)
  waiting for transfers between devices  1.98 us (5%)
  other arithmetic  1.12 us (3%)
    all_to_all x1, blocking collectives, correct_whole(): gathered = lax.all_to_all(tiles, ('gx', 'gy'), 0, 0, tiled=False)  16.4 us
    ppermute x1, starting transfers between devices, fine_halo(): far = lax.ppermute(outermost, 'gx', swap_pairs())  6.3 us
    ppermute x1, starting transfers between devices, fine_halo(): below = lax.ppermute(to_up, 'gy', shifts('gy', 1))  5.44 us
    pallas_call x1, Pallas kernels, smooth(): pl.pallas_call(smooth_kernel, out_shape=(jax.ShapeDtypeStruct((cells_x, c...  3.21 us
    pallas_call x1, Pallas kernels, correct_whole(): pl.pallas_call(functools.partial(correct_kernel, grid), out_shape=jax.Sha...  2.52 us
    ppermute x1, starting transfers between devices, fine_halo(): above = lax.ppermute(to_down, 'gy', shifts('gy', -1))  1.29 us
    mul x1, other arithmetic, stacked(): block * jnp.where((plane >= cells_x) & (plane < 2 * cells_x), 2.0, 1.0)  1.12 us
    ppermute x3, starting transfers between devices, fine_halo(): partner = tuple((lax.ppermute(v, 'gx', swap_pairs()) for v in own))  0.96 us
  transfers between devices with their start and end apart: 10, of which 4 were waited for; matrix products, arithmetic and copies ran while one was open for 3% of the time, Pallas kernels for 0%

profile of v7, /device:TPU:0, one launch (start us, length us, event | category | flops | bytes accessed | tf_op | source)
XLA Modules:
  0.0 41.9 jit_solution(6479748754287486434)
XLA Ops:
  0.0 0.5 %collective-permute-start = (f32[8,32,128]{2,1,0:T(8,128)}, f32[8,32,128]{2,1,0:T(8,128)S(1)}, u32[]{:S(2)}, u32[]{:S(2)}) collective-permute-start(f32[8,32,128]{2,1,0:T(8,128)} %param.3), channel_id=1, source_target_pairs={{0,4},{4,0},{8,12},{12,8},{16,20},{20,16},{24,28},{28,24},{1,5},{5... | collective-permute-start | bytes 393224 | tf_op jit(solution)/shard_map/ppermute | solution.py:149
  0.5 0.1 collective-permute-start.1
  0.5 0.5 %collective-permute-start.2 = (f32[8,32,128]{2,1,0:T(8,128)}, f32[8,32,128]{2,1,0:T(8,128)S(1)}, u32[]{:S(2)}, u32[]{:S(2)}) collective-permute-start(f32[8,32,128]{2,1,0:T(8,128)} %param.5), channel_id=1, source_target_pairs={{0,4},{4,0},{8,12},{12,8},{16,20},{20,16},{24,28},{28,24},{1,5},{5... | collective-permute-start | bytes 393224 | tf_op jit(solution)/shard_map/ppermute | solution.py:149
  1.0 1.1 %maximum_multiply_fusion.block = f32[24,32,128]{2,1,0:T(8,128)S(1)} fusion(f32[8,32,128]{2,1,0:T(8,128)} %param.5, f32[8,32,128]{2,1,0:T(8,128)} %param.4, f32[8,32,128]{2,1,0:T(8,128)} %param.3, f32[24]{0:T(128)S(1)} %and_select_fusion), kind=kLoop, calls=%fused_computation | loop fusion | flops 294912 | bytes 786528 | tf_op jit(solution)/shard_map/mul | solution.py:135
  2.1 0.0 collective-permute-done.pp
  2.1 0.0 collective-permute-done.1.pf
  2.1 0.1 collective-permute-done.2.pk
  2.2 0.7 %collective-permute-start.3 = (f32[280,128]{1,0:T(8,128)S(1)}, f32[280,128]{1,0:T(8,128)S(1)}, u32[]{:S(2)}, u32[]{:S(2)}) collective-permute-start(f32[280,128]{1,0:T(8,128)S(1)} %get-tuple-element.16), channel_id=1, source_target_pairs={{4,8},{12,16},{20,24},{8,4},{16,12},{24,20},{5,9},{13,17},{21,25},... | collective-permute-start | bytes 430088 | tf_op jit(solution)/shard_map/ppermute | solution.py:154
  2.9 0.7 %collective-permute-start.6 = (f32[432,128]{1,0:T(8,128)S(1)}, f32[432,128]{1,0:T(8,128)S(1)}, u32[]{:S(2)}, u32[]{:S(2)}) collective-permute-start(f32[432,128]{1,0:T(8,128)S(1)} %get-tuple-element.19), channel_id=1, source_target_pairs={{4,8},{12,16},{20,24},{8,4},{16,12},{24,20},{5,9},{13,17},{21,25},... | collective-permute-start | bytes 663560 | tf_op jit(solution)/shard_map/ppermute | solution.py:163
  3.6 0.0 collective-permute-done.3.received
  3.7 1.3 %collective-permute-start.4 = (f32[304,128]{1,0:T(8,128)S(1)}, f32[304,128]{1,0:T(8,128)S(1)}, u32[]{:S(2)}, u32[]{:S(2)}) collective-permute-start(f32[304,128]{1,0:T(8,128)S(1)} %get-tuple-element.17), channel_id=1, source_target_pairs={{1,0},{2,1},{3,2},{5,4},{6,5},{7,6},{9,8},{10,9},{11,10},{13,12},{... | collective-permute-start | bytes 466952 | tf_op jit(solution)/shard_map/ppermute | solution.py:161
  5.0 5.4 %collective-permute-start.7 = (f32[304,128]{1,0:T(8,128)S(1)}, f32[304,128]{1,0:T(8,128)S(1)}, u32[]{:S(2)}, u32[]{:S(2)}) collective-permute-start(f32[304,128]{1,0:T(8,128)S(1)} %get-tuple-element.22), channel_id=1, source_target_pairs={{0,1},{1,2},{2,3},{4,5},{5,6},{6,7},{8,9},{9,10},{10,11},{12,13},{... | collective-permute-start | bytes 466952 | tf_op jit(solution)/shard_map/ppermute | solution.py:160
  10.4 6.3 %collective-permute-start.5 = (f32[2,32,128]{2,1,0:T(8,128)S(1)}, f32[2,32,128]{2,1,0:T(8,128)S(1)}, u32[]{:S(2)}, u32[]{:S(2)}) collective-permute-start(f32[2,32,128]{2,1,0:T(8,128)S(1)} %get-tuple-element.18), channel_id=1, source_target_pairs={{0,4},{4,0},{8,12},{12,8},{16,20},{20,16},{24,28},{28,24},{1,5},{5... | collective-permute-start | bytes 98312 | tf_op jit(solution)/shard_map/ppermute | solution.py:162
  16.7 0.9 %collective-permute-done.5.far = f32[2,32,128]{2,1,0:T(8,128)S(1)} collective-permute-done((f32[2,32,128]{2,1,0:T(8,128)S(1)}, f32[2,32,128]{2,1,0:T(8,128)S(1)}, u32[]{:S(2)}, u32[]{:S(2)}) %collective-permute-start.5) | collective-permute-done | bytes 32800 | tf_op jit(solution)/shard_map/ppermute | solution.py:162
  17.6 0.0 collective-permute-done.6.rest
  17.6 0.0 collective-permute-done.4.above
  17.6 0.3 collective-permute-start.9
  17.9 0.0 collective-permute-done.7.below
  17.9 0.9 %collective-permute-start.8 = (f32[304,128]{1,0:T(8,128)S(1)}, f32[304,128]{1,0:T(8,128)S(1)}, u32[]{:S(2)}, u32[]{:S(2)}) collective-permute-start(f32[304,128]{1,0:T(8,128)S(1)} %collective-permute-done.7.below), channel_id=1, source_target_pairs={{0,4},{4,0},{8,12},{12,8},{16,20},{20,16},{24,28},{28,24},{1,5},{5... | collective-permute-start | bytes 466952 | tf_op jit(solution)/shard_map/ppermute | solution.py:165
  18.8 0.2 collective-permute-done.9.p_above
  19.0 0.9 %collective-permute-done.8.p_below = f32[304,128]{1,0:T(8,128)S(1)} collective-permute-done((f32[304,128]{1,0:T(8,128)S(1)}, f32[304,128]{1,0:T(8,128)S(1)}, u32[]{:S(2)}, u32[]{:S(2)}) %collective-permute-start.8) | collective-permute-done | bytes 155680 | tf_op jit(solution)/shard_map/ppermute | solution.py:165
  19.8 3.2 %smooth.1 = (f32[8,32,128]{2,1,0:T(8,128)S(1)}, f32[6,48,128]{2,1,0:T(8,128)S(1)}, f32[32,8,128]{2,1,0:T(8,128)S(1)}) custom-call(f32[24,32,128]{2,1,0:T(8,128)S(1)} %maximum_multiply_fusion.block, f32[8,32,128]{2,1,0:T(8,128)S(1)} %collective-permute-done.pp, f32[8,32,128]{2,1,0:T(8,128)S(1)} %collective-permute-done.1.pf, ...), custom_call_target="tpu_custom_call" | custom-call | tf_op jit(solution)/shard_map/smooth/pallas_call | solution.py:406
  23.0 16.4 %all_to_all.5.gathered = f32[32,8,128]{2,1,0:T(8,128)S(1)} all-to-all(f32[32,8,128]{2,1,0:T(8,128)S(1)} %get-tuple-element.24), channel_id=1, replica_groups=mesh['gx'=8,'gy'=4] {'gx','gy'}, dimensions={0} | all-to-all | bytes 262144 | tf_op jit(solution)/shard_map/all_to_all | solution.py:673
  39.4 2.5 %correct.1 = f32[8,32,128]{2,1,0:T(8,128)} custom-call(f32[32,8,128]{2,1,0:T(8,128)S(1)} %all_to_all.5.gathered, f32[8,32,128]{2,1,0:T(8,128)S(1)} %get-tuple-element.25.smoothed, f32[6,48,128]{2,1,0:T(8,128)S(1)} %get-tuple-element.26.error_one), custom_call_target="tpu_custom_call" | custom-call | tf_op jit(solution)/shard_map/correct/pallas_call | solution.py:675
  (3 shorter events, 0.1 us)
Async XLA Ops:
  0.0 2.1 %collective-permute-start = (f32[8,32,128]{2,1,0:T(8,128)}, f32[8,32,128]{2,1,0:T(8,128)S(1)}, u32[]{:S(2)}, u32[]{:S(2)}) collective-permute-start(f32[8,32,128]{2,1,0:T(8,128)} %param.3), channel_id=1, source_target_pairs={{0,4},{4,0},{8,12},{12,8},{16,20},{20,16},{24,28},{28,24},{1,5},{5... | collective-permute-start | bytes 393224 | tf_op jit(solution)/shard_map/ppermute | solution.py:149
  0.5 1.7 %collective-permute-start.1 = (f32[8,32,128]{2,1,0:T(8,128)}, f32[8,32,128]{2,1,0:T(8,128)S(1)}, u32[]{:S(2)}, u32[]{:S(2)}) collective-permute-start(f32[8,32,128]{2,1,0:T(8,128)} %param.4), channel_id=1, source_target_pairs={{0,4},{4,0},{8,12},{12,8},{16,20},{20,16},{24,28},{28,24},{1,5},{5... | collective-permute-start | bytes 393224 | tf_op jit(solution)/shard_map/ppermute | solution.py:149
  0.5 1.7 %collective-permute-start.2 = (f32[8,32,128]{2,1,0:T(8,128)}, f32[8,32,128]{2,1,0:T(8,128)S(1)}, u32[]{:S(2)}, u32[]{:S(2)}) collective-permute-start(f32[8,32,128]{2,1,0:T(8,128)} %param.5), channel_id=1, source_target_pairs={{0,4},{4,0},{8,12},{12,8},{16,20},{20,16},{24,28},{28,24},{1,5},{5... | collective-permute-start | bytes 393224 | tf_op jit(solution)/shard_map/ppermute | solution.py:149
  2.2 1.4 %collective-permute-start.3 = (f32[280,128]{1,0:T(8,128)S(1)}, f32[280,128]{1,0:T(8,128)S(1)}, u32[]{:S(2)}, u32[]{:S(2)}) collective-permute-start(f32[280,128]{1,0:T(8,128)S(1)} %get-tuple-element.16), channel_id=1, source_target_pairs={{4,8},{12,16},{20,24},{8,4},{16,12},{24,20},{5,9},{13,17},{21,25},... | collective-permute-start | bytes 430088 | tf_op jit(solution)/shard_map/ppermute | solution.py:154
  2.9 14.7 %collective-permute-start.6 = (f32[432,128]{1,0:T(8,128)S(1)}, f32[432,128]{1,0:T(8,128)S(1)}, u32[]{:S(2)}, u32[]{:S(2)}) collective-permute-start(f32[432,128]{1,0:T(8,128)S(1)} %get-tuple-element.19), channel_id=1, source_target_pairs={{4,8},{12,16},{20,24},{8,4},{16,12},{24,20},{5,9},{13,17},{21,25},... | collective-permute-start | bytes 663560 | tf_op jit(solution)/shard_map/ppermute | solution.py:163
  3.7 13.9 %collective-permute-start.4 = (f32[304,128]{1,0:T(8,128)S(1)}, f32[304,128]{1,0:T(8,128)S(1)}, u32[]{:S(2)}, u32[]{:S(2)}) collective-permute-start(f32[304,128]{1,0:T(8,128)S(1)} %get-tuple-element.17), channel_id=1, source_target_pairs={{1,0},{2,1},{3,2},{5,4},{6,5},{7,6},{9,8},{10,9},{11,10},{13,12},{... | collective-permute-start | bytes 466952 | tf_op jit(solution)/shard_map/ppermute | solution.py:161
  5.0 13.0 %collective-permute-start.7 = (f32[304,128]{1,0:T(8,128)S(1)}, f32[304,128]{1,0:T(8,128)S(1)}, u32[]{:S(2)}, u32[]{:S(2)}) collective-permute-start(f32[304,128]{1,0:T(8,128)S(1)} %get-tuple-element.22), channel_id=1, source_target_pairs={{0,1},{1,2},{2,3},{4,5},{5,6},{6,7},{8,9},{9,10},{10,11},{12,13},{... | collective-permute-start | bytes 466952 | tf_op jit(solution)/shard_map/ppermute | solution.py:160
  10.4 7.2 %collective-permute-start.5 = (f32[2,32,128]{2,1,0:T(8,128)S(1)}, f32[2,32,128]{2,1,0:T(8,128)S(1)}, u32[]{:S(2)}, u32[]{:S(2)}) collective-permute-start(f32[2,32,128]{2,1,0:T(8,128)S(1)} %get-tuple-element.18), channel_id=1, source_target_pairs={{0,4},{4,0},{8,12},{12,8},{16,20},{20,16},{24,28},{28,24},{1,5},{5... | collective-permute-start | bytes 98312 | tf_op jit(solution)/shard_map/ppermute | solution.py:162
  17.6 1.4 %collective-permute-start.9 = (f32[304,128]{1,0:T(8,128)S(1)}, f32[304,128]{1,0:T(8,128)S(1)}, u32[]{:S(2)}, u32[]{:S(2)}) collective-permute-start(f32[304,128]{1,0:T(8,128)S(1)} %collective-permute-done.4.above), channel_id=1, source_target_pairs={{0,4},{4,0},{8,12},{12,8},{16,20},{20,16},{24,28},{28,24},{1,5},{5... | collective-permute-start | bytes 466952 | tf_op jit(solution)/shard_map/ppermute | solution.py:166
  17.9 1.9 %collective-permute-start.8 = (f32[304,128]{1,0:T(8,128)S(1)}, f32[304,128]{1,0:T(8,128)S(1)}, u32[]{:S(2)}, u32[]{:S(2)}) collective-permute-start(f32[304,128]{1,0:T(8,128)S(1)} %collective-permute-done.7.below), channel_id=1, source_target_pairs={{0,4},{4,0},{8,12},{12,8},{16,20},{20,16},{24,28},{28,24},{1,5},{5... | collective-permute-start | bytes 466952 | tf_op jit(solution)/shard_map/ppermute | solution.py:165

commit v8 on v7

--- a/solution.py
+++ b/solution.py
@@ -33,12 +33,9 @@
     for array, distance, _ in side_entries():
         key = (array, distance)
         ends = y_rows(distance, array)
-        if array != 1 and distance == 1:
-            put(0, first, key, 0, cells_y)
-        else:
-            put(0, first, key, 0, ends)
-            put(0, first, key, cells_y - ends, ends)
-            put(1, second, key, ends, cells_y - 2 * ends)
+        put(0, first, key, 0, ends)
+        put(0, first, key, cells_y - ends, ends)
+        put(1, second, key, ends, cells_y - 2 * ends)
     return first, second, [-(-length // 8) * 8 for length in lengths]
 
 
@@ -110,7 +107,7 @@
     for_member(body)
 
 
-def pack_kernel(block, received, to_up, to_down, far):
+def pack_kernel(block, received, to_up, to_down):
     cells_x, cells_y = block.shape[0] // 3, block.shape[1]
     own = views(block, cells_x)
     plan = x_plan(cells_y)[0]
@@ -124,8 +121,14 @@
     for side, array, index, rows, start in y_plan(cells_x)[0]:
         to_up[pl.ds(start, rows), :] = piece(side, array, index, rows, cells_y - rows)
         to_down[pl.ds(start, rows), :] = piece(side, array, index, rows, 0)
-    far[0] = piece("away", 0, 1, cells_y, 0)
-    far[1] = piece("away", 2, 1, cells_y, 0)
+
+
+def far_kernel(received, rest, far):
+    plans = x_plan(far.shape[1])
+    for place, array in ((0, 0), (1, 2)):
+        for plan, ref in zip(plans, (received, rest)):
+            for row, rows, start in plan[array, 1]:
+                far[place, pl.ds(row, rows), :] = ref[pl.ds(start, rows), :]
 
 
 def stacked(pressure, source, coefficient):
@@ -154,13 +157,14 @@
     received = lax.ppermute(first, "gx", x_pairs())
     length = y_plan(cells_x)[1]
     planes = jax.ShapeDtypeStruct((2, cells_y, depth), jnp.float32)
-    to_up, to_down, outermost = pl.pallas_call(
-        pack_kernel, out_shape=[packed(length), packed(length), planes], compiler_params=params, name="pack_halo"
+    to_up, to_down = pl.pallas_call(
+        pack_kernel, out_shape=[packed(length), packed(length)], compiler_params=params, name="pack_halo"
     )(block, received)
     below = lax.ppermute(to_up, "gy", shifts("gy", 1))
     above = lax.ppermute(to_down, "gy", shifts("gy", -1))
+    rest = lax.ppermute(second, "gx", x_pairs())
+    outermost = pl.pallas_call(far_kernel, out_shape=planes, compiler_params=params, name="far_planes")(received, rest)
     far = lax.ppermute(outermost, "gx", swap_pairs())
-    rest = lax.ppermute(second, "gx", x_pairs())
     above, far, rest = lax.optimization_barrier((above, far, rest))
     p_below = lax.ppermute(below, "gx", swap_pairs())
     p_above = lax.ppermute(above, "gx", swap_pairs())

time: 42.1 us -> 41.9 us (level)
  no operation moved by 1% of the time
where the time goes in v8:
time: 41.9 us; the launch traced here: 41.7 us
  blocking collectives  16.4 us (39%)
  starting transfers between devices  16.3 us (39%)
  Pallas kernels  5.82 us (14%)
  waiting for transfers between devices  1.97 us (5%)
  other arithmetic  1.12 us (3%)
    all_to_all x1, blocking collectives, correct_whole(): gathered = lax.all_to_all(tiles, ('gx', 'gy'), 0, 0, tiled=False)  16.4 us
    ppermute x1, starting transfers between devices, fine_halo(): far = lax.ppermute(outermost, 'gx', swap_pairs())  6.24 us
    ppermute x1, starting transfers between devices, fine_halo(): below = lax.ppermute(to_up, 'gy', shifts('gy', 1))  5.44 us
    pallas_call x1, Pallas kernels, smooth(): pl.pallas_call(smooth_kernel, out_shape=(jax.ShapeDtypeStruct((cells_x, c...  3.21 us
    pallas_call x1, Pallas kernels, correct_whole(): pl.pallas_call(functools.partial(correct_kernel, grid), out_shape=jax.Sha...  2.52 us
    ppermute x1, starting transfers between devices, fine_halo(): above = lax.ppermute(to_down, 'gy', shifts('gy', -1))  1.29 us
    mul x1, other arithmetic, stacked(): block * jnp.where((plane >= cells_x) & (plane < 2 * cells_x), 2.0, 1.0)  1.12 us
    ppermute x3, starting transfers between devices, fine_halo(): partner = tuple((lax.ppermute(v, 'gx', swap_pairs()) for v in own))  0.96 us
  transfers between devices with their start and end apart: 10, of which 4 were waited for; matrix products, arithmetic and copies ran while one was open for 3% of the time, Pallas kernels for 0%

profile of v8, /device:TPU:0, one launch (start us, length us, event | category | flops | bytes accessed | tf_op | source)
XLA Modules:
  0.0 41.7 jit_solution(9573048234445765492)
XLA Ops:
  0.0 0.5 %collective-permute-start = (f32[8,32,128]{2,1,0:T(8,128)}, f32[8,32,128]{2,1,0:T(8,128)S(1)}, u32[]{:S(2)}, u32[]{:S(2)}) collective-permute-start(f32[8,32,128]{2,1,0:T(8,128)} %param.3), channel_id=1, source_target_pairs={{0,4},{4,0},{8,12},{12,8},{16,20},{20,16},{24,28},{28,24},{1,5},{5... | collective-permute-start | bytes 393224 | tf_op jit(solution)/shard_map/ppermute | solution.py:152
  0.5 0.1 collective-permute-start.1
  0.5 0.5 %collective-permute-start.2 = (f32[8,32,128]{2,1,0:T(8,128)}, f32[8,32,128]{2,1,0:T(8,128)S(1)}, u32[]{:S(2)}, u32[]{:S(2)}) collective-permute-start(f32[8,32,128]{2,1,0:T(8,128)} %param.5), channel_id=1, source_target_pairs={{0,4},{4,0},{8,12},{12,8},{16,20},{20,16},{24,28},{28,24},{1,5},{5... | collective-permute-start | bytes 393224 | tf_op jit(solution)/shard_map/ppermute | solution.py:152
  1.0 1.1 %maximum_multiply_fusion.block = f32[24,32,128]{2,1,0:T(8,128)S(1)} fusion(f32[8,32,128]{2,1,0:T(8,128)} %param.5, f32[8,32,128]{2,1,0:T(8,128)} %param.4, f32[8,32,128]{2,1,0:T(8,128)} %param.3, f32[24]{0:T(128)S(1)} %and_select_fusion), kind=kLoop, calls=%fused_computation | loop fusion | flops 294912 | bytes 786528 | tf_op jit(solution)/shard_map/mul | solution.py:138
  2.1 0.0 collective-permute-done.pp
  2.1 0.0 collective-permute-done.1.pf
  2.1 0.1 collective-permute-done.2.pk
  2.3 0.7 %collective-permute-start.3 = (f32[256,128]{1,0:T(8,128)S(1)}, f32[256,128]{1,0:T(8,128)S(1)}, u32[]{:S(2)}, u32[]{:S(2)}) collective-permute-start(f32[256,128]{1,0:T(8,128)S(1)} %get-tuple-element.15), channel_id=1, source_target_pairs={{4,8},{12,16},{20,24},{8,4},{16,12},{24,20},{5,9},{13,17},{21,25},... | collective-permute-start | bytes 393224 | tf_op jit(solution)/shard_map/ppermute | solution.py:157
  2.9 0.7 %collective-permute-start.5 = (f32[456,128]{1,0:T(8,128)S(1)}, f32[456,128]{1,0:T(8,128)S(1)}, u32[]{:S(2)}, u32[]{:S(2)}) collective-permute-start(f32[456,128]{1,0:T(8,128)S(1)} %get-tuple-element.17), channel_id=1, source_target_pairs={{4,8},{12,16},{20,24},{8,4},{16,12},{24,20},{5,9},{13,17},{21,25},... | collective-permute-start | bytes 700424 | tf_op jit(solution)/shard_map/ppermute | solution.py:165
  3.6 0.0 collective-permute-done.3.received
  3.7 1.3 %collective-permute-start.4 = (f32[304,128]{1,0:T(8,128)S(1)}, f32[304,128]{1,0:T(8,128)S(1)}, u32[]{:S(2)}, u32[]{:S(2)}) collective-permute-start(f32[304,128]{1,0:T(8,128)S(1)} %get-tuple-element.16), channel_id=1, source_target_pairs={{1,0},{2,1},{3,2},{5,4},{6,5},{7,6},{9,8},{10,9},{11,10},{13,12},{... | collective-permute-start | bytes 466952 | tf_op jit(solution)/shard_map/ppermute | solution.py:164
  5.0 5.4 %collective-permute-start.7 = (f32[304,128]{1,0:T(8,128)S(1)}, f32[304,128]{1,0:T(8,128)S(1)}, u32[]{:S(2)}, u32[]{:S(2)}) collective-permute-start(f32[304,128]{1,0:T(8,128)S(1)} %get-tuple-element.20), channel_id=1, source_target_pairs={{0,1},{1,2},{2,3},{4,5},{5,6},{6,7},{8,9},{9,10},{10,11},{12,13},{... | collective-permute-start | bytes 466952 | tf_op jit(solution)/shard_map/ppermute | solution.py:163
  10.4 0.0 collective-permute-done.5.rest
  10.4 6.2 %collective-permute-start.6 = (f32[2,32,128]{2,1,0:T(8,128)S(1)}, f32[2,32,128]{2,1,0:T(8,128)S(1)}, u32[]{:S(2)}, u32[]{:S(2)}) collective-permute-start(f32[2,32,128]{2,1,0:T(8,128)S(1)} %far_planes.1), channel_id=1, source_target_pairs={{0,4},{4,0},{8,12},{12,8},{16,20},{20,16},{24,28},{28,24},{1,5},{5... | collective-permute-start | bytes 98312 | tf_op jit(solution)/shard_map/ppermute | solution.py:167
  16.7 0.9 %collective-permute-done.6.far = f32[2,32,128]{2,1,0:T(8,128)S(1)} collective-permute-done((f32[2,32,128]{2,1,0:T(8,128)S(1)}, f32[2,32,128]{2,1,0:T(8,128)S(1)}, u32[]{:S(2)}, u32[]{:S(2)}) %collective-permute-start.6) | collective-permute-done | bytes 32800 | tf_op jit(solution)/shard_map/ppermute | solution.py:167
  17.5 0.0 collective-permute-done.4.above
  17.5 0.3 collective-permute-start.9
  17.9 0.0 collective-permute-done.7.below
  17.9 0.6 %collective-permute-start.8 = (f32[304,128]{1,0:T(8,128)S(1)}, f32[304,128]{1,0:T(8,128)S(1)}, u32[]{:S(2)}, u32[]{:S(2)}) collective-permute-start(f32[304,128]{1,0:T(8,128)S(1)} %collective-permute-done.7.below), channel_id=1, source_target_pairs={{0,4},{4,0},{8,12},{12,8},{16,20},{20,16},{24,28},{28,24},{1,5},{5... | collective-permute-start | bytes 466952 | tf_op jit(solution)/shard_map/ppermute | solution.py:169
  18.5 0.4 collective-permute-done.9.p_above
  18.9 0.6 %collective-permute-done.8.p_below = f32[304,128]{1,0:T(8,128)S(1)} collective-permute-done((f32[304,128]{1,0:T(8,128)S(1)}, f32[304,128]{1,0:T(8,128)S(1)}, u32[]{:S(2)}, u32[]{:S(2)}) %collective-permute-start.8) | collective-permute-done | bytes 155680 | tf_op jit(solution)/shard_map/ppermute | solution.py:169
  19.6 3.2 %smooth.1 = (f32[8,32,128]{2,1,0:T(8,128)S(1)}, f32[6,48,128]{2,1,0:T(8,128)S(1)}, f32[32,8,128]{2,1,0:T(8,128)S(1)}) custom-call(f32[24,32,128]{2,1,0:T(8,128)S(1)} %maximum_multiply_fusion.block, f32[8,32,128]{2,1,0:T(8,128)S(1)} %collective-permute-done.pp, f32[8,32,128]{2,1,0:T(8,128)S(1)} %collective-permute-done.1.pf, ...), custom_call_target="tpu_custom_call" | custom-call | tf_op jit(solution)/shard_map/smooth/pallas_call | solution.py:410
  22.8 16.4 %all_to_all.5.gathered = f32[32,8,128]{2,1,0:T(8,128)S(1)} all-to-all(f32[32,8,128]{2,1,0:T(8,128)S(1)} %get-tuple-element.22), channel_id=1, replica_groups=mesh['gx'=8,'gy'=4] {'gx','gy'}, dimensions={0} | all-to-all | bytes 262144 | tf_op jit(solution)/shard_map/all_to_all | solution.py:677
  39.2 2.5 %correct.1 = f32[8,32,128]{2,1,0:T(8,128)} custom-call(f32[32,8,128]{2,1,0:T(8,128)S(1)} %all_to_all.5.gathered, f32[8,32,128]{2,1,0:T(8,128)S(1)} %get-tuple-element.23.smoothed, f32[6,48,128]{2,1,0:T(8,128)S(1)} %get-tuple-element.24.error_one), custom_call_target="tpu_custom_call" | custom-call | tf_op jit(solution)/shard_map/correct/pallas_call | solution.py:679
  (4 shorter events, 0.1 us)
Async XLA Ops:
  0.0 2.1 %collective-permute-start = (f32[8,32,128]{2,1,0:T(8,128)}, f32[8,32,128]{2,1,0:T(8,128)S(1)}, u32[]{:S(2)}, u32[]{:S(2)}) collective-permute-start(f32[8,32,128]{2,1,0:T(8,128)} %param.3), channel_id=1, source_target_pairs={{0,4},{4,0},{8,12},{12,8},{16,20},{20,16},{24,28},{28,24},{1,5},{5... | collective-permute-start | bytes 393224 | tf_op jit(solution)/shard_map/ppermute | solution.py:152
  0.5 1.7 %collective-permute-start.1 = (f32[8,32,128]{2,1,0:T(8,128)}, f32[8,32,128]{2,1,0:T(8,128)S(1)}, u32[]{:S(2)}, u32[]{:S(2)}) collective-permute-start(f32[8,32,128]{2,1,0:T(8,128)} %param.4), channel_id=1, source_target_pairs={{0,4},{4,0},{8,12},{12,8},{16,20},{20,16},{24,28},{28,24},{1,5},{5... | collective-permute-start | bytes 393224 | tf_op jit(solution)/shard_map/ppermute | solution.py:152
  0.5 1.7 %collective-permute-start.2 = (f32[8,32,128]{2,1,0:T(8,128)}, f32[8,32,128]{2,1,0:T(8,128)S(1)}, u32[]{:S(2)}, u32[]{:S(2)}) collective-permute-start(f32[8,32,128]{2,1,0:T(8,128)} %param.5), channel_id=1, source_target_pairs={{0,4},{4,0},{8,12},{12,8},{16,20},{20,16},{24,28},{28,24},{1,5},{5... | collective-permute-start | bytes 393224 | tf_op jit(solution)/shard_map/ppermute | solution.py:152
  2.3 1.4 %collective-permute-start.3 = (f32[256,128]{1,0:T(8,128)S(1)}, f32[256,128]{1,0:T(8,128)S(1)}, u32[]{:S(2)}, u32[]{:S(2)}) collective-permute-start(f32[256,128]{1,0:T(8,128)S(1)} %get-tuple-element.15), channel_id=1, source_target_pairs={{4,8},{12,16},{20,24},{8,4},{16,12},{24,20},{5,9},{13,17},{21,25},... | collective-permute-start | bytes 393224 | tf_op jit(solution)/shard_map/ppermute | solution.py:157
  2.9 7.5 %collective-permute-start.5 = (f32[456,128]{1,0:T(8,128)S(1)}, f32[456,128]{1,0:T(8,128)S(1)}, u32[]{:S(2)}, u32[]{:S(2)}) collective-permute-start(f32[456,128]{1,0:T(8,128)S(1)} %get-tuple-element.17), channel_id=1, source_target_pairs={{4,8},{12,16},{20,24},{8,4},{16,12},{24,20},{5,9},{13,17},{21,25},... | collective-permute-start | bytes 700424 | tf_op jit(solution)/shard_map/ppermute | solution.py:165
  3.7 13.9 %collective-permute-start.4 = (f32[304,128]{1,0:T(8,128)S(1)}, f32[304,128]{1,0:T(8,128)S(1)}, u32[]{:S(2)}, u32[]{:S(2)}) collective-permute-start(f32[304,128]{1,0:T(8,128)S(1)} %get-tuple-element.16), channel_id=1, source_target_pairs={{1,0},{2,1},{3,2},{5,4},{6,5},{7,6},{9,8},{10,9},{11,10},{13,12},{... | collective-permute-start | bytes 466952 | tf_op jit(solution)/shard_map/ppermute | solution.py:164
  5.0 12.9 %collective-permute-start.7 = (f32[304,128]{1,0:T(8,128)S(1)}, f32[304,128]{1,0:T(8,128)S(1)}, u32[]{:S(2)}, u32[]{:S(2)}) collective-permute-start(f32[304,128]{1,0:T(8,128)S(1)} %get-tuple-element.20), channel_id=1, source_target_pairs={{0,1},{1,2},{2,3},{4,5},{5,6},{6,7},{8,9},{9,10},{10,11},{12,13},{... | collective-permute-start | bytes 466952 | tf_op jit(solution)/shard_map/ppermute | solution.py:163
  10.4 7.1 %collective-permute-start.6 = (f32[2,32,128]{2,1,0:T(8,128)S(1)}, f32[2,32,128]{2,1,0:T(8,128)S(1)}, u32[]{:S(2)}, u32[]{:S(2)}) collective-permute-start(f32[2,32,128]{2,1,0:T(8,128)S(1)} %far_planes.1), channel_id=1, source_target_pairs={{0,4},{4,0},{8,12},{12,8},{16,20},{20,16},{24,28},{28,24},{1,5},{5... | collective-permute-start | bytes 98312 | tf_op jit(solution)/shard_map/ppermute | solution.py:167
  17.5 1.4 %collective-permute-start.9 = (f32[304,128]{1,0:T(8,128)S(1)}, f32[304,128]{1,0:T(8,128)S(1)}, u32[]{:S(2)}, u32[]{:S(2)}) collective-permute-start(f32[304,128]{1,0:T(8,128)S(1)} %collective-permute-done.4.above), channel_id=1, source_target_pairs={{0,4},{4,0},{8,12},{12,8},{16,20},{20,16},{24,28},{28,24},{1,5},{5... | collective-permute-start | bytes 466952 | tf_op jit(solution)/shard_map/ppermute | solution.py:170
  17.9 1.7 %collective-permute-start.8 = (f32[304,128]{1,0:T(8,128)S(1)}, f32[304,128]{1,0:T(8,128)S(1)}, u32[]{:S(2)}, u32[]{:S(2)}) collective-permute-start(f32[304,128]{1,0:T(8,128)S(1)} %collective-permute-done.7.below), channel_id=1, source_target_pairs={{0,4},{4,0},{8,12},{12,8},{16,20},{20,16},{24,28},{28,24},{1,5},{5... | collective-permute-start | bytes 466952 | tf_op jit(solution)/shard_map/ppermute | solution.py:169

commit v9 on v8

--- a/solution.py
+++ b/solution.py
@@ -536,28 +536,35 @@
             places3.before_y(v, 2), places3.after_y(v, 2), ring(v, 8, 2), ring(v, -8, 2),
         )
 
-    direction, sides = remain, around(remain)
-    remain_sides = sides
+    def apply(v, sides):
+        coupled = weights3[0] * before_x(v) + weights3[1] * after_x(v)
+        coupled += weights3[2] * sides[0] + weights3[3] * sides[1]
+        coupled += weights3[4] * sides[2] + weights3[5] * sides[3]
+        return (diagonal3 * v - coupled) * (1.0 / 128.0)
+
+    remain_sides = around(remain)
+    direction, sides = remain, remain_sides
+    image = apply(remain, remain_sides)
+    image_sides = around(image)
     norm_now = total(remain * remain)
     error = error_before = error_after = jnp.zeros_like(remain)
     for repeat in range(CSWEEPS):
-        coupled = weights3[0] * before_x(direction) + weights3[1] * after_x(direction)
-        coupled += weights3[2] * sides[0] + weights3[3] * sides[1]
-        coupled += weights3[4] * sides[2] + weights3[5] * sides[3]
-        image = (diagonal3 * direction - coupled) * (1.0 / 128.0)
         alpha = norm_now / total(direction * image)
         error = error + alpha * direction
         error_before = error_before + alpha * sides[0]
         error_after = error_after + alpha * sides[1]
         if repeat == CSWEEPS - 1:
             break
-        image_sides = around(image)
         remain = remain - alpha * image
         remain_sides = [r - alpha * q for r, q in zip(remain_sides, image_sides)]
+        applied = apply(remain, remain_sides)
+        applied_sides = around(applied)
         norm_next = total(remain * remain)
         beta = norm_next / norm_now
         direction = remain + beta * direction
         sides = [r + beta * p for r, p in zip(remain_sides, sides)]
+        image = applied + beta * image
+        image_sides = [w + beta * q for w, q in zip(applied_sides, image_sides)]
         norm_now = norm_next
 
     near = jnp.where(

time: 41.9 us -> 41.8 us (level)
  no operation moved by 1% of the time
where the time goes in v9:
time: 41.8 us; the launch traced here: 41.6 us
  blocking collectives  16.4 us (39%)
  starting transfers between devices  16.3 us (39%)
  Pallas kernels  5.77 us (14%)
  waiting for transfers between devices  1.97 us (5%)
  other arithmetic  1.12 us (3%)
    all_to_all x1, blocking collectives, correct_whole(): gathered = lax.all_to_all(tiles, ('gx', 'gy'), 0, 0, tiled=False)  16.4 us
    ppermute x1, starting transfers between devices, fine_halo(): far = lax.ppermute(outermost, 'gx', swap_pairs())  6.24 us
    ppermute x1, starting transfers between devices, fine_halo(): below = lax.ppermute(to_up, 'gy', shifts('gy', 1))  5.44 us
    pallas_call x1, Pallas kernels, smooth(): pl.pallas_call(smooth_kernel, out_shape=(jax.ShapeDtypeStruct((cells_x, c...  3.21 us
    pallas_call x1, Pallas kernels, correct_whole(): pl.pallas_call(functools.partial(correct_kernel, grid), out_shape=jax.Sha...  2.47 us
    ppermute x1, starting transfers between devices, fine_halo(): above = lax.ppermute(to_down, 'gy', shifts('gy', -1))  1.29 us
    mul x1, other arithmetic, stacked(): block * jnp.where((plane >= cells_x) & (plane < 2 * cells_x), 2.0, 1.0)  1.12 us
    ppermute x3, starting transfers between devices, fine_halo(): partner = tuple((lax.ppermute(v, 'gx', swap_pairs()) for v in own))  0.96 us
  transfers between devices with their start and end apart: 10, of which 4 were waited for; matrix products, arithmetic and copies ran while one was open for 3% of the time, Pallas kernels for 0%

profile of v9, /device:TPU:0, one launch (start us, length us, event | category | flops | bytes accessed | tf_op | source)
XLA Modules:
  0.0 41.6 jit_solution(11444403753727789882)
XLA Ops:
  0.0 0.5 %collective-permute-start = (f32[8,32,128]{2,1,0:T(8,128)}, f32[8,32,128]{2,1,0:T(8,128)S(1)}, u32[]{:S(2)}, u32[]{:S(2)}) collective-permute-start(f32[8,32,128]{2,1,0:T(8,128)} %param.3), channel_id=1, source_target_pairs={{0,4},{4,0},{8,12},{12,8},{16,20},{20,16},{24,28},{28,24},{1,5},{5... | collective-permute-start | bytes 393224 | tf_op jit(solution)/shard_map/ppermute | solution.py:152
  0.5 0.1 collective-permute-start.1
  0.5 0.5 %collective-permute-start.2 = (f32[8,32,128]{2,1,0:T(8,128)}, f32[8,32,128]{2,1,0:T(8,128)S(1)}, u32[]{:S(2)}, u32[]{:S(2)}) collective-permute-start(f32[8,32,128]{2,1,0:T(8,128)} %param.5), channel_id=1, source_target_pairs={{0,4},{4,0},{8,12},{12,8},{16,20},{20,16},{24,28},{28,24},{1,5},{5... | collective-permute-start | bytes 393224 | tf_op jit(solution)/shard_map/ppermute | solution.py:152
  1.0 1.1 %maximum_multiply_fusion.block = f32[24,32,128]{2,1,0:T(8,128)S(1)} fusion(f32[8,32,128]{2,1,0:T(8,128)} %param.5, f32[8,32,128]{2,1,0:T(8,128)} %param.4, f32[8,32,128]{2,1,0:T(8,128)} %param.3, f32[24]{0:T(128)S(1)} %and_select_fusion), kind=kLoop, calls=%fused_computation | loop fusion | flops 294912 | bytes 786528 | tf_op jit(solution)/shard_map/mul | solution.py:138
  2.1 0.0 collective-permute-done.pp
  2.1 0.0 collective-permute-done.1.pf
  2.1 0.1 collective-permute-done.2.pk
  2.3 0.7 %collective-permute-start.3 = (f32[256,128]{1,0:T(8,128)S(1)}, f32[256,128]{1,0:T(8,128)S(1)}, u32[]{:S(2)}, u32[]{:S(2)}) collective-permute-start(f32[256,128]{1,0:T(8,128)S(1)} %get-tuple-element.15), channel_id=1, source_target_pairs={{4,8},{12,16},{20,24},{8,4},{16,12},{24,20},{5,9},{13,17},{21,25},... | collective-permute-start | bytes 393224 | tf_op jit(solution)/shard_map/ppermute | solution.py:157
  2.9 0.7 %collective-permute-start.5 = (f32[456,128]{1,0:T(8,128)S(1)}, f32[456,128]{1,0:T(8,128)S(1)}, u32[]{:S(2)}, u32[]{:S(2)}) collective-permute-start(f32[456,128]{1,0:T(8,128)S(1)} %get-tuple-element.17), channel_id=1, source_target_pairs={{4,8},{12,16},{20,24},{8,4},{16,12},{24,20},{5,9},{13,17},{21,25},... | collective-permute-start | bytes 700424 | tf_op jit(solution)/shard_map/ppermute | solution.py:165
  3.6 0.0 collective-permute-done.3.received
  3.7 1.3 %collective-permute-start.4 = (f32[304,128]{1,0:T(8,128)S(1)}, f32[304,128]{1,0:T(8,128)S(1)}, u32[]{:S(2)}, u32[]{:S(2)}) collective-permute-start(f32[304,128]{1,0:T(8,128)S(1)} %get-tuple-element.16), channel_id=1, source_target_pairs={{1,0},{2,1},{3,2},{5,4},{6,5},{7,6},{9,8},{10,9},{11,10},{13,12},{... | collective-permute-start | bytes 466952 | tf_op jit(solution)/shard_map/ppermute | solution.py:164
  5.0 5.4 %collective-permute-start.7 = (f32[304,128]{1,0:T(8,128)S(1)}, f32[304,128]{1,0:T(8,128)S(1)}, u32[]{:S(2)}, u32[]{:S(2)}) collective-permute-start(f32[304,128]{1,0:T(8,128)S(1)} %get-tuple-element.20), channel_id=1, source_target_pairs={{0,1},{1,2},{2,3},{4,5},{5,6},{6,7},{8,9},{9,10},{10,11},{12,13},{... | collective-permute-start | bytes 466952 | tf_op jit(solution)/shard_map/ppermute | solution.py:163
  10.4 0.0 collective-permute-done.5.rest
  10.4 6.2 %collective-permute-start.6 = (f32[2,32,128]{2,1,0:T(8,128)S(1)}, f32[2,32,128]{2,1,0:T(8,128)S(1)}, u32[]{:S(2)}, u32[]{:S(2)}) collective-permute-start(f32[2,32,128]{2,1,0:T(8,128)S(1)} %far_planes.1), channel_id=1, source_target_pairs={{0,4},{4,0},{8,12},{12,8},{16,20},{20,16},{24,28},{28,24},{1,5},{5... | collective-permute-start | bytes 98312 | tf_op jit(solution)/shard_map/ppermute | solution.py:167
  16.7 0.9 %collective-permute-done.6.far = f32[2,32,128]{2,1,0:T(8,128)S(1)} collective-permute-done((f32[2,32,128]{2,1,0:T(8,128)S(1)}, f32[2,32,128]{2,1,0:T(8,128)S(1)}, u32[]{:S(2)}, u32[]{:S(2)}) %collective-permute-start.6) | collective-permute-done | bytes 32800 | tf_op jit(solution)/shard_map/ppermute | solution.py:167
  17.5 0.0 collective-permute-done.4.above
  17.5 0.3 collective-permute-start.9
  17.9 0.0 collective-permute-done.7.below
  17.9 0.6 %collective-permute-start.8 = (f32[304,128]{1,0:T(8,128)S(1)}, f32[304,128]{1,0:T(8,128)S(1)}, u32[]{:S(2)}, u32[]{:S(2)}) collective-permute-start(f32[304,128]{1,0:T(8,128)S(1)} %collective-permute-done.7.below), channel_id=1, source_target_pairs={{0,4},{4,0},{8,12},{12,8},{16,20},{20,16},{24,28},{28,24},{1,5},{5... | collective-permute-start | bytes 466952 | tf_op jit(solution)/shard_map/ppermute | solution.py:169
  18.5 0.4 collective-permute-done.9.p_above
  18.9 0.6 %collective-permute-done.8.p_below = f32[304,128]{1,0:T(8,128)S(1)} collective-permute-done((f32[304,128]{1,0:T(8,128)S(1)}, f32[304,128]{1,0:T(8,128)S(1)}, u32[]{:S(2)}, u32[]{:S(2)}) %collective-permute-start.8) | collective-permute-done | bytes 155680 | tf_op jit(solution)/shard_map/ppermute | solution.py:169
  19.6 3.2 %smooth.1 = (f32[8,32,128]{2,1,0:T(8,128)S(1)}, f32[6,48,128]{2,1,0:T(8,128)S(1)}, f32[32,8,128]{2,1,0:T(8,128)S(1)}) custom-call(f32[24,32,128]{2,1,0:T(8,128)S(1)} %maximum_multiply_fusion.block, f32[8,32,128]{2,1,0:T(8,128)S(1)} %collective-permute-done.pp, f32[8,32,128]{2,1,0:T(8,128)S(1)} %collective-permute-done.1.pf, ...), custom_call_target="tpu_custom_call" | custom-call | tf_op jit(solution)/shard_map/smooth/pallas_call | solution.py:410
  22.8 16.4 %all_to_all.5.gathered = f32[32,8,128]{2,1,0:T(8,128)S(1)} all-to-all(f32[32,8,128]{2,1,0:T(8,128)S(1)} %get-tuple-element.22), channel_id=1, replica_groups=mesh['gx'=8,'gy'=4] {'gx','gy'}, dimensions={0} | all-to-all | bytes 262144 | tf_op jit(solution)/shard_map/all_to_all | solution.py:684
  39.2 2.5 %correct.1 = f32[8,32,128]{2,1,0:T(8,128)} custom-call(f32[32,8,128]{2,1,0:T(8,128)S(1)} %all_to_all.5.gathered, f32[8,32,128]{2,1,0:T(8,128)S(1)} %get-tuple-element.23.smoothed, f32[6,48,128]{2,1,0:T(8,128)S(1)} %get-tuple-element.24.error_one), custom_call_target="tpu_custom_call" | custom-call | tf_op jit(solution)/shard_map/correct/pallas_call | solution.py:686
  (4 shorter events, 0.1 us)
Async XLA Ops:
  0.0 2.1 %collective-permute-start = (f32[8,32,128]{2,1,0:T(8,128)}, f32[8,32,128]{2,1,0:T(8,128)S(1)}, u32[]{:S(2)}, u32[]{:S(2)}) collective-permute-start(f32[8,32,128]{2,1,0:T(8,128)} %param.3), channel_id=1, source_target_pairs={{0,4},{4,0},{8,12},{12,8},{16,20},{20,16},{24,28},{28,24},{1,5},{5... | collective-permute-start | bytes 393224 | tf_op jit(solution)/shard_map/ppermute | solution.py:152
  0.5 1.7 %collective-permute-start.1 = (f32[8,32,128]{2,1,0:T(8,128)}, f32[8,32,128]{2,1,0:T(8,128)S(1)}, u32[]{:S(2)}, u32[]{:S(2)}) collective-permute-start(f32[8,32,128]{2,1,0:T(8,128)} %param.4), channel_id=1, source_target_pairs={{0,4},{4,0},{8,12},{12,8},{16,20},{20,16},{24,28},{28,24},{1,5},{5... | collective-permute-start | bytes 393224 | tf_op jit(solution)/shard_map/ppermute | solution.py:152
  0.5 1.7 %collective-permute-start.2 = (f32[8,32,128]{2,1,0:T(8,128)}, f32[8,32,128]{2,1,0:T(8,128)S(1)}, u32[]{:S(2)}, u32[]{:S(2)}) collective-permute-start(f32[8,32,128]{2,1,0:T(8,128)} %param.5), channel_id=1, source_target_pairs={{0,4},{4,0},{8,12},{12,8},{16,20},{20,16},{24,28},{28,24},{1,5},{5... | collective-permute-start | bytes 393224 | tf_op jit(solution)/shard_map/ppermute | solution.py:152
  2.3 1.4 %collective-permute-start.3 = (f32[256,128]{1,0:T(8,128)S(1)}, f32[256,128]{1,0:T(8,128)S(1)}, u32[]{:S(2)}, u32[]{:S(2)}) collective-permute-start(f32[256,128]{1,0:T(8,128)S(1)} %get-tuple-element.15), channel_id=1, source_target_pairs={{4,8},{12,16},{20,24},{8,4},{16,12},{24,20},{5,9},{13,17},{21,25},... | collective-permute-start | bytes 393224 | tf_op jit(solution)/shard_map/ppermute | solution.py:157
  2.9 7.5 %collective-permute-start.5 = (f32[456,128]{1,0:T(8,128)S(1)}, f32[456,128]{1,0:T(8,128)S(1)}, u32[]{:S(2)}, u32[]{:S(2)}) collective-permute-start(f32[456,128]{1,0:T(8,128)S(1)} %get-tuple-element.17), channel_id=1, source_target_pairs={{4,8},{12,16},{20,24},{8,4},{16,12},{24,20},{5,9},{13,17},{21,25},... | collective-permute-start | bytes 700424 | tf_op jit(solution)/shard_map/ppermute | solution.py:165
  3.7 13.9 %collective-permute-start.4 = (f32[304,128]{1,0:T(8,128)S(1)}, f32[304,128]{1,0:T(8,128)S(1)}, u32[]{:S(2)}, u32[]{:S(2)}) collective-permute-start(f32[304,128]{1,0:T(8,128)S(1)} %get-tuple-element.16), channel_id=1, source_target_pairs={{1,0},{2,1},{3,2},{5,4},{6,5},{7,6},{9,8},{10,9},{11,10},{13,12},{... | collective-permute-start | bytes 466952 | tf_op jit(solution)/shard_map/ppermute | solution.py:164
  5.0 12.9 %collective-permute-start.7 = (f32[304,128]{1,0:T(8,128)S(1)}, f32[304,128]{1,0:T(8,128)S(1)}, u32[]{:S(2)}, u32[]{:S(2)}) collective-permute-start(f32[304,128]{1,0:T(8,128)S(1)} %get-tuple-element.20), channel_id=1, source_target_pairs={{0,1},{1,2},{2,3},{4,5},{5,6},{6,7},{8,9},{9,10},{10,11},{12,13},{... | collective-permute-start | bytes 466952 | tf_op jit(solution)/shard_map/ppermute | solution.py:163
  10.4 7.1 %collective-permute-start.6 = (f32[2,32,128]{2,1,0:T(8,128)S(1)}, f32[2,32,128]{2,1,0:T(8,128)S(1)}, u32[]{:S(2)}, u32[]{:S(2)}) collective-permute-start(f32[2,32,128]{2,1,0:T(8,128)S(1)} %far_planes.1), channel_id=1, source_target_pairs={{0,4},{4,0},{8,12},{12,8},{16,20},{20,16},{24,28},{28,24},{1,5},{5... | collective-permute-start | bytes 98312 | tf_op jit(solution)/shard_map/ppermute | solution.py:167
  17.5 1.4 %collective-permute-start.9 = (f32[304,128]{1,0:T(8,128)S(1)}, f32[304,128]{1,0:T(8,128)S(1)}, u32[]{:S(2)}, u32[]{:S(2)}) collective-permute-start(f32[304,128]{1,0:T(8,128)S(1)} %collective-permute-done.4.above), channel_id=1, source_target_pairs={{0,4},{4,0},{8,12},{12,8},{16,20},{20,16},{24,28},{28,24},{1,5},{5... | collective-permute-start | bytes 466952 | tf_op jit(solution)/shard_map/ppermute | solution.py:170
  17.9 1.7 %collective-permute-start.8 = (f32[304,128]{1,0:T(8,128)S(1)}, f32[304,128]{1,0:T(8,128)S(1)}, u32[]{:S(2)}, u32[]{:S(2)}) collective-permute-start(f32[304,128]{1,0:T(8,128)S(1)} %collective-permute-done.7.below), channel_id=1, source_target_pairs={{0,4},{4,0},{8,12},{12,8},{16,20},{20,16},{24,28},{28,24},{1,5},{5... | collective-permute-start | bytes 466952 | tf_op jit(solution)/shard_map/ppermute | solution.py:169

commit v10 on v9

--- a/solution.py
+++ b/solution.py
@@ -165,7 +165,8 @@
     rest = lax.ppermute(second, "gx", x_pairs())
     outermost = pl.pallas_call(far_kernel, out_shape=planes, compiler_params=params, name="far_planes")(received, rest)
     far = lax.ppermute(outermost, "gx", swap_pairs())
-    above, far, rest = lax.optimization_barrier((above, far, rest))
+    above, rest = lax.optimization_barrier((above, rest))
+    below, far = lax.optimization_barrier((below, far))
     p_below = lax.ppermute(below, "gx", swap_pairs())
     p_above = lax.ppermute(above, "gx", swap_pairs())
     return *partner, received, rest, far, below, above, p_below, p_above

time: 41.8 us -> 41.8 us (level)
  transfers between devices with their start and end apart: 10 -> 10, of which waited for: 4 -> 3; matrix products, arithmetic and copies ran while one was open for 3% -> 3% of each run, Pallas kernels for 0% -> 0%
where the time goes in v10:
time: 41.8 us; the launch traced here: 41.6 us
  starting transfers between devices  16.7 us (40%)
  blocking collectives  16.4 us (39%)
  Pallas kernels  5.77 us (14%)
  waiting for transfers between devices  1.59 us (4%)
  other arithmetic  1.12 us (3%)
    all_to_all x1, blocking collectives, correct_whole(): gathered = lax.all_to_all(tiles, ('gx', 'gy'), 0, 0, tiled=False)  16.4 us
    ppermute x1, starting transfers between devices, fine_halo(): far = lax.ppermute(outermost, 'gx', swap_pairs())  6.24 us
    ppermute x1, starting transfers between devices, fine_halo(): below = lax.ppermute(to_up, 'gy', shifts('gy', 1))  5.44 us
    pallas_call x1, Pallas kernels, smooth(): pl.pallas_call(smooth_kernel, out_shape=(jax.ShapeDtypeStruct((cells_x, c...  3.21 us
    pallas_call x1, Pallas kernels, correct_whole(): pl.pallas_call(functools.partial(correct_kernel, grid), out_shape=jax.Sha...  2.47 us
    ppermute x1, starting transfers between devices, fine_halo(): above = lax.ppermute(to_down, 'gy', shifts('gy', -1))  1.29 us
    mul x1, other arithmetic, stacked(): block * jnp.where((plane >= cells_x) & (plane < 2 * cells_x), 2.0, 1.0)  1.12 us
    ppermute x1, waiting for transfers between devices, fine_halo(): p_below = lax.ppermute(below, 'gx', swap_pairs())  1.01 us
  transfers between devices with their start and end apart: 10, of which 3 were waited for; matrix products, arithmetic and copies ran while one was open for 3% of the time, Pallas kernels for 0%

profile of v10, /device:TPU:0, one launch (start us, length us, event | category | flops | bytes accessed | tf_op | source)
XLA Modules:
  0.0 41.6 jit_solution(12069990581152830990)
XLA Ops:
  0.0 0.5 %collective-permute-start = (f32[8,32,128]{2,1,0:T(8,128)}, f32[8,32,128]{2,1,0:T(8,128)S(1)}, u32[]{:S(2)}, u32[]{:S(2)}) collective-permute-start(f32[8,32,128]{2,1,0:T(8,128)} %param.3), channel_id=1, source_target_pairs={{0,4},{4,0},{8,12},{12,8},{16,20},{20,16},{24,28},{28,24},{1,5},{5... | collective-permute-start | bytes 393224 | tf_op jit(solution)/shard_map/ppermute | solution.py:152
  0.5 0.1 collective-permute-start.1
  0.5 0.5 %collective-permute-start.2 = (f32[8,32,128]{2,1,0:T(8,128)}, f32[8,32,128]{2,1,0:T(8,128)S(1)}, u32[]{:S(2)}, u32[]{:S(2)}) collective-permute-start(f32[8,32,128]{2,1,0:T(8,128)} %param.5), channel_id=1, source_target_pairs={{0,4},{4,0},{8,12},{12,8},{16,20},{20,16},{24,28},{28,24},{1,5},{5... | collective-permute-start | bytes 393224 | tf_op jit(solution)/shard_map/ppermute | solution.py:152
  1.0 1.1 %maximum_multiply_fusion.block = f32[24,32,128]{2,1,0:T(8,128)S(1)} fusion(f32[8,32,128]{2,1,0:T(8,128)} %param.5, f32[8,32,128]{2,1,0:T(8,128)} %param.4, f32[8,32,128]{2,1,0:T(8,128)} %param.3, f32[24]{0:T(128)S(1)} %and_select_fusion), kind=kLoop, calls=%fused_computation | loop fusion | flops 294912 | bytes 786528 | tf_op jit(solution)/shard_map/mul | solution.py:138
  2.1 0.0 collective-permute-done.pp
  2.1 0.0 collective-permute-done.1.pf
  2.1 0.1 collective-permute-done.2.pk
  2.3 0.7 %collective-permute-start.3 = (f32[256,128]{1,0:T(8,128)S(1)}, f32[256,128]{1,0:T(8,128)S(1)}, u32[]{:S(2)}, u32[]{:S(2)}) collective-permute-start(f32[256,128]{1,0:T(8,128)S(1)} %get-tuple-element.16), channel_id=1, source_target_pairs={{4,8},{12,16},{20,24},{8,4},{16,12},{24,20},{5,9},{13,17},{21,25},... | collective-permute-start | bytes 393224 | tf_op jit(solution)/shard_map/ppermute | solution.py:157
  2.9 0.7 %collective-permute-start.5 = (f32[456,128]{1,0:T(8,128)S(1)}, f32[456,128]{1,0:T(8,128)S(1)}, u32[]{:S(2)}, u32[]{:S(2)}) collective-permute-start(f32[456,128]{1,0:T(8,128)S(1)} %get-tuple-element.18), channel_id=1, source_target_pairs={{4,8},{12,16},{20,24},{8,4},{16,12},{24,20},{5,9},{13,17},{21,25},... | collective-permute-start | bytes 700424 | tf_op jit(solution)/shard_map/ppermute | solution.py:165
  3.6 0.0 collective-permute-done.3.received
  3.7 1.3 %collective-permute-start.4 = (f32[304,128]{1,0:T(8,128)S(1)}, f32[304,128]{1,0:T(8,128)S(1)}, u32[]{:S(2)}, u32[]{:S(2)}) collective-permute-start(f32[304,128]{1,0:T(8,128)S(1)} %get-tuple-element.17), channel_id=1, source_target_pairs={{1,0},{2,1},{3,2},{5,4},{6,5},{7,6},{9,8},{10,9},{11,10},{13,12},{... | collective-permute-start | bytes 466952 | tf_op jit(solution)/shard_map/ppermute | solution.py:164
  5.0 5.4 %collective-permute-start.6 = (f32[304,128]{1,0:T(8,128)S(1)}, f32[304,128]{1,0:T(8,128)S(1)}, u32[]{:S(2)}, u32[]{:S(2)}) collective-permute-start(f32[304,128]{1,0:T(8,128)S(1)} %get-tuple-element.20), channel_id=1, source_target_pairs={{0,1},{1,2},{2,3},{4,5},{5,6},{6,7},{8,9},{9,10},{10,11},{12,13},{... | collective-permute-start | bytes 466952 | tf_op jit(solution)/shard_map/ppermute | solution.py:163
  10.4 0.0 collective-permute-done.5.rest
  10.4 6.2 %collective-permute-start.7 = (f32[2,32,128]{2,1,0:T(8,128)S(1)}, f32[2,32,128]{2,1,0:T(8,128)S(1)}, u32[]{:S(2)}, u32[]{:S(2)}) collective-permute-start(f32[2,32,128]{2,1,0:T(8,128)S(1)} %far_planes.1), channel_id=1, source_target_pairs={{0,4},{4,0},{8,12},{12,8},{16,20},{20,16},{24,28},{28,24},{1,5},{5... | collective-permute-start | bytes 98312 | tf_op jit(solution)/shard_map/ppermute | solution.py:167
  16.7 0.0 collective-permute-done.4.above
  16.7 0.4 collective-permute-start.9
  17.1 0.5 %collective-permute-done.7.far = f32[2,32,128]{2,1,0:T(8,128)S(1)} collective-permute-done((f32[2,32,128]{2,1,0:T(8,128)S(1)}, f32[2,32,128]{2,1,0:T(8,128)S(1)}, u32[]{:S(2)}, u32[]{:S(2)}) %collective-permute-start.7) | collective-permute-done | bytes 32800 | tf_op jit(solution)/shard_map/ppermute | solution.py:167
  17.5 0.0 collective-permute-done.6.below
  17.5 1.0 %collective-permute-start.8 = (f32[304,128]{1,0:T(8,128)S(1)}, f32[304,128]{1,0:T(8,128)S(1)}, u32[]{:S(2)}, u32[]{:S(2)}) collective-permute-start(f32[304,128]{1,0:T(8,128)S(1)} %collective-permute-done.6.below), channel_id=1, source_target_pairs={{0,4},{4,0},{8,12},{12,8},{16,20},{20,16},{24,28},{28,24},{1,5},{5... | collective-permute-start | bytes 466952 | tf_op jit(solution)/shard_map/ppermute | solution.py:170
  18.5 0.0 collective-permute-done.9.p_above
  18.5 1.0 %collective-permute-done.8.p_below = f32[304,128]{1,0:T(8,128)S(1)} collective-permute-done((f32[304,128]{1,0:T(8,128)S(1)}, f32[304,128]{1,0:T(8,128)S(1)}, u32[]{:S(2)}, u32[]{:S(2)}) %collective-permute-start.8) | collective-permute-done | bytes 155680 | tf_op jit(solution)/shard_map/ppermute | solution.py:170
  19.6 3.2 %smooth.1 = (f32[8,32,128]{2,1,0:T(8,128)S(1)}, f32[6,48,128]{2,1,0:T(8,128)S(1)}, f32[32,8,128]{2,1,0:T(8,128)S(1)}) custom-call(f32[24,32,128]{2,1,0:T(8,128)S(1)} %maximum_multiply_fusion.block, f32[8,32,128]{2,1,0:T(8,128)S(1)} %collective-permute-done.pp, f32[8,32,128]{2,1,0:T(8,128)S(1)} %collective-permute-done.1.pf, ...), custom_call_target="tpu_custom_call" | custom-call | tf_op jit(solution)/shard_map/smooth/pallas_call | solution.py:411
  22.8 16.4 %all_to_all.5.gathered = f32[32,8,128]{2,1,0:T(8,128)S(1)} all-to-all(f32[32,8,128]{2,1,0:T(8,128)S(1)} %get-tuple-element.24), channel_id=1, replica_groups=mesh['gx'=8,'gy'=4] {'gx','gy'}, dimensions={0} | all-to-all | bytes 262144 | tf_op jit(solution)/shard_map/all_to_all | solution.py:685
  39.2 2.5 %correct.1 = f32[8,32,128]{2,1,0:T(8,128)} custom-call(f32[32,8,128]{2,1,0:T(8,128)S(1)} %all_to_all.5.gathered, f32[8,32,128]{2,1,0:T(8,128)S(1)} %get-tuple-element.25.smoothed, f32[6,48,128]{2,1,0:T(8,128)S(1)} %get-tuple-element.26.error_one), custom_call_target="tpu_custom_call" | custom-call | tf_op jit(solution)/shard_map/correct/pallas_call | solution.py:687
  (4 shorter events, 0.1 us)
Async XLA Ops:
  0.0 2.1 %collective-permute-start = (f32[8,32,128]{2,1,0:T(8,128)}, f32[8,32,128]{2,1,0:T(8,128)S(1)}, u32[]{:S(2)}, u32[]{:S(2)}) collective-permute-start(f32[8,32,128]{2,1,0:T(8,128)} %param.3), channel_id=1, source_target_pairs={{0,4},{4,0},{8,12},{12,8},{16,20},{20,16},{24,28},{28,24},{1,5},{5... | collective-permute-start | bytes 393224 | tf_op jit(solution)/shard_map/ppermute | solution.py:152
  0.5 1.7 %collective-permute-start.1 = (f32[8,32,128]{2,1,0:T(8,128)}, f32[8,32,128]{2,1,0:T(8,128)S(1)}, u32[]{:S(2)}, u32[]{:S(2)}) collective-permute-start(f32[8,32,128]{2,1,0:T(8,128)} %param.4), channel_id=1, source_target_pairs={{0,4},{4,0},{8,12},{12,8},{16,20},{20,16},{24,28},{28,24},{1,5},{5... | collective-permute-start | bytes 393224 | tf_op jit(solution)/shard_map/ppermute | solution.py:152
  0.5 1.7 %collective-permute-start.2 = (f32[8,32,128]{2,1,0:T(8,128)}, f32[8,32,128]{2,1,0:T(8,128)S(1)}, u32[]{:S(2)}, u32[]{:S(2)}) collective-permute-start(f32[8,32,128]{2,1,0:T(8,128)} %param.5), channel_id=1, source_target_pairs={{0,4},{4,0},{8,12},{12,8},{16,20},{20,16},{24,28},{28,24},{1,5},{5... | collective-permute-start | bytes 393224 | tf_op jit(solution)/shard_map/ppermute | solution.py:152
  2.3 1.4 %collective-permute-start.3 = (f32[256,128]{1,0:T(8,128)S(1)}, f32[256,128]{1,0:T(8,128)S(1)}, u32[]{:S(2)}, u32[]{:S(2)}) collective-permute-start(f32[256,128]{1,0:T(8,128)S(1)} %get-tuple-element.16), channel_id=1, source_target_pairs={{4,8},{12,16},{20,24},{8,4},{16,12},{24,20},{5,9},{13,17},{21,25},... | collective-permute-start | bytes 393224 | tf_op jit(solution)/shard_map/ppermute | solution.py:157
  2.9 7.5 %collective-permute-start.5 = (f32[456,128]{1,0:T(8,128)S(1)}, f32[456,128]{1,0:T(8,128)S(1)}, u32[]{:S(2)}, u32[]{:S(2)}) collective-permute-start(f32[456,128]{1,0:T(8,128)S(1)} %get-tuple-element.18), channel_id=1, source_target_pairs={{4,8},{12,16},{20,24},{8,4},{16,12},{24,20},{5,9},{13,17},{21,25},... | collective-permute-start | bytes 700424 | tf_op jit(solution)/shard_map/ppermute | solution.py:165
  3.7 13.0 %collective-permute-start.4 = (f32[304,128]{1,0:T(8,128)S(1)}, f32[304,128]{1,0:T(8,128)S(1)}, u32[]{:S(2)}, u32[]{:S(2)}) collective-permute-start(f32[304,128]{1,0:T(8,128)S(1)} %get-tuple-element.17), channel_id=1, source_target_pairs={{1,0},{2,1},{3,2},{5,4},{6,5},{7,6},{9,8},{10,9},{11,10},{13,12},{... | collective-permute-start | bytes 466952 | tf_op jit(solution)/shard_map/ppermute | solution.py:164
  5.0 12.6 %collective-permute-start.6 = (f32[304,128]{1,0:T(8,128)S(1)}, f32[304,128]{1,0:T(8,128)S(1)}, u32[]{:S(2)}, u32[]{:S(2)}) collective-permute-start(f32[304,128]{1,0:T(8,128)S(1)} %get-tuple-element.20), channel_id=1, source_target_pairs={{0,1},{1,2},{2,3},{4,5},{5,6},{6,7},{8,9},{9,10},{10,11},{12,13},{... | collective-permute-start | bytes 466952 | tf_op jit(solution)/shard_map/ppermute | solution.py:163
  10.4 7.1 %collective-permute-start.7 = (f32[2,32,128]{2,1,0:T(8,128)S(1)}, f32[2,32,128]{2,1,0:T(8,128)S(1)}, u32[]{:S(2)}, u32[]{:S(2)}) collective-permute-start(f32[2,32,128]{2,1,0:T(8,128)S(1)} %far_planes.1), channel_id=1, source_target_pairs={{0,4},{4,0},{8,12},{12,8},{16,20},{20,16},{24,28},{28,24},{1,5},{5... | collective-permute-start | bytes 98312 | tf_op jit(solution)/shard_map/ppermute | solution.py:167
  16.7 1.9 %collective-permute-start.9 = (f32[304,128]{1,0:T(8,128)S(1)}, f32[304,128]{1,0:T(8,128)S(1)}, u32[]{:S(2)}, u32[]{:S(2)}) collective-permute-start(f32[304,128]{1,0:T(8,128)S(1)} %collective-permute-done.4.above), channel_id=1, source_target_pairs={{0,4},{4,0},{8,12},{12,8},{16,20},{20,16},{24,28},{28,24},{1,5},{5... | collective-permute-start | bytes 466952 | tf_op jit(solution)/shard_map/ppermute | solution.py:171
  17.5 2.0 %collective-permute-start.8 = (f32[304,128]{1,0:T(8,128)S(1)}, f32[304,128]{1,0:T(8,128)S(1)}, u32[]{:S(2)}, u32[]{:S(2)}) collective-permute-start(f32[304,128]{1,0:T(8,128)S(1)} %collective-permute-done.6.below), channel_id=1, source_target_pairs={{0,4},{4,0},{8,12},{12,8},{16,20},{20,16},{24,28},{28,24},{1,5},{5... | collective-permute-start | bytes 466952 | tf_op jit(solution)/shard_map/ppermute | solution.py:170
